TPU v7x, 32 devices: a whole 2x2x4 slice. The times are simulated.
32 devices in a mesh: fsdp: 4 (over z), ctx: 2 (over x), tp: 4 (over y, core).
Axes of the slice: x: 2, y: 2, z: 4, core: 2. Of those that a mesh axis runs over, the one named last changes fastest.
Arguments:
- tokens: bfloat16 [8, 1024, 1024], P('fsdp', ('ctx', 'tp')), may hold values from -6 to 6
- key_valid: int32 [8, 1024], P('fsdp'), may hold values from 0 to 1, as said below
- first_gain: bfloat16 [2, 1024], P(None, 'fsdp'), may hold values from 0.25 to 1.75
- first_shift: bfloat16 [2, 1024], P(None, 'fsdp'), may hold values from -1.75 to 1.75
- joint_weight: bfloat16 [2, 1024, 3, 1024], P(None, 'fsdp', None, 'tp'), may hold values from -0.1875 to 0.1875
- query_bias: bfloat16 [2, 16, 64], P(None, 'tp', 'fsdp'), may hold values from -3 to 3
- value_bias: bfloat16 [2, 16, 64], P(None, 'tp', 'fsdp'), may hold values from -0.625 to 0.625
- out_weight: bfloat16 [2, 1024, 1024], P(None, 'tp', 'fsdp'), may hold values from -0.75 to 0.75
- out_bias: bfloat16 [2, 1024], P(None, 'fsdp'), may hold values from -1.75 to 1.75
- second_gain: bfloat16 [2, 1024], P(None, 'fsdp'), may hold values from 0.25 to 1.75
- second_shift: bfloat16 [2, 1024], P(None, 'fsdp'), may hold values from -1.75 to 1.75
- expand_weight: bfloat16 [2, 1024, 4096], P(None, 'fsdp', 'tp'), may hold values from -0.1875 to 0.1875
- expand_bias: bfloat16 [2, 64, 64], P(None, 'tp', 'fsdp'), may hold values from -3 to 3
- reduce_weight: bfloat16 [2, 4096, 1024], P(None, 'tp', 'fsdp'), may hold values from -0.09375 to 0.09375
- reduce_bias: bfloat16 [2, 1024], P(None, 'fsdp'), may hold values from -1.75 to 1.75
- cotangent: bfloat16 [8, 1024, 1024], P('fsdp', ('ctx', 'tp')), may hold values from -6 to 6
Outputs:
- output: bfloat16 [8, 1024, 1024], P('fsdp', ('ctx', 'tp'))
- input_grad: bfloat16 [8, 1024, 1024], P('fsdp', ('ctx', 'tp'))
- grad_first_gain: float32 [2, 1024], P(None, 'fsdp')
- grad_first_shift: float32 [2, 1024], P(None, 'fsdp')
- grad_joint_weight: float32 [2, 1024, 3, 1024], P(None, 'fsdp', None, 'tp')
- grad_query_bias: float32 [2, 16, 64], P(None, 'tp', 'fsdp')
- grad_value_bias: float32 [2, 16, 64], P(None, 'tp', 'fsdp')
- grad_out_weight: float32 [2, 1024, 1024], P(None, 'tp', 'fsdp')
- grad_out_bias: float32 [2, 1024], P(None, 'fsdp')
- grad_second_gain: float32 [2, 1024], P(None, 'fsdp')
- grad_second_shift: float32 [2, 1024], P(None, 'fsdp')
- grad_expand_weight: float32 [2, 1024, 4096], P(None, 'fsdp', 'tp')
- grad_expand_bias: float32 [2, 64, 64], P(None, 'tp', 'fsdp')
- grad_reduce_weight: float32 [2, 4096, 1024], P(None, 'tp', 'fsdp')
- grad_reduce_bias: float32 [2, 1024], P(None, 'fsdp')
Inputs may be any that keep to these rules, and one draw needn't show every extreme that they name: `key_valid`: in each clip the ones form a prefix of 128 tokens or more; clip 0 has ones throughout.
All inputs are finite; a program needn't handle non-finite values.
Results may differ from a plain program's by a relative error of at most 0.02.
Values may be sent and summed in bfloat16 or wider, within the bound.
A program may use at most 256 MiB of HBM per device.

v0:
```python
import jax
import jax.numpy as jnp
from jax import lax
from jax.sharding import PartitionSpec as P

HD = 64
LAYERS = 2
MB = 2


epsilon = 1e-06
masked_score = -10000.0


def norm_rows(rows, gain, shift):
    middle = jnp.mean(rows, axis=-1, keepdims=True)
    centred = rows - middle
    spread = jnp.mean(centred * centred, axis=-1, keepdims=True)
    return centred * lax.rsqrt(spread + epsilon) * gain + shift


def exact_gelu(values):
    return jax.nn.gelu(values, approximate=False)


def dense(left, right):
    return jnp.dot(left, right, preferred_element_type=jnp.float32)


def dense_left(left, right):
    return lax.dot_general(
        left, right, (((0,), (0,)), ((), ())), preferred_element_type=jnp.float32
    )


def dense_right(left, right):
    return lax.dot_general(
        left, right, (((1,), (1,)), ((), ())), preferred_element_type=jnp.float32
    )


def head_major(rows):
    return rows.reshape(rows.shape[0], -1, HD).transpose(1, 0, 2)


def row_major(heads):
    return heads.transpose(1, 0, 2).reshape(heads.shape[1], -1)


def spread_rows(rows):
    return lax.all_gather(rows, "tp", axis=0, tiled=True)


def gather_grad(rows):
    return lax.all_gather(rows, "tp", axis=0, tiled=True)


def combine_rows(partial_value):
    return lax.psum_scatter(
        partial_value.astype(jnp.bfloat16), "tp", scatter_dimension=0, tiled=True
    ).astype(jnp.float32)


def combine_grads(partial_value):
    return lax.psum_scatter(
        partial_value.astype(jnp.bfloat16), "tp", scatter_dimension=0, tiled=True
    ).astype(jnp.float32)


def fetch(params, layer_id):
    (
        first_gain,
        first_shift,
        joint_weight,
        query_bias,
        value_bias,
        out_weight,
        out_bias,
        second_gain,
        second_shift,
        expand_weight,
        expand_bias,
        reduce_weight,
        reduce_bias,
    ) = params
    return (
        lax.all_gather(first_gain[layer_id], "fsdp", axis=0, tiled=True),
        lax.all_gather(first_shift[layer_id], "fsdp", axis=0, tiled=True),
        lax.all_gather(joint_weight[layer_id], "fsdp", axis=0, tiled=True),
        lax.all_gather(query_bias[layer_id], "fsdp", axis=1, tiled=True),
        lax.all_gather(value_bias[layer_id], "fsdp", axis=1, tiled=True),
        lax.all_gather(out_weight[layer_id], "fsdp", axis=1, tiled=True),
        lax.all_gather(out_bias[layer_id], "fsdp", axis=0, tiled=True),
        lax.all_gather(second_gain[layer_id], "fsdp", axis=0, tiled=True),
        lax.all_gather(second_shift[layer_id], "fsdp", axis=0, tiled=True),
        lax.all_gather(expand_weight[layer_id], "fsdp", axis=0, tiled=True),
        lax.all_gather(expand_bias[layer_id], "fsdp", axis=1, tiled=True),
        lax.all_gather(reduce_weight[layer_id], "fsdp", axis=1, tiled=True),
        lax.all_gather(reduce_bias[layer_id], "fsdp", axis=0, tiled=True),
    )


def attention_scores(query_heads, key_heads, key_bias):
    raw_scores = jnp.einsum(
        "hqd,hkd->hqk", query_heads, key_heads, preferred_element_type=jnp.float32
    )
    return raw_scores * HD ** (-0.5) + key_bias


def forward_layer(residual, layer_weights, key_bias):
    (
        gain_attn,
        shift_attn,
        joint_mat,
        query_add,
        value_add,
        out_mat,
        out_add,
        gain_mlp,
        shift_mlp,
        expand_mat,
        expand_add,
        reduce_mat,
        reduce_add,
    ) = layer_weights
    normed = norm_rows(residual, gain_attn.astype(jnp.float32), shift_attn.astype(jnp.float32))
    first_in = spread_rows(normed.astype(jnp.bfloat16))
    joint = jnp.einsum("nd,dce->nce", first_in, joint_mat, preferred_element_type=jnp.float32)
    queries = (joint[:, 0] + query_add.reshape(-1).astype(jnp.float32)).astype(jnp.bfloat16)
    keys_local = joint[:, 1].astype(jnp.bfloat16)
    values_local = (joint[:, 2] + value_add.reshape(-1).astype(jnp.float32)).astype(jnp.bfloat16)
    keys_all, values_all = (
        lax.all_gather(keys_local, "ctx", axis=0, tiled=True),
        lax.all_gather(values_local, "ctx", axis=0, tiled=True),
    )
    query_heads = head_major(queries)
    key_heads = head_major(keys_all)
    value_heads = head_major(values_all)
    scores = attention_scores(query_heads, key_heads, key_bias)
    row_top = jnp.max(scores, axis=-1, keepdims=True)
    exponent = jnp.exp(scores - row_top)
    row_total = jnp.sum(exponent, axis=-1, keepdims=True)
    probs_low = (exponent / row_total).astype(jnp.bfloat16)
    log_total = row_top + jnp.log(row_total)
    mixed_heads = jnp.einsum(
        "hqk,hkd->hqd", probs_low, value_heads, preferred_element_type=jnp.float32
    )
    mixed = row_major(mixed_heads.astype(jnp.bfloat16))
    middle = residual + (combine_rows(dense(mixed, out_mat)) + out_add.astype(jnp.float32))
    normed_mlp = norm_rows(middle, gain_mlp.astype(jnp.float32), shift_mlp.astype(jnp.float32))
    second_in = spread_rows(normed_mlp.astype(jnp.bfloat16))
    before = dense(second_in, expand_mat) + expand_add.reshape(-1).astype(jnp.float32)
    active = exact_gelu(before).astype(jnp.bfloat16)
    result = middle + (combine_rows(dense(active, reduce_mat)) + reduce_add.astype(jnp.float32))
    stored = (
        residual,
        first_in,
        query_heads,
        key_heads,
        value_heads,
        log_total,
        mixed,
        middle,
        second_in,
        before,
        active,
    )
    return (result, stored)


def backward_layer(carry, stored, layer_weights, key_bias):
    (
        gain_attn,
        shift_attn,
        joint_mat,
        query_add,
        value_add,
        out_mat,
        out_add,
        gain_mlp,
        shift_mlp,
        expand_mat,
        expand_add,
        reduce_mat,
        reduce_add,
    ) = layer_weights
    (
        residual,
        first_in,
        query_heads,
        key_heads,
        value_heads,
        log_total,
        mixed,
        middle,
        second_in,
        before,
        active,
    ) = stored
    low_mlp = carry.astype(jnp.bfloat16)
    mlp_rows = gather_grad(low_mlp)
    d_reduce_mat = dense_left(active, mlp_rows)
    d_reduce_add = jnp.sum(low_mlp.astype(jnp.float32), axis=0)
    d_active = dense_right(mlp_rows, reduce_mat)
    gelu_value, gelu_back = jax.vjp(exact_gelu, before)
    d_before = gelu_back(d_active)[0].astype(jnp.bfloat16)
    d_expand_add = jnp.sum(d_before.astype(jnp.float32), axis=0).reshape(expand_add.shape)
    d_expand_mat = dense_left(second_in, d_before)
    d_second = combine_grads(dense_right(d_before, expand_mat))
    norm_value, norm_back = jax.vjp(
        norm_rows, middle, gain_mlp.astype(jnp.float32), shift_mlp.astype(jnp.float32)
    )
    d_middle, d_gain_mlp, d_shift_mlp = norm_back(d_second)
    carry_mid = carry + d_middle
    low_attn = carry_mid.astype(jnp.bfloat16)
    attn_rows = gather_grad(low_attn)
    d_out_mat = dense_left(mixed, attn_rows)
    d_out_add = jnp.sum(low_attn.astype(jnp.float32), axis=0)
    d_mixed = head_major(dense_right(attn_rows, out_mat).astype(jnp.bfloat16))
    scores = attention_scores(query_heads, key_heads, key_bias)
    attn_probs = jnp.exp(scores - log_total)
    d_values = jnp.einsum(
        "hqk,hqd->hkd", attn_probs.astype(jnp.bfloat16), d_mixed, preferred_element_type=jnp.float32
    )
    d_probs = jnp.einsum("hqd,hkd->hqk", d_mixed, value_heads, preferred_element_type=jnp.float32)
    d_scores = attn_probs * (d_probs - jnp.sum(attn_probs * d_probs, axis=-1, keepdims=True))
    d_raw = (d_scores * HD ** (-0.5)).astype(jnp.bfloat16)
    d_queries = jnp.einsum("hqk,hkd->hqd", d_raw, key_heads, preferred_element_type=jnp.float32)
    d_queries = row_major(d_queries.astype(jnp.bfloat16))
    d_keys = jnp.einsum("hqk,hqd->hkd", d_raw, query_heads, preferred_element_type=jnp.float32)
    d_keys = row_major(d_keys)
    d_values = row_major(d_values)
    d_keys, d_values = (
        lax.psum_scatter(
            d_keys.astype(jnp.bfloat16), "ctx", scatter_dimension=0, tiled=True
        ).astype(jnp.float32),
        lax.psum_scatter(
            d_values.astype(jnp.bfloat16), "ctx", scatter_dimension=0, tiled=True
        ).astype(jnp.float32),
    )
    d_keys = d_keys.astype(jnp.bfloat16)
    d_values = d_values.astype(jnp.bfloat16)
    d_joint = jnp.stack((d_queries, d_keys, d_values), axis=1)
    d_joint_mat = jnp.einsum("nd,nce->dce", first_in, d_joint, preferred_element_type=jnp.float32)
    d_query_add = jnp.sum(d_queries.astype(jnp.float32), axis=0).reshape(query_add.shape)
    d_value_add = jnp.sum(d_values.astype(jnp.float32), axis=0).reshape(value_add.shape)
    d_first = combine_grads(
        jnp.einsum("nce,dce->nd", d_joint, joint_mat, preferred_element_type=jnp.float32)
    )
    first_value, first_back = jax.vjp(
        norm_rows, residual, gain_attn.astype(jnp.float32), shift_attn.astype(jnp.float32)
    )
    d_residual, d_gain_attn, d_shift_attn = first_back(d_first)
    carry_in = carry_mid + d_residual
    layer_grads = (
        d_gain_attn,
        d_shift_attn,
        d_joint_mat,
        d_query_add,
        d_value_add,
        d_out_mat,
        d_out_add,
        d_gain_mlp,
        d_shift_mlp,
        d_expand_mat,
        d_expand_add,
        d_reduce_mat,
        d_reduce_add,
    )
    return (carry_in, layer_grads)


def local(
    tokens,
    key_valid,
    first_gain,
    first_shift,
    joint_weight,
    query_bias,
    value_bias,
    out_weight,
    out_bias,
    second_gain,
    second_shift,
    expand_weight,
    expand_bias,
    reduce_weight,
    reduce_bias,
    cotangent,
):
    params = (
        first_gain,
        first_shift,
        joint_weight,
        query_bias,
        value_bias,
        out_weight,
        out_bias,
        second_gain,
        second_shift,
        expand_weight,
        expand_bias,
        reduce_weight,
        reduce_bias,
    )
    fetched = tuple((fetch(params, layer_id) for layer_id in range(LAYERS)))
    totals = [None] * LAYERS
    outputs = []
    row_grads = []
    for batch_id in range(MB):
        key_bias = jnp.where(key_valid[batch_id] == 1, 0.0, masked_score).astype(jnp.float32)
        residual = tokens[batch_id].astype(jnp.float32)
        stores = []
        for layer_id in range(LAYERS):
            residual, stored = forward_layer(residual, fetched[layer_id], key_bias)
            stores.append(stored)
        outputs.append(residual.astype(jnp.bfloat16))
        carry = cotangent[batch_id].astype(jnp.float32)
        for layer_id in reversed(range(LAYERS)):
            carry, layer_grads = backward_layer(
                carry, stores[layer_id], fetched[layer_id], key_bias
            )
            if totals[layer_id] is None:
                totals[layer_id] = layer_grads
            else:
                totals[layer_id] = tuple(
                    (old + new for old, new in zip(totals[layer_id], layer_grads))
                )
        row_grads.append(carry.astype(jnp.bfloat16))
    stacked = [
        jnp.stack([totals[layer_id][index] for layer_id in range(LAYERS)]) for index in range(13)
    ]
    shards = (
        lax.psum_scatter(
            stacked[0].astype(jnp.bfloat16), "fsdp", scatter_dimension=1, tiled=True
        ).astype(jnp.float32),
        lax.psum_scatter(
            stacked[1].astype(jnp.bfloat16), "fsdp", scatter_dimension=1, tiled=True
        ).astype(jnp.float32),
        lax.psum_scatter(
            stacked[2].astype(jnp.bfloat16), "fsdp", scatter_dimension=1, tiled=True
        ).astype(jnp.float32),
        lax.psum_scatter(
            stacked[3].astype(jnp.bfloat16), "fsdp", scatter_dimension=2, tiled=True
        ).astype(jnp.float32),
        lax.psum_scatter(
            stacked[4].astype(jnp.bfloat16), "fsdp", scatter_dimension=2, tiled=True
        ).astype(jnp.float32),
        lax.psum_scatter(
            stacked[5].astype(jnp.bfloat16), "fsdp", scatter_dimension=2, tiled=True
        ).astype(jnp.float32),
        lax.psum_scatter(
            stacked[6].astype(jnp.bfloat16), "fsdp", scatter_dimension=1, tiled=True
        ).astype(jnp.float32),
        lax.psum_scatter(
            stacked[7].astype(jnp.bfloat16), "fsdp", scatter_dimension=1, tiled=True
        ).astype(jnp.float32),
        lax.psum_scatter(
            stacked[8].astype(jnp.bfloat16), "fsdp", scatter_dimension=1, tiled=True
        ).astype(jnp.float32),
        lax.psum_scatter(
            stacked[9].astype(jnp.bfloat16), "fsdp", scatter_dimension=1, tiled=True
        ).astype(jnp.float32),
        lax.psum_scatter(
            stacked[10].astype(jnp.bfloat16), "fsdp", scatter_dimension=2, tiled=True
        ).astype(jnp.float32),
        lax.psum_scatter(
            stacked[11].astype(jnp.bfloat16), "fsdp", scatter_dimension=2, tiled=True
        ).astype(jnp.float32),
        lax.psum_scatter(
            stacked[12].astype(jnp.bfloat16), "fsdp", scatter_dimension=1, tiled=True
        ).astype(jnp.float32),
    )
    split_sums = (
        lax.psum(shards[2].astype(jnp.bfloat16), "ctx").astype(jnp.float32),
        lax.psum(shards[3].astype(jnp.bfloat16), "ctx").astype(jnp.float32),
        lax.psum(shards[4].astype(jnp.bfloat16), "ctx").astype(jnp.float32),
        lax.psum(shards[5].astype(jnp.bfloat16), "ctx").astype(jnp.float32),
        lax.psum(shards[9].astype(jnp.bfloat16), "ctx").astype(jnp.float32),
        lax.psum(shards[10].astype(jnp.bfloat16), "ctx").astype(jnp.float32),
        lax.psum(shards[11].astype(jnp.bfloat16), "ctx").astype(jnp.float32),
    )
    vector_part = lax.psum(
        (shards[0], shards[1], shards[6], shards[7], shards[8], shards[12]), ("ctx", "tp")
    )
    return (
        jnp.stack(outputs),
        jnp.stack(row_grads),
        vector_part[0],
        vector_part[1],
        split_sums[0],
        split_sums[1],
        split_sums[2],
        split_sums[3],
        vector_part[2],
        vector_part[3],
        vector_part[4],
        split_sums[4],
        split_sums[5],
        split_sums[6],
        vector_part[5],
    )


def solution(mesh):
    placed = (
        P("fsdp", ("ctx", "tp"), None),
        P("fsdp", None),
        P(None, "fsdp"),
        P(None, "fsdp"),
        P(None, "fsdp", None, "tp"),
        P(None, "tp", "fsdp"),
        P(None, "tp", "fsdp"),
        P(None, "tp", "fsdp"),
        P(None, "fsdp"),
        P(None, "fsdp"),
        P(None, "fsdp"),
        P(None, "fsdp", "tp"),
        P(None, "tp", "fsdp"),
        P(None, "tp", "fsdp"),
        P(None, "fsdp"),
        P("fsdp", ("ctx", "tp"), None),
    )
    return jax.shard_map(
        local,
        mesh=mesh,
        in_specs=placed,
        out_specs=(
            P("fsdp", ("ctx", "tp"), None),
            P("fsdp", ("ctx", "tp"), None),
            P(None, "fsdp"),
            P(None, "fsdp"),
            P(None, "fsdp", None, "tp"),
            P(None, "tp", "fsdp"),
            P(None, "tp", "fsdp"),
            P(None, "tp", "fsdp"),
            P(None, "fsdp"),
            P(None, "fsdp"),
            P(None, "fsdp"),
            P(None, "fsdp", "tp"),
            P(None, "tp", "fsdp"),
            P(None, "tp", "fsdp"),
            P(None, "fsdp"),
        ),
        check_vma=False,
    )
```

profile of v0, /device:TPU:0, one launch (start us, length us, event | category | flops | bytes accessed | tf_op | source)
XLA Modules:
  0.0 1841.4 jit_solution(5257562722936392963)
XLA Ops:
  61.3 19.5 %all-gather.6 = bf16[1,256,1024]{2,1,0:T(8,128)(2,1)S(1)} all-gather(bf16[1,256,256]{2,1,0:T(8,128)(2,1)S(1)} %get-tuple-element.130), channel_id=8, replica_groups=mesh['fsdp'=4,'ctx'=2,'tp'=4] {'fsdp'}, dimensions={2}, use_global_device_ids=true | all-gather | bytes 655360 | tf_op jit(solution)/shard_map/all_gather | solution.py:92
  240.8 27.9 %all-gather.85.cloned.1.call-done = bf16[1,1024,1024]{2,1,0:T(8,128)(2,1)} async-done(((bf16[1,256,1024]{2,1,0:T(8,128)(2,1)}), bf16[1,1024,1024]{2,1,0:T(8,128)(2,1)}) %all-gather.85.cloned.1.call-update) | async-done | bytes 2097168 | tf_op jit(solution)/shard_map/all_gather | solution.py:96
  318.6 35.0 %all-gather.87.cloned.1.call-done = bf16[1,1024,1024]{2,1,0:T(8,128)(2,1)} async-done(((bf16[1,1024,256]{2,1,0:T(8,128)(2,1)}), bf16[1,1024,1024]{2,1,0:T(8,128)(2,1)}) %all-gather.87.cloned.1.call-update) | async-done | bytes 2097168 | tf_op jit(solution)/shard_map/all_gather | solution.py:98
  388.2 20.1 %reduce-scatter.66.cloned.1.call-done = bf16[128,1024]{1,0:T(8,128)(2,1)} async-done(((bf16[512,1024]{1,0:T(8,128)(2,1)}), bf16[128,1024]{1,0:T(8,128)(2,1)}) %reduce-scatter.66.cloned.1.call-update) | async-done | bytes 262160 | tf_op jit(solution)/shard_map/reduce_scatter | solution.py:59
  597.3 27.3 %all-gather.91.cloned.1.call-done = bf16[1,1024,1024]{2,1,0:T(8,128)(2,1)} async-done(((bf16[1,256,1024]{2,1,0:T(8,128)(2,1)}), bf16[1,1024,1024]{2,1,0:T(8,128)(2,1)}) %all-gather.91.cloned.1.call-update) | async-done | bytes 2097168 | tf_op jit(solution)/shard_map/all_gather | solution.py:96
  678.8 48.4 %all-gather.93.cloned.1.call-done = bf16[1,1024,1024]{2,1,0:T(8,128)(2,1)} async-done(((bf16[1,1024,256]{2,1,0:T(8,128)(2,1)}), bf16[1,1024,1024]{2,1,0:T(8,128)(2,1)}) %all-gather.93.cloned.1.call-update) | async-done | bytes 2097168 | tf_op jit(solution)/shard_map/all_gather | solution.py:98
  771.9 26.8 %reduce-scatter.72.cloned.1.call-done = bf16[128,1024]{1,0:T(8,128)(2,1)} async-done(((bf16[512,1024]{1,0:T(8,128)(2,1)}), bf16[128,1024]{1,0:T(8,128)(2,1)}) %reduce-scatter.72.cloned.1.call-update) | async-done | bytes 262160 | tf_op jit(solution)/shard_map/reduce_scatter | solution.py:65
  800.1 26.0 %reduce-scatter.62.cloned.1.call-done = bf16[128,1024]{1,0:T(8,128)(2,1)} async-done(((bf16[512,1024]{1,0:T(8,128)(2,1)}), bf16[128,1024]{1,0:T(8,128)(2,1)}) %reduce-scatter.62.cloned.1.call-update) | async-done | bytes 262160 | tf_op jit(solution)/shard_map/reduce_scatter | solution.py:59
  826.1 27.5 %reduce-scatter.70.cloned.1.call-done = bf16[128,1024]{1,0:T(8,128)(2,1)} async-done(((bf16[512,1024]{1,0:T(8,128)(2,1)}), bf16[128,1024]{1,0:T(8,128)(2,1)}) %reduce-scatter.70.cloned.1.call-update) | async-done | bytes 262160 | tf_op jit(solution)/shard_map/reduce_scatter | solution.py:59
  881.5 23.0 %fusion.221 = bf16[4,1024,64]{1,2,0:T(8,128)(2,1)} fusion(f32[4,512,1024]{2,1,0:T(8,128)} %fusion.467, f32[4,512,1024]{2,1,0:T(8,128)} %copy-done.4, f32[4,512]{1,0:T(4,128)S(1)} %log_add_fusion.1, f32[1024]{0:T(1024)S(1)} %bitcast.661, f32[512,4,64]{0,2,1:T(8,128)S(1)} %bitcast.579, f32[4,64]{1,0:T(4,128)S(1)} %copy.126), kind=kOutput, calls=%fused_computation.234 | convolution fusion | flops 292031488 | bytes 17839104 | tf_op jit(solution)/shard_map/hqk,hqd->hkd/dot_general | solution.py:230
  921.5 22.2 %fusion.227 = bf16[4,1024,64]{1,2,0:T(8,128)(2,1)S(1)} fusion(f32[4,512,1024]{2,1,0:T(8,128)} %fusion.465, f32[4,512,1024]{2,1,0:T(8,128)} %copy-done.3, f32[4,512]{1,0:T(4,128)S(1)} %log_add_fusion.3, f32[1024]{0:T(1024)S(1)} %bitcast.649, f32[512,4,64]{0,2,1:T(8,128)S(1)} %bitcast.577, f32[4,64]{1,0:T(4,128)S(1)} %copy.126), kind=kOutput, calls=%fused_computation.236 | convolution fusion | flops 292031488 | bytes 17839104 | tf_op jit(solution)/shard_map/hqk,hqd->hkd/dot_general | solution.py:230
  951.3 21.7 %convert_reduce_fusion.26 = (f32[4,64]{1,0:T(4,128)S(1)}, bf16[4,512,64]{1,2,0:T(8,128)(2,1)S(1)}) fusion(bf16[4,1024,64]{1,2,0:T(8,128)(2,1)S(1)} %bitcast.575, f32[4,512,1024]{2,1,0:T(8,128)} %fusion.467, f32[4,512,1024]{2,1,0:T(8,128)} %copy-done.4, f32[4,512]{1,0:T(4,128)S(1)} %log_add_fusion.1, f32[1024]{0:T(1024)S(1)} %bitcast.663), kind=kOutput, calls=%fused_computation.405 | convolution fusion | flops 291900160 | bytes 17576960 | tf_op jit(solution)/shard_map/hqk,hkd->hqd/dot_general | solution.py:228
  977.0 21.7 %convert_reduce_fusion.27 = (f32[4,64]{1,0:T(4,128)S(1)}, bf16[4,512,64]{1,2,0:T(8,128)(2,1)S(1)}) fusion(bf16[4,1024,64]{1,2,0:T(8,128)(2,1)S(1)} %bitcast.573, f32[4,512,1024]{2,1,0:T(8,128)} %fusion.465, f32[4,512,1024]{2,1,0:T(8,128)} %copy-done.3, f32[4,512]{1,0:T(4,128)S(1)} %log_add_fusion.3, f32[1024]{0:T(1024)S(1)} %bitcast.651), kind=kOutput, calls=%fused_computation.406 | convolution fusion | flops 291900160 | bytes 17576960 | tf_op jit(solution)/shard_map/hqk,hkd->hqd/dot_general | solution.py:228
  1004.4 27.6 %reduce-scatter.78.cloned.1.call-done = bf16[128,1024]{1,0:T(8,128)(2,1)} async-done(((bf16[512,1024]{1,0:T(8,128)(2,1)}), bf16[128,1024]{1,0:T(8,128)(2,1)}) %reduce-scatter.78.cloned.1.call-update) | async-done | bytes 262160 | tf_op jit(solution)/shard_map/reduce_scatter | solution.py:65
  1081.1 18.7 %reduce-scatter.96.cloned.1.call-done = bf16[128,1024]{1,0:T(8,128)(2,1)} async-done(((bf16[512,1024]{1,0:T(8,128)(2,1)}), bf16[128,1024]{1,0:T(8,128)(2,1)}) %reduce-scatter.96.cloned.1.call-update) | async-done | bytes 262160 | tf_op jit(solution)/shard_map/reduce_scatter | solution.py:65
  1099.8 28.2 %reduce-scatter.80.cloned.1.call-done = bf16[128,1024]{1,0:T(8,128)(2,1)} async-done(((bf16[512,1024]{1,0:T(8,128)(2,1)}), bf16[128,1024]{1,0:T(8,128)(2,1)}) %reduce-scatter.80.cloned.1.call-update) | async-done | bytes 262160 | tf_op jit(solution)/shard_map/reduce_scatter | solution.py:65
  1157.4 22.8 %fusion.218 = bf16[4,1024,64]{1,2,0:T(8,128)(2,1)} fusion(f32[4,512,1024]{2,1,0:T(8,128)} %fusion.468, f32[4,512,1024]{2,1,0:T(8,128)} %copy-done.2, f32[4,512]{1,0:T(4,128)S(1)} %log_add_fusion, f32[1024]{0:T(1024)S(1)} %bitcast.664, f32[512,4,64]{0,2,1:T(8,128)S(1)} %bitcast.569, f32[4,64]{1,0:T(4,128)S(1)} %copy-done.104), kind=kOutput, calls=%fused_computation.233 | convolution fusion | flops 292031488 | bytes 17839104 | tf_op jit(solution)/shard_map/hqk,hqd->hkd/dot_general | solution.py:230
  1196.9 22.0 %fusion.224 = bf16[4,1024,64]{1,2,0:T(8,128)(2,1)S(1)} fusion(f32[4,512,1024]{2,1,0:T(8,128)} %fusion.466, f32[4,512,1024]{2,1,0:T(8,128)} %copy-done.1, f32[4,512]{1,0:T(4,128)S(1)} %log_add_fusion.2, f32[1024]{0:T(1024)S(1)} %bitcast.652, f32[512,4,64]{0,2,1:T(8,128)S(1)} %bitcast.563, f32[4,64]{1,0:T(4,128)S(1)} %copy-done.104), kind=kOutput, calls=%fused_computation.235 | convolution fusion | flops 292031488 | bytes 17839104 | tf_op jit(solution)/shard_map/hqk,hqd->hkd/dot_general | solution.py:230
  1226.5 22.1 %convert_reduce_fusion.28 = (f32[4,64]{1,0:T(4,128)}, bf16[4,512,64]{1,2,0:T(8,128)(2,1)S(1)}) fusion(bf16[4,1024,64]{1,2,0:T(8,128)(2,1)S(1)} %bitcast.567, f32[4,512,1024]{2,1,0:T(8,128)} %fusion.468, f32[4,512,1024]{2,1,0:T(8,128)} %copy-done.2, f32[4,512]{1,0:T(4,128)S(1)} %log_add_fusion, f32[1024]{0:T(1024)S(1)} %bitcast.666), kind=kOutput, calls=%fused_computation.407 | convolution fusion | flops 291900160 | bytes 17576960 | tf_op jit(solution)/shard_map/hqk,hkd->hqd/dot_general | solution.py:228
  1252.5 22.1 %convert_reduce_fusion.29 = (f32[4,64]{1,0:T(4,128)}, bf16[4,512,64]{1,2,0:T(8,128)(2,1)S(1)}) fusion(bf16[4,1024,64]{1,2,0:T(8,128)(2,1)S(1)} %bitcast.561, f32[4,512,1024]{2,1,0:T(8,128)} %fusion.466, f32[4,512,1024]{2,1,0:T(8,128)} %copy-done.1, f32[4,512]{1,0:T(4,128)S(1)} %log_add_fusion.2, f32[1024]{0:T(1024)S(1)} %bitcast.654), kind=kOutput, calls=%fused_computation.408 | convolution fusion | flops 291900160 | bytes 17576960 | tf_op jit(solution)/shard_map/hqk,hkd->hqd/dot_general | solution.py:228
  1337.6 77.7 %reduce-scatter.110.cloned.1.call-done = bf16[2,1024,256]{2,1,0:T(8,128)(2,1)} async-done(((bf16[2,1024,1024]{2,1,0:T(8,128)(2,1)}), bf16[2,1024,256]{2,1,0:T(8,128)(2,1)}) %reduce-scatter.110.cloned.1.call-update) | async-done | bytes 1048592 | tf_op jit(solution)/shard_map/reduce_scatter | solution.py:367
  1415.3 79.5 %reduce-scatter.108.cloned.1.call-done = bf16[2,256,1024]{2,1,0:T(8,128)(2,1)} async-done(((bf16[2,1024,1024]{2,1,0:T(8,128)(2,1)}), bf16[2,256,1024]{2,1,0:T(8,128)(2,1)}) %reduce-scatter.108.cloned.1.call-update) | async-done | bytes 1048592 | tf_op jit(solution)/shard_map/reduce_scatter | solution.py:361
  1494.7 63.2 %reduce-scatter.104.cloned.1.call-done = bf16[2,256,3,256]{3,1,2,0:T(8,128)(2,1)} async-done(((bf16[2,1024,3,256]{3,1,2,0:T(8,128)(2,1)}), bf16[2,256,3,256]{3,1,2,0:T(8,128)(2,1)}) %reduce-scatter.104.cloned.1.call-update) | async-done | bytes 786448 | tf_op jit(solution)/shard_map/reduce_scatter | solution.py:340
  1559.9 19.9 %reduce-scatter.128.cloned.1.call-done = bf16[256,2]{1,0:T(8,128)(2,1)} async-done(((bf16[1024,2]{1,0:T(8,128)(2,1)}), bf16[256,2]{1,0:T(8,128)(2,1)}) %reduce-scatter.128.cloned.1.call-update) | async-done | bytes 1040
  1580.7 18.6 %reduce-scatter.126.cloned.1.call-done = bf16[16,32]{1,0:T(8,128)(2,1)} async-done(((bf16[64,32]{1,0:T(8,128)(2,1)}), bf16[16,32]{1,0:T(8,128)(2,1)}) %reduce-scatter.126.cloned.1.call-update) | async-done | bytes 1040
  1600.1 19.1 %reduce-scatter.124.cloned.1.call-done = bf16[256,2]{1,0:T(8,128)(2,1)} async-done(((bf16[1024,2]{1,0:T(8,128)(2,1)}), bf16[256,2]{1,0:T(8,128)(2,1)}) %reduce-scatter.124.cloned.1.call-update) | async-done | bytes 1040
  1620.1 19.4 %reduce-scatter.122.cloned.1.call-done = bf16[256,2]{1,0:T(8,128)(2,1)} async-done(((bf16[1024,2]{1,0:T(8,128)(2,1)}), bf16[256,2]{1,0:T(8,128)(2,1)}) %reduce-scatter.122.cloned.1.call-update) | async-done | bytes 1040
  1640.4 19.2 %reduce-scatter.120.cloned.1.call-done = bf16[256,2]{1,0:T(8,128)(2,1)} async-done(((bf16[1024,2]{1,0:T(8,128)(2,1)}), bf16[256,2]{1,0:T(8,128)(2,1)}) %reduce-scatter.120.cloned.1.call-update) | async-done | bytes 1040
  1660.6 19.1 %reduce-scatter.116.cloned.1.call-done = bf16[16,8]{1,0:T(8,128)(2,1)} async-done(((bf16[64,8]{1,0:T(8,128)(2,1)}), bf16[16,8]{1,0:T(8,128)(2,1)}) %reduce-scatter.116.cloned.1.call-update) | async-done | bytes 272
  1720.6 19.7 %reduce-scatter.112.cloned.1.call-done = bf16[256,2]{1,0:T(8,128)(2,1)} async-done(((bf16[1024,2]{1,0:T(8,128)(2,1)}), bf16[256,2]{1,0:T(8,128)(2,1)}) %reduce-scatter.112.cloned.1.call-update) | async-done | bytes 1040
  1741.2 22.8 %all-reduce = (f32[2,256]{1,0:T(2,128)}, f32[2,256]{1,0:T(2,128)}, f32[2,256]{1,0:T(2,128)}, f32[2,256]{1,0:T(2,128)}, f32[2,256]{1,0:T(2,128)}, /*index=5*/f32[2,256]{1,0:T(2,128)}) all-reduce(bf16[2,256]{1,0:T(2,128)(2,1)S(1)} %copy.164, bf16[2,256]{1,0:T(2,128)(2,1)S(1)} %copy.166, ...), channel_id=1, replica_groups=mesh['fsdp'=4,'ctx'=2,'tp'=4] {'ctx','tp'}, use_global_device_ids=true, to_apply=%region_73.74 | all-reduce | flops 3072 | bytes 18432 | tf_op jit(solution)/shard_map/psum | solution.py:383
  1764.0 63.7 %all-reduce.5.cloned.1.call-done = (bf16[2,256,3,256]{3,1,2,0:T(8,128)(2,1)}, bf16[2,256,256]{2,1,0:T(8,128)(2,1)}, bf16[2,256,1024]{2,1,0:T(8,128)(2,1)}, bf16[2,1024,256]{2,1,0:T(8,128)(2,1)}) async-done(((bf16[2,256,3,256]{3,1,2,0:T(8,128)(2,1)}, bf16[2,256,256]{2,1,0:T(8,128)(2,1)}, bf16[2,256,1024]{2,1,0:T(8,128)(2,1)}, bf16[2,1024,256]{2,1,0:T(8,128)(2,1)}), (bf16[2,256,3,256]{3,1,2,0:T(8,128)(2,1)}, ...) | async-done | bytes 3145744 | tf_op jit(solution)/shard_map/psum | solution.py:375
  (773 shorter events, 871.1 us)
Async XLA Ops:
  34.5 112.5 %reduce-scatter.56.cloned.1.call-start = ((), (), s32[]{:S(2)}) async-start(), calls=%async_computation.38 | async-start | bytes 1310720 | tf_op jit(solution)/shard_map/reduce_scatter | solution.py:59
  197.7 88.6 %all-gather.65.cloned.1.call-start = ((), (), s32[]{:S(2)}) async-start(), calls=%async_computation.47 | async-start | bytes 1310720 | tf_op jit(solution)/shard_map/all_gather | solution.py:51
  225.7 127.9 %all-gather.87.cloned.1.call-start = ((), (), s32[]{:S(2)}) async-start(), calls=%async_computation.81 | async-start | bytes 2621440 | tf_op jit(solution)/shard_map/all_gather | solution.py:98
  226.9 161.3 %reduce-scatter.58.cloned.1.call-start = ((), (), s32[]{:S(2)}) async-start(), calls=%async_computation.40 | async-start | bytes 1310720 | tf_op jit(solution)/shard_map/reduce_scatter | solution.py:59
  361.7 99.1 %all-gather.89.cloned.1.call-start = ((), (), s32[]{:S(2)}) async-start(), calls=%async_computation.82 | async-start | bytes 1966080 | tf_op jit(solution)/shard_map/all_gather | solution.py:89
  362.7 110.7 %all-gather.67.cloned.1.call-start = ((), (), s32[]{:S(2)}) async-start(), calls=%async_computation.49 | async-start | bytes 1310720 | tf_op jit(solution)/shard_map/all_gather | solution.py:51
  411.8 164.8 %reduce-scatter.68.cloned.1.call-start = ((), (), s32[]{:S(2)}) async-start(), calls=%async_computation.50 | async-start | bytes 1310720 | tf_op jit(solution)/shard_map/reduce_scatter | solution.py:59
  548.5 93.2 %all-gather.69.cloned.1.call-start = ((), (), s32[]{:S(2)}) async-start(), calls=%async_computation.51 | async-start | bytes 1310720 | tf_op jit(solution)/shard_map/all_gather | solution.py:51
  580.2 98.6 %all-gather.97.cloned.1.call-start = ((), (), s32[]{:S(2)}) async-start(), calls=%async_computation.86 | async-start | bytes 1310720 | tf_op jit(solution)/shard_map/all_gather | solution.py:55
  582.1 145.1 %all-gather.93.cloned.1.call-start = ((), (), s32[]{:S(2)}) async-start(), calls=%async_computation.84 | async-start | bytes 2621440 | tf_op jit(solution)/shard_map/all_gather | solution.py:98
  582.8 160.9 %all-gather.95.cloned.1.call-start = ((), (), s32[]{:S(2)}) async-start(), calls=%async_computation.85 | async-start | bytes 1310720 | tf_op jit(solution)/shard_map/all_gather | solution.py:55
  583.6 188.3 %reduce-scatter.88.cloned.1.call-start = ((), (), s32[]{:S(2)}) async-start(), calls=%async_computation.64 | async-start | bytes 1310720 | tf_op jit(solution)/shard_map/reduce_scatter | solution.py:65
  756.7 96.9 %reduce-scatter.70.cloned.1.call-start = ((), (), s32[]{:S(2)}) async-start(), calls=%async_computation.52 | async-start | bytes 1310720 | tf_op jit(solution)/shard_map/reduce_scatter | solution.py:59
  760.9 113.2 %all-gather.77.cloned.1.call-start = ((), (), s32[]{:S(2)}) async-start(), calls=%async_computation.65 | async-start | bytes 1310720 | tf_op jit(solution)/shard_map/all_gather | solution.py:55
  858.0 115.2 %reduce-scatter.90.cloned.1.call-start = ((), (), s32[]{:S(2)}) async-start(), calls=%async_computation.66 | async-start | bytes 786432 | tf_op jit(solution)/shard_map/reduce_scatter | solution.py:234
  915.1 83.7 %reduce-scatter.74.cloned.1.call-start = ((), (), s32[]{:S(2)}) async-start(), calls=%async_computation.55 | async-start | bytes 786432 | tf_op jit(solution)/shard_map/reduce_scatter | solution.py:234
  1135.2 113.6 %reduce-scatter.98.cloned.1.call-start = ((), (), s32[]{:S(2)}) async-start(), calls=%async_computation.72 | async-start | bytes 786432 | tf_op jit(solution)/shard_map/reduce_scatter | solution.py:234
  1190.5 84.3 %reduce-scatter.82.cloned.1.call-start = ((), (), s32[]{:S(2)}) async-start(), calls=%async_computation.61 | async-start | bytes 786432 | tf_op jit(solution)/shard_map/reduce_scatter | solution.py:234
  1226.4 94.5 %reduce-scatter.102.cloned.1.call-start = ((), (), s32[]{:S(2)}) async-start(), calls=%async_computation.74 | async-start | bytes 1310720 | tf_op jit(solution)/shard_map/reduce_scatter | solution.py:65
  1283.2 132.0 %reduce-scatter.110.cloned.1.call-start = ((), (), s32[]{:S(2)}) async-start(), calls=%async_computation.78 | async-start | bytes 5242880 | tf_op jit(solution)/shard_map/reduce_scatter | solution.py:367
  1293.4 201.3 %reduce-scatter.108.cloned.1.call-start = ((), (), s32[]{:S(2)}) async-start(), calls=%async_computation.77 | async-start | bytes 5242880 | tf_op jit(solution)/shard_map/reduce_scatter | solution.py:361
  1303.4 254.6 %reduce-scatter.104.cloned.1.call-start = ((), (), s32[]{:S(2)}) async-start(), calls=%async_computation.75 | async-start | bytes 3932160 | tf_op jit(solution)/shard_map/reduce_scatter | solution.py:340
  1312.7 267.0 %reduce-scatter.128.cloned.1.call-start = ((), (), s32[]{:S(2)}) async-start(), calls=%async_computation.95 | async-start | bytes 327680
  1314.8 284.5 %reduce-scatter.126.cloned.1.call-start = ((), (), s32[]{:S(2)}) async-start(), calls=%async_computation.94 | async-start | bytes 20480
  1315.8 303.4 %reduce-scatter.124.cloned.1.call-start = ((), (), s32[]{:S(2)}) async-start(), calls=%async_computation.93 | async-start | bytes 327680
  1316.8 322.7 %reduce-scatter.122.cloned.1.call-start = ((), (), s32[]{:S(2)}) async-start(), calls=%async_computation.92 | async-start | bytes 327680
  1317.8 341.9 %reduce-scatter.120.cloned.1.call-start = ((), (), s32[]{:S(2)}) async-start(), calls=%async_computation.91 | async-start | bytes 327680
  1318.7 361.0 %reduce-scatter.116.cloned.1.call-start = ((), (), s32[]{:S(2)}) async-start(), calls=%async_computation.89 | async-start | bytes 20480
  1319.7 379.4 %reduce-scatter.118.cloned.1.call-start = ((), (), s32[]{:S(2)}) async-start(), calls=%async_computation.90 | async-start | bytes 20480
  1320.9 398.8 %reduce-scatter.114.cloned.1.call-start = ((), (), s32[]{:S(2)}) async-start(), calls=%async_computation.88 | async-start | bytes 327680
  1325.1 415.2 %reduce-scatter.112.cloned.1.call-start = ((), (), s32[]{:S(2)}) async-start(), calls=%async_computation.87 | async-start | bytes 327680
  1326.1 501.6 %all-reduce.5.cloned.1.call-start = ((), (), s32[]{:S(2)}) async-start(), calls=%async_computation.96 | async-start | bytes 6291456 | tf_op jit(solution)/shard_map/psum | solution.py:375
  (178 other events, 4581.9 us)
Sparse Core Ops, SparseCore 0:
  52.1 41.7 all-gather.82
  121.3 25.6 reduce-scatter.55
  195.5 24.8 reduce-scatter.63
  222.4 46.2 all-gather.84
  307.4 46.2 all-gather.86
  357.6 23.1 reduce-scatter.57
  383.4 24.8 reduce-scatter.65
  410.3 44.1 all-gather.88
  523.5 24.8 reduce-scatter.67
  551.5 24.9 reduce-scatter.59
  578.5 46.1 all-gather.90
  680.9 46.2 all-gather.92
  746.3 24.8 reduce-scatter.87
  773.7 24.8 reduce-scatter.71
  801.2 24.9 reduce-scatter.61
  828.7 24.8 reduce-scatter.69
  979.3 25.0 reduce-scatter.93
  1007.1 24.8 reduce-scatter.77
  1074.9 24.8 reduce-scatter.95
  1103.1 24.9 reduce-scatter.79
  1255.3 24.8 reduce-scatter.101
  1283.3 24.9 reduce-scatter.85
  1310.4 27.1 reduce-scatter.105
  1339.8 75.4 reduce-scatter.109
  1417.4 77.2 reduce-scatter.107
  1497.1 60.7 reduce-scatter.103
  1560.1 19.5 reduce-scatter.127
  1621.5 17.9 reduce-scatter.121
  1641.8 17.7 reduce-scatter.119
  1701.8 17.8 reduce-scatter.113
  1722.4 17.7 reduce-scatter.111
  1742.7 84.8 all-reduce.4
  (28 shorter events, 447.4 us)
where the time goes:
time: 1850 us; the launch traced here: 1840 us
  waiting for transfers between devices  986 us (53%)
  matrix products  382 us (21%)
  blocking collectives  331 us (18%)
  other arithmetic  66.7 us (4%)
  local copies, waits for them, and re-layouts  54.1 us (3%)
    unnamed x69, waiting for transfers between devices  168 us
    all_gather x8, waiting for transfers between devices, spread_rows(): return lax.all_gather(rows, 'tp', axis=0, tiled=True)  106 us
    reduce_scatter x8, waiting for transfers between devices, combine_grads(): lax.psum_scatter(partial_value.astype(jnp.bfloat16), 'tp', scatter_dimens...  103 us
    reduce_scatter x8, waiting for transfers between devices, combine_rows(): lax.psum_scatter(partial_value.astype(jnp.bfloat16), 'tp', scatter_dimens...  92.7 us
    dot_general x4, matrix products, backward_layer(): jnp.einsum('hqk,hqd->hkd', d_raw, query_heads, preferred_element_type=jnp...  89.9 us
    dot_general x4, matrix products, backward_layer(): jnp.einsum('hqk,hkd->hqd', d_raw, key_heads, preferred_element_type=jnp.f...  87.6 us
    all_gather x2, waiting for transfers between devices, fetch(): lax.all_gather(reduce_weight[layer_id], 'fsdp', axis=1, tiled=True)  83.4 us
    reduce_scatter x1, waiting for transfers between devices, local(): lax.psum_scatter(stacked[9].astype(jnp.bfloat16), 'fsdp', scatter_dimensi...  79.5 us
  transfers between devices with their start and end apart: 60, of which 42 were waited for; matrix products, arithmetic and copies ran while one was open for 23% of the time, Pallas kernels for 0%

commit v1 on v0

v1 whole, which is shorter than its diff:
```python
import functools
import math

import jax
import jax.numpy as jnp
from jax import lax
from jax.experimental import pallas as pl
from jax.experimental.pallas import tpu as pltpu
from jax.sharding import PartitionSpec as P

HD = 64
LAYERS = 2
LANES = 128
EPS = 1e-06
MASKED = -10000.0
SCALE = HD ** (-0.5)
VMEM_LIMIT = 60 * 1024 * 1024
F32 = jnp.float32
BF16 = jnp.bfloat16
VMEM = pltpu.VMEM
INV_SQRT2 = 1.0 / math.sqrt(2.0)
INV_SQRT_2PI = 1.0 / math.sqrt(2.0 * math.pi)


def mm(a, b):
    return lax.dot_general(a, b, (((1,), (0,)), ((), ())), preferred_element_type=F32)


def mm_nt(a, b):
    return lax.dot_general(a, b, (((1,), (1,)), ((), ())), preferred_element_type=F32)


def mm_tn(a, b):
    return lax.dot_general(a, b, (((0,), (0,)), ((), ())), preferred_element_type=F32)


def partners():
    t = lax.axis_index("tp")
    return t, t + 1 - 2 * (t % 2), (t + 2) % 4


def entry_barrier(sib, peer):
    barrier = pltpu.get_barrier_semaphore()
    for other in (sib, peer):
        pl.semaphore_signal(
            barrier, inc=1, device_id={"tp": other}, device_id_type=pl.DeviceIdType.MESH
        )
    pl.semaphore_wait(barrier, 2)


class Links:
    def __init__(self, send, recv, sib, peer):
        self.send, self.recv, self.sib, self.peer = send, recv, sib, peer

    def make(self, kind, s, src, dst, other):
        return pltpu.make_async_remote_copy(
            src_ref=src,
            dst_ref=dst,
            send_sem=self.send.at[kind, s],
            recv_sem=self.recv.at[kind, s],
            device_id={"tp": other},
            device_id_type=pl.DeviceIdType.MESH,
        )


def statistics(rows):
    mean = jnp.mean(rows, axis=-1, keepdims=True)
    centred = rows - mean
    inverse = lax.rsqrt(jnp.mean(centred * centred, axis=-1, keepdims=True) + EPS)
    return centred * inverse, inverse


def norm_back(rows, d_out, gain):
    unit, inverse = statistics(rows)
    e = d_out * gain
    back = inverse * (
        e
        - jnp.mean(e, axis=-1, keepdims=True)
        - unit * jnp.mean(e * unit, axis=-1, keepdims=True)
    )
    d_gain = jnp.sum(d_out * unit, axis=0, keepdims=True)
    d_shift = jnp.sum(d_out, axis=0, keepdims=True)
    return back, d_gain, d_shift


def rows_of(ref, b):
    block = ref[b]
    return block.reshape(block.shape[0] * block.shape[1], block.shape[2])


def gather_start(links, base, out, s):
    links.make(base, s, out.at[2 + s, 0], out.at[2 + s, 1], links.sib).start()
    links.make(base + 1, s, out.at[2 + s, 0], out.at[s, 0], links.peer).start()


def gather_end(links, base, out):
    for s in range(2):
        links.make(base + 1, s, out.at[2 + s, 0], out.at[s, 0], links.peer).wait_recv()
        links.make(base + 2, s, out.at[s, 0], out.at[s, 1], links.sib).start()
    for s in range(2):
        for kind, src, dst, other in (
            (base, out.at[2 + s, 0], out.at[2 + s, 1], links.sib),
            (base + 2, out.at[s, 0], out.at[s, 1], links.sib),
        ):
            links.make(kind, s, src, dst, other).wait()
        links.make(base + 1, s, out.at[2 + s, 0], out.at[s, 0], links.peer).wait_send()


class Scatter:
    def __init__(self, links, part, sent, got, own):
        self.links, self.part, self.sent, self.got, self.own = links, part, sent, got, own

    def copy(self, kind, s):
        other = self.links.peer if kind == 1 else self.links.sib
        return self.links.make(kind, s, self.sent.at[kind, s], self.got.at[kind, s], other)

    def block(self, b):
        s = b % 2
        half = self.part.shape[0] // 2

        @pl.when(b < 2)
        def _():
            self.sent[0, s] = self.part[half:].astype(BF16)
            first = self.copy(0, s)
            first.start()
            first.wait_recv()
            self.sent[1, s] = (self.part[:half] + self.got[0, s].astype(F32)).astype(BF16)
            self.copy(1, s).start()

        @pl.when(b >= 2)
        def _():
            self.sent[2, s] = self.part[half:].astype(BF16)
            self.copy(2, s).start()
            self.own[s] = self.part[:half]

    def total(self, s):
        self.copy(2, s).wait_recv()
        self.copy(1, s).wait_recv()
        return self.own[s] + self.got[2, s].astype(F32) + self.got[1, s].astype(F32)

    def end(self):
        for s in range(2):
            for kind in range(3):
                self.copy(kind, s).wait_send()


def scatter_scratch(half, width):
    return [
        VMEM((2 * half, width), F32),
        VMEM((3, 2, half, width), BF16),
        VMEM((3, 2, half, width), BF16),
        VMEM((2, half, width), F32),
        pltpu.SemaphoreType.DMA((6, 2)),
        pltpu.SemaphoreType.DMA((6, 2)),
    ]


def enter_kernel(tok, cot, gain, shift, first, grad, send, recv):
    t, sib, peer = partners()
    entry_barrier(sib, peer)
    links = Links(send, recv, sib, peer)
    for s in range(2):
        unit, _ = statistics(tok[s].astype(F32))
        first[2 + s, 0] = (unit * gain[...] + shift[...]).astype(BF16)
        gather_start(links, 0, first, s)
    for s in range(2):
        grad[2 + s, 0] = cot[s]
        gather_start(links, 3, grad, s)
    gather_end(links, 0, first)
    gather_end(links, 3, grad)


def pair_tile(pair, h):
    tile = pair if h % 2 == 0 else pltpu.roll(pair, HD, 1)
    return tile


def attention_kernel(
    heads,
    first, weight, q_bias, v_bias, key_extra, resid, out_bias, gain, shift,
    second, middle, q_out, k_out, v_out, mixed_out,
    part, sent, got, own, send, recv,
):
    t, sib, peer = partners()
    entry_barrier(sib, peer)
    links = Links(send, recv, sib, peer)
    scatter = Scatter(links, part, sent, got, own)
    width = heads * HD
    half = first.shape[2]
    rows = 2 * half
    lane = lax.broadcasted_iota(jnp.int32, (rows, LANES), 1)
    head_lane = lane < HD
    q_extra = jnp.where(lane < HD + 2, 1.0, 0.0).astype(BF16)
    v_extra = jnp.where(lane < HD + 3, 1.0, 0.0).astype(BF16)

    def project(b, carry):
        x = rows_of(first, b)
        y = mm(x, weight[:, : 3 * width])
        q = ((y[:, :width] + q_bias[...]).astype(BF16) * SCALE).astype(BF16)
        k = y[:, width : 2 * width].astype(BF16)
        v = (y[:, 2 * width :] + v_bias[...]).astype(BF16)
        g, s = b // 2, b % 2
        mine = jnp.where(g == 1, t, peer)
        other = mine + 1 - 2 * (mine % 2)
        extra = jnp.concatenate([key_extra[mine, s], key_extra[other, s]], axis=0)
        at = pl.ds(pl.multiple_of(b * rows, rows), rows)
        for h in range(heads):
            cut = slice(LANES * (h // 2), LANES * (h // 2 + 1))
            q_out[h, at, :] = jnp.where(head_lane, pair_tile(q[:, cut], h), q_extra)
            k_out[h, at, :] = jnp.where(head_lane, pair_tile(k[:, cut], h), extra)
            v_out[h, at, :] = jnp.where(head_lane, pair_tile(v[:, cut], h), v_extra)
        return carry

    lax.fori_loop(0, 4, project, 0)

    def attend(b, carry):
        at = pl.ds(pl.multiple_of(b * rows, rows), rows)
        outs = []
        for h in range(heads):
            q = q_out[h, at, :]
            scores = mm_nt(q, k_out[h])
            top = jnp.max(scores, axis=-1, keepdims=True)
            weights = jnp.exp(scores - top).astype(BF16)
            summed = mm(weights, v_out[h])
            total = summed[:, HD : HD + 1]
            outs.append(summed / total)
            log_total = -(top + jnp.log(total))
            high = log_total.astype(BF16).astype(F32)
            rest = log_total - high
            mid = rest.astype(BF16).astype(F32)
            low = rest - mid
            tail = jnp.where(lane == HD + 2, high, jnp.where(lane == HD + 3, mid, low))
            q_out[h, at, :] = jnp.where(
                (lane >= HD + 2) & (lane < HD + 5), tail.astype(BF16), q
            )
        tiles = [
            jnp.where(head_lane, outs[h], pltpu.roll(outs[h + 1], HD, 1))
            for h in range(0, heads, 2)
        ]
        mixed = jnp.concatenate(tiles, axis=1).astype(BF16)
        mixed_out[at, :] = mixed
        part[...] = mm_nt(mixed, weight[:, 3 * width :])
        scatter.block(b)
        return carry

    lax.fori_loop(0, 4, attend, 0)
    for s in range(2):
        mid = resid[s].astype(F32) + (scatter.total(s) + out_bias[...])
        middle[s] = mid
        unit, _ = statistics(mid)
        second[2 + s, 0] = (unit * gain[...] + shift[...]).astype(BF16)
        gather_start(links, 3, second, s)
    gather_end(links, 3, second)
    scatter.end()


def mlp_kernel(
    last,
    second, weight, bias, middle, out_bias, gain, shift,
    active_out, slope_out, resid, nxt,
    part, sent, got, own, send, recv,
):
    t, sib, peer = partners()
    entry_barrier(sib, peer)
    links = Links(send, recv, sib, peer)
    scatter = Scatter(links, part, sent, got, own)
    half = second.shape[2]
    rows = 2 * half
    hidden = bias.shape[1]
    step = 256

    def block(b, carry):
        at = pl.ds(pl.multiple_of(b * rows, rows), rows)
        x = rows_of(second, b)
        for n in range(0, hidden, step):
            before = mm(x, weight[:, n : n + step]) + bias[:, n : n + step]
            cdf = 0.5 * (1.0 + lax.erf(before * INV_SQRT2))
            active_out[at, n : n + step] = (before * cdf).astype(BF16)
            slope = cdf + before * (jnp.exp(before * before * -0.5) * INV_SQRT_2PI)
            slope_out[at, n : n + step] = slope.astype(BF16)
        part[...] = mm_nt(active_out[at, :], weight[:, hidden:])
        scatter.block(b)
        return carry

    lax.fori_loop(0, 4, block, 0)
    for s in range(2):
        res = middle[s] + (scatter.total(s) + out_bias[...])
        if last:
            nxt[s] = res.astype(BF16)
        else:
            resid[s] = res
            unit, _ = statistics(res)
            nxt[2 + s, 0] = (unit * gain[...] + shift[...]).astype(BF16)
            gather_start(links, 3, nxt, s)
    if not last:
        gather_end(links, 3, nxt)
    scatter.end()


def token_product(left, right, out, at, rows, offset):
    depth = left.shape[-1]
    total = left.shape[0] * left.shape[1] * left.shape[2]
    step = 256

    def body(j, carry):
        cut = pl.ds(pl.multiple_of(j * step, step), step)
        x = left[:, :, :, cut].reshape(total, step)
        out[cut, offset : offset + right.shape[-1]] = mm_tn(x, right[...]).astype(BF16)
        return carry

    lax.fori_loop(0, depth // step, body, 0)


def mlp_back_kernel(
    grad, weight, active, slope, second, middle, carry_in, gain,
    weight_grad, carry_out, rows_out, vectors,
    part, sent, got, own, send, recv, d_before,
):
    t, sib, peer = partners()
    entry_barrier(sib, peer)
    links = Links(send, recv, sib, peer)
    scatter = Scatter(links, part, sent, got, own)
    half = grad.shape[2]
    rows = 2 * half
    hidden = active.shape[1]
    step = 256
    vectors[...] = jnp.zeros_like(vectors)

    def block(b, carry):
        at = pl.ds(pl.multiple_of(b * rows, rows), rows)
        x = rows_of(grad, b)
        for n in range(0, hidden, step):
            d_act = mm(x, weight[:, hidden + n : hidden + n + step])
            d_bef = (d_act * slope[at, n : n + step].astype(F32)).astype(BF16)
            d_before[at, n : n + step] = d_bef
            vectors[4:5, n : n + step] += jnp.sum(d_bef.astype(F32), axis=0, keepdims=True)
        part[...] = mm_nt(d_before[at, :], weight[:, :hidden])
        scatter.block(b)
        return carry

    lax.fori_loop(0, 4, block, 0)
    token_product(grad, active, weight_grad, None, rows, hidden)

    def finish(s):
        back, d_gain, d_shift = norm_back(middle[s], scatter.total(s), gain[...])
        carry = carry_in[s].astype(F32)
        mid = carry + back
        carry_out[s] = mid
        low = mid.astype(BF16)
        rows_out[2 + s, 0] = low
        gather_start(links, 3, rows_out, s)
        vectors[0:1, :] += d_gain
        vectors[1:2, :] += d_shift
        vectors[2:3, :] += jnp.sum(low.astype(F32), axis=0, keepdims=True)
        vectors[3:4, :] += jnp.sum(carry.astype(BF16).astype(F32), axis=0, keepdims=True)

    finish(0)
    token_product(second, d_before, weight_grad, None, rows, 0)
    finish(1)
    gather_end(links, 3, rows_out)
    scatter.end()


def attention_back_kernel(
    heads, last,
    grad, weight, mixed, q_in, k_in, v_in, first, carry_in, resid, gain,
    weight_grad, carry_out, rows_out, vectors,
    part, sent, got, own, send, recv, d_out, d_joint, d_key, d_value,
):
    t, sib, peer = partners()
    entry_barrier(sib, peer)
    links = Links(send, recv, sib, peer)
    scatter = Scatter(links, part, sent, got, own)
    width = heads * HD
    half = grad.shape[2]
    rows = 2 * half
    lane = lax.broadcasted_iota(jnp.int32, (rows, LANES), 1)
    head_lane = lane < HD
    vectors[...] = jnp.zeros_like(vectors)
    d_key[...] = jnp.zeros_like(d_key)
    d_value[...] = jnp.zeros_like(d_value)

    def pairs(tiles):
        return jnp.concatenate(
            [
                jnp.where(head_lane, tiles[h], pltpu.roll(tiles[h + 1], HD, 1))
                for h in range(0, heads, 2)
            ],
            axis=1,
        )

    def attend(b, carry):
        at = pl.ds(pl.multiple_of(b * rows, rows), rows)
        d_mixed = mm(rows_of(grad, b), weight[:, 3 * width :]).astype(BF16)
        product = d_mixed.astype(F32) * mixed[at, :].astype(F32)
        d_queries = []
        for h in range(heads):
            cut = slice(LANES * (h // 2), LANES * (h // 2 + 1))
            keep = head_lane if h % 2 == 0 else lane >= HD
            delta = -jnp.sum(jnp.where(keep, product[:, cut], 0.0), axis=-1, keepdims=True)
            high = delta.astype(BF16).astype(F32)
            rest = delta - high
            mid = rest.astype(BF16).astype(F32)
            low = rest - mid
            tail = jnp.where(
                lane == HD,
                high,
                jnp.where(lane == HD + 1, mid, jnp.where(lane == HD + 2, low, 0.0)),
            ).astype(BF16)
            d_o = jnp.where(head_lane, pair_tile(d_mixed[:, cut], h), tail)
            q = q_in[h, at, :]
            probs = jnp.exp(mm_nt(k_in[h], q))
            d_value[h] += mm(probs.astype(BF16), d_o)
            d_raw = (probs * mm_nt(v_in[h], d_o)).astype(BF16)
            d_key[h] += mm(d_raw, q)
            d_queries.append(mm_tn(d_raw, k_in[h]) * SCALE)
        d_joint[at, :width] = pairs(d_queries).astype(BF16)
        return carry

    lax.fori_loop(0, 4, attend, 0)

    def project(b, carry):
        at = pl.ds(pl.multiple_of(b * rows, rows), rows)
        d_joint[at, width : 2 * width] = pairs([d_key[h, at, :] for h in range(heads)]).astype(BF16)
        d_joint[at, 2 * width :] = pairs([d_value[h, at, :] for h in range(heads)]).astype(BF16)
        d_rows = d_joint[at, :]
        sums = jnp.sum(d_rows.astype(F32), axis=0, keepdims=True)
        vectors[2:3, :width] += sums[:, :width]
        vectors[2:3, width : 2 * width] += sums[:, 2 * width :]
        part[...] = mm_nt(d_rows, weight[:, : 3 * width])
        scatter.block(b)
        return carry

    lax.fori_loop(0, 4, project, 0)
    token_product(grad, mixed, weight_grad, None, rows, 3 * width)

    def finish(s):
        back, d_gain, d_shift = norm_back(resid[s].astype(F32), scatter.total(s), gain[...])
        carry = carry_in[s] + back
        if last:
            rows_out[s] = carry.astype(BF16)
        else:
            carry_out[s] = carry
            rows_out[2 + s, 0] = carry.astype(BF16)
            gather_start(links, 3, rows_out, s)
        vectors[0:1, :] += d_gain
        vectors[1:2, :] += d_shift

    finish(0)
    token_product(first, d_joint, weight_grad, None, rows, 0)
    finish(1)
    if not last:
        gather_end(links, 3, rows_out)
    scatter.end()


def call(kernel, name, outs, scratch, collective_id, flops, args):
    size = sum(a.size * a.dtype.itemsize for a in args) + sum(
        math.prod(o.shape) * o.dtype.itemsize for o in outs
    )
    return pl.pallas_call(
        kernel,
        name=name,
        out_shape=tuple(outs),
        in_specs=[pl.BlockSpec(memory_space=VMEM)] * len(args),
        out_specs=tuple(pl.BlockSpec(memory_space=VMEM) for _ in outs),
        scratch_shapes=scratch,
        compiler_params=pltpu.CompilerParams(
            collective_id=collective_id, has_side_effects=True, vmem_limit_bytes=VMEM_LIMIT
        ),
        cost_estimate=pl.CostEstimate(flops=flops, bytes_accessed=size, transcendentals=0),
    )(*args)


def local(
    tokens, key_valid, first_gain, first_shift, joint_weight, query_bias, value_bias,
    out_weight, out_bias, second_gain, second_shift, expand_weight, expand_bias,
    reduce_weight, reduce_bias, cotangent,
):
    ctx_size = lax.axis_size("ctx")
    tp_size = lax.axis_size("tp")
    fsdp_size = lax.axis_size("fsdp")
    clips, half, dim = tokens.shape
    assert clips == ctx_size == 2 and tp_size == 4 and joint_weight.shape[0] == LAYERS
    c = lax.axis_index("ctx")
    t = lax.axis_index("tp")
    shard = joint_weight.shape[1]
    width = joint_weight.shape[3]
    heads = width // HD
    hidden = expand_weight.shape[2]
    swap = [(0, 1), (1, 0)]

    piece = shard // ctx_size

    def gathered(parts):
        packed = jnp.concatenate(parts, axis=1)
        mine = lax.dynamic_slice_in_dim(packed, c * piece, piece, 0)
        return lax.all_gather(mine, ("fsdp", "ctx"), axis=0, tiled=True)

    attn_weights, mlp_weights = [], []
    for l in range(LAYERS):
        joint = joint_weight[l]
        attn_weights.append(
            gathered([joint[:, 0], joint[:, 1], joint[:, 2], out_weight[l].T])
        )
        mlp_weights.append(gathered([expand_weight[l], reduce_weight[l].T]))

    wide = [first_gain, first_shift, out_bias, second_gain, second_shift, reduce_bias]
    narrow = [query_bias, value_bias, expand_bias]
    small = jnp.concatenate([a.reshape(-1) for a in wide + narrow])
    small = lax.all_gather(small, "fsdp", axis=0).astype(F32)
    params = []
    at = 0
    for a in wide:
        n = a.size
        got = small[:, at : at + n].reshape(fsdp_size, LAYERS, shard)
        params.append(got.transpose(1, 0, 2).reshape(LAYERS, 1, dim))
        at += n
    for a in narrow:
        n = a.size
        got = small[:, at : at + n].reshape(fsdp_size, *a.shape)
        params.append(got.transpose(1, 2, 0, 3).reshape(LAYERS, 1, a.shape[1] * HD))
        at += n
    g1, s1, ob, g2, s2, rb, qb, vb, eb = params

    def regroup(both):
        mine = lax.dynamic_index_in_dim(both, c, 0, keepdims=False)
        theirs = lax.dynamic_index_in_dim(both, 1 - c, 0, keepdims=False)
        got = lax.ppermute(theirs, "ctx", swap)
        return jnp.where(c == 0, jnp.stack([mine, got]), jnp.stack([got, mine]))

    tok = regroup(tokens)
    cot = regroup(cotangent)
    valid = lax.dynamic_index_in_dim(key_valid, c, 0, keepdims=False)
    bias = jnp.where(valid == 1, 0.0, MASKED).astype(F32)
    bias = bias.reshape(ctx_size, tp_size, half, 1).transpose(1, 0, 2, 3)
    high = bias.astype(BF16).astype(F32)
    col = lax.broadcasted_iota(jnp.int32, (1, 1, 1, LANES), 3) - HD
    key_extra = jnp.where(
        col == 0, high, jnp.where(col == 1, bias - high, jnp.where((col >= 2) & (col < 5), 1.0, 0.0))
    ).astype(BF16)

    every = jax.ShapeDtypeStruct((4, 2, half, dim), BF16)
    own = jax.ShapeDtypeStruct((2, half, dim), F32)
    own_low = jax.ShapeDtypeStruct((2, half, dim), BF16)
    count = 8 * half
    scratch = scatter_scratch(half, dim)

    first, grad = call(
        enter_kernel, "enter", [every, every],
        [pltpu.SemaphoreType.DMA((6, 2)), pltpu.SemaphoreType.DMA((6, 2))],
        0, 10**7, [tok, cot, g1[0], s1[0]],
    )
    resid = tok
    saved = []
    for l in range(LAYERS):
        heads_shape = jax.ShapeDtypeStruct((heads, count, LANES), BF16)
        second, middle, q, k, v, mixed = call(
            functools.partial(attention_kernel, heads), "attention",
            [every, own, heads_shape, heads_shape, heads_shape, jax.ShapeDtypeStruct((count, width), BF16)],
            scratch, 1 + 6 * l, 2 * count * dim * 4 * width + 16 * heads * count * count * HD,
            [first, attn_weights[l], qb[l], vb[l], key_extra, resid, ob[l], g2[l], s2[l]],
        )
        last = l == LAYERS - 1
        nxt_l = l if last else l + 1
        rows_hidden = jax.ShapeDtypeStruct((count, hidden), BF16)
        active, slope, out, nxt = call(
            functools.partial(mlp_kernel, last), "mlp_last" if last else "mlp",
            [rows_hidden, rows_hidden,
             jax.ShapeDtypeStruct((8, LANES), F32) if last else own, own_low if last else every],
            scratch, 2 + 6 * l, 4 * count * dim * hidden,
            [second, mlp_weights[l], eb[l], middle, rb[l], g1[nxt_l], s1[nxt_l]],
        )
        saved.append((resid, first, q, k, v, mixed, middle, second, active, slope))
        resid, first = out, nxt
    output = nxt

    vec = jax.ShapeDtypeStruct((8, dim), F32)
    carry = cot
    attn_grads, mlp_grads, attn_vec, mlp_vec = ([None] * LAYERS for _ in range(4))

    def reduced(full):
        part = lax.psum_scatter(full, ("fsdp", "ctx"), scatter_dimension=0, tiled=True)
        return lax.all_gather(part, "ctx", axis=0, tiled=True).astype(F32)

    for l in reversed(range(LAYERS)):
        resid, first, q, k, v, mixed, middle, second, active, slope = saved[l]
        w_grad, carry, grad, mlp_vec[l] = call(
            mlp_back_kernel, "mlp_back",
            [jax.ShapeDtypeStruct((dim, 2 * hidden), BF16), own, every, vec],
            scratch + [VMEM((count, hidden), BF16)], 3 + 6 * l, 8 * count * dim * hidden,
            [grad, mlp_weights[l], active, slope, second, middle, carry, g2[l]],
        )
        mlp_grads[l] = reduced(w_grad)
        last = l == 0
        w_grad, carry, grad, attn_vec[l] = call(
            functools.partial(attention_back_kernel, heads, last),
            "attention_back_last" if last else "attention_back",
            [jax.ShapeDtypeStruct((dim, 4 * width), BF16),
             jax.ShapeDtypeStruct((8, LANES), F32) if last else own, own_low if last else every, vec],
            scratch
            + [
                VMEM((heads, 8, LANES), BF16),
                VMEM((count, 3 * width), BF16),
                VMEM((heads, count, LANES), F32),
                VMEM((heads, count, LANES), F32),
            ],
            4 + 6 * l, 4 * count * dim * 4 * width + 40 * heads * count * count * HD,
            [grad, attn_weights[l], mixed, q, k, v, first, carry, resid, g1[l]],
        )
        attn_grads[l] = reduced(w_grad)
    row_grad = grad

    def ungroup(both):
        mine = lax.dynamic_index_in_dim(both, c, 0, keepdims=False)
        theirs = lax.dynamic_index_in_dim(both, 1 - c, 0, keepdims=False)
        got = lax.ppermute(theirs, "ctx", swap)
        return jnp.where(c == 0, jnp.stack([mine, got]), jnp.stack([got, mine]))

    pieces = []
    for l in range(LAYERS):
        pieces += [attn_vec[l][0], attn_vec[l][1], mlp_vec[l][2], mlp_vec[l][0], mlp_vec[l][1], mlp_vec[l][3]]
    flat = jnp.concatenate(pieces)
    slots = jnp.concatenate(
        [jnp.concatenate([attn_vec[l][2][: 2 * width], mlp_vec[l][4][:hidden]]) for l in range(LAYERS)]
    )
    placed = jnp.where(
        lax.broadcasted_iota(jnp.int32, (tp_size, 1), 0) == t, slots[None, :], 0.0
    )
    summed = lax.psum(jnp.concatenate([flat, placed.reshape(-1)]), ("fsdp", "ctx", "tp"))
    f = lax.axis_index("fsdp")
    rows = summed[: flat.size].reshape(LAYERS, 6, fsdp_size, shard)
    rows = lax.dynamic_index_in_dim(rows, f, 2, keepdims=False)
    mine = lax.dynamic_index_in_dim(summed[flat.size :].reshape(tp_size, -1), t, 0, keepdims=False)
    mine = mine.reshape(LAYERS, 2 * width + hidden)
    cut = HD // fsdp_size

    def spread(block, n):
        block = block.reshape(LAYERS, n // HD, fsdp_size, cut)
        return lax.dynamic_index_in_dim(block, f, 2, keepdims=False)

    joint = [g[:, : 3 * width].reshape(shard, 3, width) for g in attn_grads]
    return (
        ungroup(output),
        ungroup(row_grad),
        rows[:, 0],
        rows[:, 1],
        jnp.stack(joint),
        spread(mine[:, :width], width),
        spread(mine[:, width : 2 * width], width),
        jnp.stack([g[:, 3 * width :].T for g in attn_grads]),
        rows[:, 2],
        rows[:, 3],
        rows[:, 4],
        jnp.stack([g[:, :hidden] for g in mlp_grads]),
        spread(mine[:, 2 * width :], hidden),
        jnp.stack([g[:, hidden:].T for g in mlp_grads]),
        rows[:, 5],
    )


def solution(mesh):
    vector = P(None, "fsdp")
    by_head = P(None, "tp", "fsdp")
    rows = P("fsdp", ("ctx", "tp"), None)
    return jax.shard_map(
        local,
        mesh=mesh,
        in_specs=(
            rows, P("fsdp", None), vector, vector, P(None, "fsdp", None, "tp"), by_head, by_head,
            by_head, vector, vector, vector, P(None, "fsdp", "tp"), by_head, by_head, vector, rows,
        ),
        out_specs=(
            rows, rows, vector, vector, P(None, "fsdp", None, "tp"), by_head, by_head,
            by_head, vector, vector, vector, P(None, "fsdp", "tp"), by_head, by_head, vector,
        ),
        check_vma=False,
    )
```

time: 1850 us -> 966 us (0.52)
  waiting for transfers between devices: 986 us -> 529 us
  matrix products: 382 us -> 0 us
  Pallas kernels: 0 us -> 330 us
  blocking collectives: 331 us -> 28.5 us
  other arithmetic: 66.7 us -> 17 us
    dot_general x72 -> x0, matrix products: 382 us -> none  [the longest x4 89.9 us: backward_layer(): jnp.einsum('hqk,hqd->hkd', d_raw, query_heads, preferred_element_type=jnp...]
    pallas_call x0 -> x9, Pallas kernels: none -> 330 us  [call(): pl.pallas_call(kernel, name=name, out_shape=tuple(outs), in_specs=[pl.Blo...]
    all_gather x28 -> x3, blocking collectives: 300 us -> 28.5 us  [the longest x2 14.6 us: reduced(): return lax.all_gather(part, 'ctx', axis=0, tiled=True).astype(F32)]
    all_gather x22 -> x6, waiting for transfers between devices: 326 us -> 110 us  [the longest x4 71.8 us: gathered(): return lax.all_gather(mine, ('fsdp', 'ctx'), axis=0, tiled=True)]
    unnamed x69 -> x11, waiting for transfers between devices: 168 us -> 2.69 us
    reduce_scatter x28 -> x4, waiting for transfers between devices: 428 us -> 303 us  [reduced(): lax.psum_scatter(full, ('fsdp', 'ctx'), scatter_dimension=0, tiled=True)]
    psum x1, waiting for transfers between devices: 63.7 us -> 114 us  [local(): lax.psum(jnp.concatenate([flat, placed.reshape(-1)]), ('fsdp', 'ctx', 'tp'))]
    reduce_sum x32 -> x0, other arithmetic: 37.6 us -> none  [the longest x6 9.09 us: norm_rows(): return centred * lax.rsqrt(spread + epsilon) * gain + shift]
  transfers between devices with their start and end apart: 60 -> 15, of which waited for: 42 -> 10; matrix products, arithmetic and copies ran while one was open for 23% -> 4% of each run, Pallas kernels for 0% -> 15%
where the time goes in v1:
time: 966 us; the launch traced here: 961 us
  waiting for transfers between devices  529 us (55%)
  Pallas kernels  330 us (34%)
  local copies, waits for them, and re-layouts  35.7 us (4%)
  blocking collectives  28.5 us (3%)
  other arithmetic  17 us (2%)
  between operations  15.2 us (2%)
    pallas_call x9, Pallas kernels, call(): pl.pallas_call(kernel, name=name, out_shape=tuple(outs), in_specs=[pl.Blo...  330 us
    reduce_scatter x4, waiting for transfers between devices, reduced(): lax.psum_scatter(full, ('fsdp', 'ctx'), scatter_dimension=0, tiled=True)  303 us
    psum x1, waiting for transfers between devices, local(): lax.psum(jnp.concatenate([flat, placed.reshape(-1)]), ('fsdp', 'ctx', 'tp'))  114 us
    all_gather x4, waiting for transfers between devices, gathered(): return lax.all_gather(mine, ('fsdp', 'ctx'), axis=0, tiled=True)  71.8 us
    all_gather x2, waiting for transfers between devices, reduced(): return lax.all_gather(part, 'ctx', axis=0, tiled=True).astype(F32)  37.9 us
  transfers between devices with their start and end apart: 15, of which 10 were waited for; matrix products, arithmetic and copies ran while one was open for 4% of the time, Pallas kernels for 15%

profile of v1, /device:TPU:0, one launch (start us, length us, event | category | flops | bytes accessed | tf_op | source)
XLA Modules:
  0.0 961.0 jit_solution(16226749882505553120)
XLA Ops:
  8.4 1.7 fusion.12
  11.0 1.7 fusion.7
  16.3 3.0 collective-permute-start
  21.7 13.9 %all-gather.1 = bf16[4,1,3840]{2,1,0:T(2,128)(2,1)S(1)} all-gather(bf16[1,1,3840]{2,1,0:T(2,128)(2,1)S(1)} %reshape.235), channel_id=2, replica_groups=mesh['fsdp'=4,'ctx'=2,'tp'=4] {'fsdp'}, dimensions={0}, use_global_device_ids=true | all-gather | bytes 38400 | tf_op jit(solution)/shard_map/all_gather | solution.py:511
  50.1 30.2 %enter.1 = (bf16[4,2,128,1024]{3,2,1,0:T(8,128)(2,1)}, bf16[4,2,128,1024]{3,2,1,0:T(8,128)(2,1)}) custom-call(bf16[2,128,1024]{2,1,0:T(8,128)(2,1)} %maximum_select_fusion.tok.resid, bf16[2,128,1024]{2,1,0:T(8,128)(2,1)} %maximum_select_fusion.1.cot.carry_in, f32[1,1024]{1,0:T(1,128)} %bitcast.214, f32[1,1024]{1,0:T(1,128)} %bitcast.216), custom_call_target="tpu_custom_call" | custom-call | flops 10000000 | bytes 5251072 | tf_op jit(solution)/shard_map/enter/pallas_call | solution.py:461
  80.3 38.9 %attention.2 = (bf16[4,2,128,1024]{3,2,1,0:T(8,128)(2,1)}, f32[2,128,1024]{2,1,0:T(8,128)}, bf16[4,1024,128]{2,1,0:T(8,128)(2,1)}, bf16[4,1024,128]{2,1,0:T(8,12...) custom-call(bf16[4,2,128,1024]{3,2,1,0:T(8,128)(2,1)} %get-tuple-element.51.first, ...), custom_call_target="tpu_custom_call" | custom-call | flops 6442450944 | bytes 11810816 | tf_op jit(solution)/shard_map/attention/pallas_call | solution.py:461
  119.2 22.9 %all-gather.11.cloned.1.call-done.weight = bf16[1024,2048]{1,0:T(8,128)(2,1)} async-done(((bf16[128,2048]{1,0:T(8,128)(2,1)}), bf16[1024,2048]{1,0:T(8,128)(2,1)}) %all-gather.11.cloned.1.call-update) | async-done | bytes 4194320 | tf_op jit(solution)/shard_map/all_gather | solution.py:498
  142.1 36.3 %mlp.1 = (bf16[1024,1024]{1,0:T(8,128)(2,1)}, bf16[1024,1024]{1,0:T(8,128)(2,1)}, f32[2,128,1024]{2,1,0:T(8,128)}, bf16[4,2,128,1024]{3,2,1,0:T(8,128)(2,1)}) custom-call(bf16[4,2,128,1024]{3,2,1,0:T(8,128)(2,1)} %get-tuple-element.52.second, bf16[1024,2048]{1,0:T(8,128)(2,1)} %all-gather.11.cloned.1.call-done.weight, f32[1,1024]{1,0:T(1,128)} %squeeze.216.bias, ...), custom_call_target="tpu_custom_call" | custom-call | flops 4294967296 | bytes 14696448 | tf_op jit(solution)/shard_map/mlp/pallas_call | solution.py:461
  178.4 13.4 %all-gather.13.cloned.1.call-done.weight = bf16[1024,1024]{1,0:T(8,128)(2,1)} async-done(((bf16[128,1024]{1,0:T(8,128)(2,1)}), bf16[1024,1024]{1,0:T(8,128)(2,1)}) %all-gather.13.cloned.1.call-update) | async-done | bytes 2097168 | tf_op jit(solution)/shard_map/all_gather | solution.py:498
  191.8 39.0 %attention.3 = (bf16[4,2,128,1024]{3,2,1,0:T(8,128)(2,1)}, f32[2,128,1024]{2,1,0:T(8,128)}, bf16[4,1024,128]{2,1,0:T(8,128)(2,1)}, bf16[4,1024,128]{2,1,0:T(8,12...) custom-call(bf16[4,2,128,1024]{3,2,1,0:T(8,128)(2,1)} %get-tuple-element.54.first, ...), custom_call_target="tpu_custom_call" | custom-call | flops 6442450944 | bytes 12335104 | tf_op jit(solution)/shard_map/attention/pallas_call | solution.py:461
  230.8 35.5 %all-gather.15.cloned.1.call-done.weight = bf16[1024,2048]{1,0:T(8,128)(2,1)} async-done(((bf16[128,2048]{1,0:T(8,128)(2,1)}), bf16[1024,2048]{1,0:T(8,128)(2,1)}) %all-gather.15.cloned.1.call-update) | async-done | bytes 4194320 | tf_op jit(solution)/shard_map/all_gather | solution.py:498
  266.3 23.1 %mlp_last.1 = (bf16[1024,1024]{1,0:T(8,128)(2,1)}, bf16[1024,1024]{1,0:T(8,128)(2,1)}, f32[8,128]{1,0:T(8,128)}, bf16[2,128,1024]{2,1,0:T(8,128)(2,1)}) custom-call(bf16[4,2,128,1024]{3,2,1,0:T(8,128)(2,1)} %get-tuple-element.56.second, bf16[1024,2048]{1,0:T(8,128)(2,1)} %all-gather.15.cloned.1.call-done.weight, f32[1,1024]{1,0:T(1,128)} %squeeze.232.bias, ...), custom_call_target="tpu_custom_call" | custom-call | flops 4294967296 | bytes 12079104 | tf_op jit(solution)/shard_map/mlp_last/pallas_call | solution.py:461
  289.4 37.5 %mlp_back.2 = (bf16[1024,2048]{1,0:T(8,128)(2,1)}, f32[2,128,1024]{2,1,0:T(8,128)}, bf16[4,2,128,1024]{3,2,1,0:T(8,128)(2,1)}, f32[8,1024]{1,0:T(8,128)}) custom-call(bf16[4,2,128,1024]{3,2,1,0:T(8,128)(2,1)} %get-tuple-element.59.grad, bf16[1024,2048]{1,0:T(8,128)(2,1)} %all-gather.15.cloned.1.call-done.weight, ...), custom_call_target="tpu_custom_call" | custom-call | flops 8589934592 | bytes 21532672 | tf_op jit(solution)/shard_map/mlp_back/pallas_call | solution.py:461
  326.9 50.1 %attention_back.1 = (bf16[1024,1024]{1,0:T(8,128)(2,1)}, f32[2,128,1024]{2,1,0:T(8,128)}, bf16[4,2,128,1024]{3,2,1,0:T(8,128)(2,1)}, f32[8,1024]{1,0:T(8,128)}) custom-call(bf16[4,2,128,1024]{3,2,1,0:T(8,128)(2,1)} %get-tuple-element.62.grad, bf16[1024,1024]{1,0:T(8,128)(2,1)} %all-gather.13.cloned.1.call-done.weight, ...), custom_call_target="tpu_custom_call" | custom-call | flops 15032385536 | bytes 17338368 | tf_op jit(solution)/shard_map/attention_back/pallas_call | solution.py:461
  378.6 37.9 %mlp_back.3 = (bf16[1024,2048]{1,0:T(8,128)(2,1)}, f32[2,128,1024]{2,1,0:T(8,128)}, bf16[4,2,128,1024]{3,2,1,0:T(8,128)(2,1)}, f32[8,1024]{1,0:T(8,128)}) custom-call(bf16[4,2,128,1024]{3,2,1,0:T(8,128)(2,1)} %get-tuple-element.68.grad, bf16[1024,2048]{1,0:T(8,128)(2,1)} %all-gather.11.cloned.1.call-done.weight, ...), custom_call_target="tpu_custom_call" | custom-call | flops 8589934592 | bytes 22056960 | tf_op jit(solution)/shard_map/mlp_back/pallas_call | solution.py:461
  416.5 37.2 %attention_back_last.1 = (bf16[1024,1024]{1,0:T(8,128)(2,1)}, f32[8,128]{1,0:T(8,128)}, bf16[2,128,1024]{2,1,0:T(8,128)(2,1)}, f32[8,1024]{1,0:T(8,128)}) custom-call(bf16[4,2,128,1024]{3,2,1,0:T(8,128)(2,1)} %get-tuple-element.72.grad, bf16[1024,1024]{1,0:T(8,128)(2,1)} %all-gather.9.cloned.1.call-done.weight, bf16[1024,256]{1,0:T(8,128)(2,1)} %get-tuple-element.73.mixed, ...), custom_call_target="tpu_custom_call" | custom-call | flops 15032385536 | bytes 14196736 | tf_op jit(solution)/shard_map/attention_back_last/pallas_call | solution.py:461
  460.2 1.5 collective-permute-start.3
  461.7 113.7 %all-reduce.2.cloned.1.call-done = f32[24576]{0:T(1024)} async-done(((f32[24576]{0:T(1024)}), f32[24576]{0:T(1024)}) %all-reduce.2.cloned.1.call-update) | async-done | bytes 98320 | tf_op jit(solution)/shard_map/psum | solution.py:630
  576.5 91.3 %reduce-scatter.11.cloned.1.call-done = bf16[128,2048]{1,0:T(8,128)(2,1)} async-done(((bf16[1024,2048]{1,0:T(8,128)(2,1)}), bf16[128,2048]{1,0:T(8,128)(2,1)}) %reduce-scatter.11.cloned.1.call-update) | async-done | bytes 524304 | tf_op jit(solution)/shard_map/reduce_scatter | solution.py:583
  672.3 67.1 %reduce-scatter.7.cloned.1.call-done = bf16[128,1024]{1,0:T(8,128)(2,1)} async-done(((bf16[1024,1024]{1,0:T(8,128)(2,1)}), bf16[128,1024]{1,0:T(8,128)(2,1)}) %reduce-scatter.7.cloned.1.call-update) | async-done | bytes 262160 | tf_op jit(solution)/shard_map/reduce_scatter | solution.py:583
  739.4 7.2 all_gather.37
  747.7 62.2 %reduce-scatter.5.cloned.1.call-done = bf16[128,1024]{1,0:T(8,128)(2,1)} async-done(((bf16[1024,1024]{1,0:T(8,128)(2,1)}), bf16[128,1024]{1,0:T(8,128)(2,1)}) %reduce-scatter.5.cloned.1.call-update) | async-done | bytes 262160 | tf_op jit(solution)/shard_map/reduce_scatter | solution.py:583
  809.9 7.3 all_gather.36
  819.0 81.9 %reduce-scatter.9.cloned.1.call-done = bf16[128,2048]{1,0:T(8,128)(2,1)} async-done(((bf16[1024,2048]{1,0:T(8,128)(2,1)}), bf16[128,2048]{1,0:T(8,128)(2,1)}) %reduce-scatter.9.cloned.1.call-update) | async-done | bytes 524304 | tf_op jit(solution)/shard_map/reduce_scatter | solution.py:583
  901.1 1.6 copy.105
  905.7 17.7 %all-gather.19.cloned.1.call-done = bf16[256,2048]{1,0:T(8,128)(2,1)} async-done(((bf16[128,2048]{1,0:T(8,128)(2,1)}), bf16[256,2048]{1,0:T(8,128)(2,1)}) %all-gather.19.cloned.1.call-update) | async-done | bytes 1048592 | tf_op jit(solution)/shard_map/all_gather | solution.py:584
  923.4 1.5 convert_element_type.35
  926.0 20.3 %all-gather.17.cloned.1.call-done = bf16[256,2048]{1,0:T(8,128)(2,1)} async-done(((bf16[128,2048]{1,0:T(8,128)(2,1)}), bf16[256,2048]{1,0:T(8,128)(2,1)}) %all-gather.17.cloned.1.call-update) | async-done | bytes 1048592 | tf_op jit(solution)/shard_map/all_gather | solution.py:584
  946.3 1.5 convert_element_type.34
  947.8 1.2 slice_bitcast_fusion.1
  949.5 1.8 copy.107
  951.3 2.7 pad_maximum_fusion
  (207 shorter events, 42.9 us)
Async XLA Ops:
  7.2 73.1 %all-gather.9.cloned.1.call-start = ((), (), s32[]{:S(2)}) async-start(), calls=%async_computation.4 | async-start | bytes 2359296 | tf_op jit(solution)/shard_map/all_gather | solution.py:498
  8.4 4.3 copy-start.1
  11.0 2.1 copy-start.2
  12.7 129.4 %all-gather.11.cloned.1.call-start = ((), (), s32[]{:S(2)}) async-start(), calls=%async_computation.5 | async-start | bytes 4718592 | tf_op jit(solution)/shard_map/all_gather | solution.py:498
  14.0 177.8 %all-gather.13.cloned.1.call-start = ((), (), s32[]{:S(2)}) async-start(), calls=%async_computation.6 | async-start | bytes 2359296 | tf_op jit(solution)/shard_map/all_gather | solution.py:498
  14.1 2.1 copy-start.3
  14.9 251.3 %all-gather.15.cloned.1.call-start = ((), (), s32[]{:S(2)}) async-start(), calls=%async_computation.7 | async-start | bytes 4718592 | tf_op jit(solution)/shard_map/all_gather | solution.py:498
  15.0 4.3 copy-start.4
  15.2 4.2 copy-start.15
  15.2 4.2 copy-start.16
  15.2 4.3 copy-start.17
  15.2 4.3 copy-start.18
  15.3 4.3 copy-start.19
  15.3 4.3 copy-start.20
  15.3 4.3 copy-start.12
  15.3 4.4 copy-start.13
  15.3 4.5 copy-start.11
  15.3 20.5 %copy-start.14 = (s32[2,1024]{1,0:T(2,128)S(1)}, s32[2,1024]{1,0:T(2,128)}, u32[]{:S(2)}) copy-start(s32[2,1024]{1,0:T(2,128)} %param.17) | copy-start | bytes 24580
  16.2 559.2 %all-reduce.2.cloned.1.call-start = ((), (), s32[]{:S(2)}) async-start(), calls=%async_computation.8 | async-start | bytes 196608 | tf_op jit(solution)/shard_map/psum | solution.py:630
  16.3 32.0 %collective-permute-start = (bf16[128,1024]{1,0:T(8,128)(2,1)S(1)}, bf16[128,1024]{1,0:T(8,128)(2,1)S(1)}, u32[]{:S(2)}, u32[]{:S(2)}) collective-permute-start(bf16[128,1024]{1,0:T(8,128)(2,1)S(1)} %get-tuple-element.164), channel_id=1, source_target_pairs={{0,4},{4,0},{1,5},{5,1},{2,6},{6,2},{3,7},{7,3},{8,12},{12,8},{9,1... | collective-permute-start | bytes 786440 | tf_op jit(solution)/shard_map/ppermute | solution.py:529
  19.4 29.9 %collective-permute-start.1 = (bf16[128,1024]{1,0:T(8,128)(2,1)S(1)}, bf16[128,1024]{1,0:T(8,128)(2,1)S(1)}, u32[]{:S(2)}, u32[]{:S(2)}) collective-permute-start(bf16[128,1024]{1,0:T(8,128)(2,1)S(1)} %get-tuple-element.162), channel_id=1, source_target_pairs={{0,4},{4,0},{1,5},{5,1},{2,6},{6,2},{3,7},{7,3},{8,12},{12,8},{9,1... | collective-permute-start | bytes 786440 | tf_op jit(solution)/shard_map/ppermute | solution.py:529
  416.5 38.8 %copy-start.10 = (f32[8,1024]{1,0:T(8,128)S(1)}, f32[8,1024]{1,0:T(8,128)}, u32[]{:S(2)}) copy-start(f32[8,1024]{1,0:T(8,128)} %get-tuple-element.80) | copy-start | bytes 98308
  416.5 38.8 %copy-start.9 = (f32[8,1024]{1,0:T(8,128)S(1)}, f32[8,1024]{1,0:T(8,128)}, u32[]{:S(2)}) copy-start(f32[8,1024]{1,0:T(8,128)} %get-tuple-element.82) | copy-start | bytes 98308
  456.3 211.5 %reduce-scatter.11.cloned.1.call-start = ((), (), s32[]{:S(2)}) async-start(), calls=%async_computation.13 | async-start | bytes 4718592 | tf_op jit(solution)/shard_map/reduce_scatter | solution.py:583
  456.9 282.5 %reduce-scatter.7.cloned.1.call-start = ((), (), s32[]{:S(2)}) async-start(), calls=%async_computation.10 | async-start | bytes 2359296 | tf_op jit(solution)/shard_map/reduce_scatter | solution.py:583
  457.6 352.3 %reduce-scatter.5.cloned.1.call-start = ((), (), s32[]{:S(2)}) async-start(), calls=%async_computation.9 | async-start | bytes 2359296 | tf_op jit(solution)/shard_map/reduce_scatter | solution.py:583
  458.4 442.5 %reduce-scatter.9.cloned.1.call-start = ((), (), s32[]{:S(2)}) async-start(), calls=%async_computation.11 | async-start | bytes 4718592 | tf_op jit(solution)/shard_map/reduce_scatter | solution.py:583
  458.4 1.7 copy-start.6
  459.1 464.3 %all-gather.19.cloned.1.call-start = ((), (), s32[]{:S(2)}) async-start(), calls=%async_computation.14 | async-start | bytes 1572864 | tf_op jit(solution)/shard_map/all_gather | solution.py:584
  459.5 211.0 %collective-permute-start.2 = (bf16[128,1024]{1,0:T(8,128)(2,1)S(1)}, bf16[128,1024]{1,0:T(8,128)(2,1)S(1)}, u32[]{:S(2)}, u32[]{:S(2)}) collective-permute-start(bf16[128,1024]{1,0:T(8,128)(2,1)S(1)} %get-tuple-element.160), channel_id=1, source_target_pairs={{0,4},{4,0},{1,5},{5,1},{2,6},{6,2},{3,7},{7,3},{8,12},{12,8},{9,1... | collective-permute-start | bytes 786440 | tf_op jit(solution)/shard_map/ppermute | solution.py:617
  460.2 211.2 %collective-permute-start.3 = (bf16[128,1024]{1,0:T(8,128)(2,1)S(1)}, bf16[128,1024]{1,0:T(8,128)(2,1)S(1)}, u32[]{:S(2)}, u32[]{:S(2)}) collective-permute-start(bf16[128,1024]{1,0:T(8,128)(2,1)S(1)} %get-tuple-element.158), channel_id=1, source_target_pairs={{0,4},{4,0},{1,5},{5,1},{2,6},{6,2},{3,7},{7,3},{8,12},{12,8},{9,1... | collective-permute-start | bytes 786440 | tf_op jit(solution)/shard_map/ppermute | solution.py:617
  667.8 278.5 %all-gather.17.cloned.1.call-start = ((), (), s32[]{:S(2)}) async-start(), calls=%async_computation.12 | async-start | bytes 1572864 | tf_op jit(solution)/shard_map/all_gather | solution.py:584
  (4 other events, 4.2 us)
Sparse Core Ops, SparseCore 0:
  12.8 54.6 all-gather.8
  70.2 71.8 all-gather.10
  144.2 47.5 all-gather.12
  194.4 71.8 all-gather.14
  456.4 118.9 all-reduce.1
  578.9 88.8 reduce-scatter.10
  671.8 67.5 reduce-scatter.6
  743.3 66.5 reduce-scatter.4
  814.0 86.8 reduce-scatter.8
  902.3 21.0 all-gather.18
  925.0 21.2 all-gather.16

commit v2 on v1

--- a/solution.py
+++ b/solution.py
@@ -39,13 +39,469 @@
     return t, t + 1 - 2 * (t % 2), (t + 2) % 4
 
 
-def entry_barrier(sib, peer):
+def entry_barrier(jobs=()):
+    t, sib, peer = partners()
+    others = [{"tp": sib}, {"tp": peer}]
+    if any(job.uses_ctx for job in jobs):
+        others.append({"ctx": 1 - lax.axis_index("ctx")})
+    if any(job.uses_fsdp for job in jobs):
+        n = lax.axis_size("fsdp")
+        z = lax.axis_index("fsdp")
+        others += [{"fsdp": (z + k) % n} for k in range(1, n)]
     barrier = pltpu.get_barrier_semaphore()
-    for other in (sib, peer):
-        pl.semaphore_signal(
-            barrier, inc=1, device_id={"tp": other}, device_id_type=pl.DeviceIdType.MESH
-        )
-    pl.semaphore_wait(barrier, 2)
+    for other in others:
+        pl.semaphore_signal(barrier, inc=1, device_id=other, device_id_type=pl.DeviceIdType.MESH)
+    pl.semaphore_wait(barrier, len(others))
+
+
+def remote(src, dst, send, recv, device):
+    return pltpu.make_async_remote_copy(
+        src_ref=src,
+        dst_ref=dst,
+        send_sem=send,
+        recv_sem=recv,
+        device_id=device,
+        device_id_type=pl.DeviceIdType.MESH,
+    )
+
+
+DMA = pltpu.SemaphoreType.DMA
+HBM_SPEC = pl.BlockSpec(memory_space=pl.ANY)
+VMEM_SPEC = pl.BlockSpec(memory_space=VMEM)
+
+
+class Job:
+    uses_ctx = False
+    uses_fsdp = False
+    ins = ()
+    outs = ()
+    scratch = ()
+
+    def bind(self, ins, outs, scratch):
+        self.c = lax.axis_index("ctx")
+        self.z = lax.axis_index("fsdp")
+        self.refs(ins, outs, scratch)
+
+    def start(self):
+        pass
+
+    def steps(self):
+        return []
+
+    def end(self):
+        pass
+
+
+def chunks_of(rows):
+    return 2 if rows % 128 == 0 else 1
+
+
+class WeightGather(Job):
+    uses_ctx = uses_fsdp = True
+
+    def __init__(self, packed, n, hooks):
+        self.n, self.hooks = n, hooks
+        self.ins = [(packed, HBM_SPEC)]
+        self.outs = [(jax.ShapeDtypeStruct((n, *packed.shape), BF16), HBM_SPEC)]
+        self.rows = packed.shape[1]
+        self.ch = chunks_of(self.rows)
+        self.scratch = [DMA((max(n, 5), self.ch))] + [DMA((n, self.ch))] * 3 + [DMA]
+
+    def refs(self, ins, outs, scratch):
+        (self.src,), (self.out,) = ins, outs
+        self.z_send, self.z_recv, self.x_send, self.x_recv, self.near = scratch
+
+    def cut(self, ref, ch):
+        size = self.rows // self.ch
+        return ref.at[pl.ds(ch * size, size)]
+
+    def over_z(self, k, ch, to):
+        return remote(
+            self.cut(self.src.at[self.c], ch), self.cut(self.out.at[self.z, self.c], ch),
+            self.z_send.at[k, ch], self.z_recv.at[self.z, ch], {"fsdp": to},
+        )
+
+    def arrived(self, frm, ch):
+        block = self.cut(self.out.at[frm, self.c], ch)
+        return remote(block, block, self.z_send.at[4, ch], self.z_recv.at[frm, ch], {"fsdp": 3 - frm})
+
+    def over_x(self, frm, half, ch):
+        block = self.cut(self.out.at[frm, half], ch)
+        return remote(
+            block, block, self.x_send.at[frm, ch], self.x_recv.at[frm, ch], {"ctx": 1 - self.c}
+        )
+
+    def copy_near(self):
+        return pltpu.make_async_copy(self.src, self.out.at[self.z], self.near)
+
+    def offsets(self):
+        if self.n == 4:
+            return [(k, off) for k, off in enumerate((1, -1, 2, -2))]
+        return [(k, k) for k in range(1, self.n)]
+
+    def inside(self, off):
+        other = self.z + off
+        return (other >= 0) & (other < self.n) if self.n == 4 else (other > -1)
+
+    def start(self):
+        for ch in range(self.ch):
+            for k, off in self.offsets():
+                @pl.when(self.inside(off))
+                def _():
+                    self.over_z(k, ch, (self.z + off + self.n) % self.n).start()
+        self.copy_near().start()
+
+    def take(self, off):
+        frm = (self.z + off + self.n) % self.n
+
+        @pl.when(self.inside(off))
+        def _():
+            for ch in range(self.ch):
+                self.arrived(frm, ch).wait_recv()
+                if self.n == 4 and abs(off) == 2:
+                    @pl.when((self.z == 2) & (frm == 0) | (self.z == 1) & (frm == 3))
+                    def _():
+                        self.arrived(frm, ch).start()
+                self.over_x(frm, self.c, ch).start()
+
+    def steps(self):
+        if self.n == 4:
+            groups = [(1, -1), (2, -2), (3, -3)]
+        else:
+            groups = [tuple(range(1, self.n))]
+        out = []
+        for hook, group in zip(self.hooks, groups):
+            for off in group:
+                out.append((hook, functools.partial(self.take, off)))
+        return out
+
+    def end(self):
+        for ch in range(self.ch):
+            for off in (1, -1, 2, -2, 3, -3) if self.n == 4 else range(1, self.n):
+                frm = (self.z + off + self.n) % self.n
+
+                @pl.when(self.inside(off))
+                def _():
+                    self.over_x(frm, 1 - self.c, ch).wait_recv()
+                    self.over_x(frm, self.c, ch).wait_send()
+            for k, off in self.offsets():
+                @pl.when(self.inside(off))
+                def _():
+                    self.over_z(k, ch, (self.z + off + self.n) % self.n).wait_send()
+            if self.n == 4:
+                @pl.when((self.z == 1) | (self.z == 2))
+                def _():
+                    self.arrived(jnp.where(self.z == 2, 0, 3), ch).wait_send()
+        self.copy_near().wait()
+
+
+class Exchange(Job):
+    uses_ctx = True
+
+    def __init__(self, both):
+        self.ins = [(both, VMEM_SPEC)]
+        self.outs = [(jax.ShapeDtypeStruct(both.shape, both.dtype), VMEM_SPEC)]
+        self.scratch = [DMA, DMA]
+
+    def refs(self, ins, outs, scratch):
+        (self.src,), (self.out,), (self.ssem, self.rsem) = ins, outs, scratch
+
+    def copy(self):
+        c = self.c
+        return remote(self.src.at[1 - c], self.out.at[c], self.ssem, self.rsem, {"ctx": 1 - c})
+
+    def start(self):
+        self.copy().start()
+        self.out[self.c] = self.src[self.c]
+
+    def end(self):
+        self.copy().wait()
+
+
+class RowGather(Job):
+    def __init__(self, own, hook):
+        self.hook = hook
+        self.ins = [(own, VMEM_SPEC)]
+        self.outs = [(jax.ShapeDtypeStruct((4, 2, *own.shape[1:]), own.dtype), VMEM_SPEC)]
+        self.scratch = [DMA((3, 2)), DMA((3, 2))]
+
+    def refs(self, ins, outs, scratch):
+        (self.src,), (self.out,) = ins, outs
+        t, sib, peer = partners()
+        self.links = Links(*scratch, sib, peer)
+
+    def start(self):
+        for s in range(2):
+            self.out[2 + s, 0] = self.src[s]
+            gather_start(self.links, 0, self.out, s)
+
+    def steps(self):
+        return [(self.hook, lambda: gather_forward(self.links, 0, self.out))]
+
+    def end(self):
+        gather_wait(self.links, 0, self.out)
+
+
+class ParamSum(Job):
+    uses_fsdp = True
+
+    def __init__(self, placed, n):
+        self.n = n
+        self.ins = [(placed, VMEM_SPEC)]
+        self.outs = [(jax.ShapeDtypeStruct(placed.shape, F32), VMEM_SPEC)]
+        self.scratch = [VMEM((n, *placed.shape), BF16), DMA((n,)), DMA((n,))]
+
+    def refs(self, ins, outs, scratch):
+        (self.src,), (self.out,), (self.got, self.ssem, self.rsem) = ins, outs, scratch
+
+    def copy(self, k):
+        return remote(
+            self.src, self.got.at[k], self.ssem.at[k], self.rsem.at[k],
+            {"fsdp": (self.z + k) % self.n},
+        )
+
+    def start(self):
+        for k in range(1, self.n):
+            self.copy(k).start()
+
+    def finish(self):
+        total = self.src[...].astype(F32)
+        for k in range(1, self.n):
+            self.copy(k).wait_recv()
+            total += self.got[k].astype(F32)
+        self.out[...] = total
+
+    def end(self):
+        for k in range(1, self.n):
+            self.copy(k).wait_send()
+
+
+class CtxSum(Job):
+    uses_ctx = True
+
+    def __init__(self, full, n, hooks, keep=False):
+        self.n, self.hooks = n, hooks
+        full = full.reshape(n, 2, full.shape[0] // (2 * n), full.shape[1])
+        shape = (n, *full.shape[2:])
+        self.ins = [(full, HBM_SPEC)]
+        self.keep = keep
+        self.outs = [] if keep else [(jax.ShapeDtypeStruct(shape, BF16), VMEM_SPEC)]
+        self.scratch = [VMEM(shape, BF16), DMA((n,)), DMA((n,)), DMA((n,))]
+        if keep:
+            self.scratch.append(VMEM(shape, BF16))
+
+    def refs(self, ins, outs, scratch):
+        (self.full,) = ins
+        self.got, self.ssem, self.rsem, self.near = scratch[:4]
+        self.out = scratch[4] if self.keep else outs[0]
+
+    def order(self):
+        return (0, 3, 1, 2) if self.n == 4 else range(self.n)
+
+    def copy(self, k):
+        return remote(
+            self.full.at[k, 1 - self.c], self.got.at[k], self.ssem.at[k], self.rsem.at[k],
+            {"ctx": 1 - self.c},
+        )
+
+    def load(self, k):
+        return pltpu.make_async_copy(self.full.at[k, self.c], self.out.at[k], self.near.at[k])
+
+    def start(self):
+        for k in self.order():
+            self.copy(k).start()
+        for k in self.order():
+            self.load(k).start()
+
+    def add(self, k):
+        self.load(k).wait()
+        self.copy(k).wait_recv()
+        self.out[k] = (self.out[k].astype(F32) + self.got[k].astype(F32)).astype(BF16)
+
+    def steps(self):
+        per = -(-self.n // len(self.hooks))
+        return [
+            (self.hooks[i // per], functools.partial(self.add, k))
+            for i, k in enumerate(self.order())
+        ]
+
+    def end(self):
+        for k in range(self.n):
+            self.copy(k).wait_send()
+
+
+class FsdpSum(Job):
+    uses_ctx = uses_fsdp = True
+
+    def __init__(self, rows, n, hooks, source=None):
+        self.n, self.hooks, self.source = n, hooks, source
+        shape = rows.shape
+        self.ins = [] if source else [(rows, VMEM_SPEC)]
+        self.outs = [(jax.ShapeDtypeStruct((2, *shape[1:]), BF16), VMEM_SPEC)]
+        self.rows = shape[1]
+        self.ch = chunks_of(self.rows)
+        self.scratch = [
+            VMEM(shape, BF16), VMEM((2, *shape[1:]), BF16),
+            DMA((n, self.ch)), DMA((n, self.ch)), DMA((2, self.ch)), DMA((2, self.ch)),
+            DMA((self.ch,)), DMA((self.ch,)),
+        ]
+
+    def refs(self, ins, outs, scratch):
+        self.src = self.source.out if self.source else ins[0]
+        (self.out,) = outs
+        (self.got, self.via, self.ssem, self.rsem, self.via_send, self.via_recv, self.x_send,
+         self.x_recv) = scratch
+
+    def cut(self, ref, ch):
+        size = self.rows // self.ch
+        return ref.at[pl.ds(ch * size, size)]
+
+    def direct(self, d, ch):
+        return remote(
+            self.cut(self.src.at[d], ch), self.cut(self.got.at[self.z], ch),
+            self.ssem.at[d, ch], self.rsem.at[self.z, ch], {"fsdp": d},
+        )
+
+    def landed(self, frm, ch):
+        block = self.cut(self.got.at[frm], ch)
+        return remote(block, block, self.ssem.at[frm, ch], self.rsem.at[frm, ch], {"fsdp": frm})
+
+    def to_relay(self, d, ch):
+        return remote(
+            self.cut(self.src.at[d], ch), self.cut(self.via.at[0], ch),
+            self.via_send.at[0, ch], self.via_recv.at[0, ch], {"fsdp": 1 if d == 0 else 2},
+        )
+
+    def relayed(self, d, ch):
+        return remote(
+            self.cut(self.via.at[1], ch), self.cut(self.got.at[self.z], ch),
+            self.via_send.at[1, ch], self.rsem.at[self.z, ch], {"fsdp": d},
+        )
+
+    def directly(self, d):
+        if self.n == 4 and d in (0, 3):
+            return (self.z == 2) if d == 0 else (self.z == 1)
+        return self.z != d
+
+    def send(self, d):
+        if self.n == 4 and d in (0, 3):
+            @pl.when(self.z == 3 - d)
+            def _():
+                for ch in range(self.ch):
+                    self.to_relay(d, ch).start()
+
+        @pl.when(self.directly(d))
+        def _():
+            for ch in range(self.ch):
+                self.direct(d, ch).start()
+
+    def order(self):
+        return (0, 3, 1, 2) if self.n == 4 else range(self.n)
+
+    def start(self):
+        if not self.source:
+            for d in self.order():
+                self.send(d)
+
+    def relay(self):
+        for d, me in ((0, 1), (3, 2)):
+            @pl.when(self.z == me)
+            def _():
+                for ch in range(self.ch):
+                    self.to_relay(d, ch).wait_recv()
+                    mine = self.cut(self.src.at[d], ch)[...].astype(F32)
+                    theirs = self.cut(self.via.at[0], ch)[...].astype(F32)
+                    self.cut(self.via.at[1], ch)[...] = (mine + theirs).astype(BF16)
+                    self.relayed(d, ch).start()
+
+    def over_x(self, ch):
+        block = self.cut(self.out.at[self.c], ch)
+        return remote(block, block, self.x_send.at[ch], self.x_recv.at[ch], {"ctx": 1 - self.c})
+
+    def total(self):
+        n = self.n
+        for ch in range(self.ch):
+            mine = self.cut(self.src.at[self.z], ch)
+            if n == 4:
+                near = (self.z + 1) % 4
+                last = jnp.where(self.z == 0, 2, jnp.where(self.z == 3, 1, (self.z + 3) % 4))
+                first = jnp.where(self.z == 3, 2, near)
+                inner = (self.z == 1) | (self.z == 2)
+                self.landed(first, ch).wait_recv()
+                self.landed(last, ch).wait_recv()
+                part = (
+                    mine[...].astype(F32)
+                    + self.cut(self.got.at[first], ch)[...].astype(F32)
+                    + self.cut(self.got.at[last], ch)[...].astype(F32)
+                )
+                block = self.cut(self.out.at[self.c], ch)
+
+                @pl.when(inner)
+                def _():
+                    middle = (self.z + 2) % 4
+                    self.landed(middle, ch).wait_recv()
+                    block[...] = (part + self.cut(self.got.at[middle], ch)[...].astype(F32)).astype(BF16)
+
+                @pl.when(jnp.logical_not(inner))
+                def _():
+                    block[...] = part.astype(BF16)
+            else:
+                part = mine[...].astype(F32)
+                for k in range(1, n):
+                    frm = (self.z + k) % n
+                    self.landed(frm, ch).wait_recv()
+                    part += self.cut(self.got.at[frm], ch)[...].astype(F32)
+                self.cut(self.out.at[self.c], ch)[...] = part.astype(BF16)
+            self.over_x(ch).start()
+
+    def steps(self):
+        out = [(self.hooks[0], self.relay)] if self.n == 4 else []
+        return out + [(self.hooks[1], self.total)]
+
+    def end(self):
+        for ch in range(self.ch):
+            other = self.cut(self.out.at[1 - self.c], ch)
+            remote(other, other, self.x_send.at[ch], self.x_recv.at[ch], {"ctx": 1 - self.c}).wait_recv()
+            self.over_x(ch).wait_send()
+            for d in range(self.n):
+                if self.n == 4 and d in (0, 3):
+                    @pl.when(self.z == 3 - d)
+                    def _():
+                        self.to_relay(d, ch).wait_send()
+
+                    @pl.when(self.z == (1 if d == 0 else 2))
+                    def _():
+                        self.relayed(d, ch).wait_send()
+
+                @pl.when(self.directly(d))
+                def _():
+                    self.direct(d, ch).wait_send()
+
+
+class Background:
+    def __init__(self, jobs):
+        self.jobs = jobs
+        self.todo = [step for job in jobs for step in job.steps()]
+
+    def start(self):
+        for job in self.jobs:
+            job.start()
+
+    def at(self, hook):
+        for when, function in self.todo:
+            if when == hook:
+                function()
+
+    def loop(self, b, count=4, base=0):
+        for k in range(count):
+            if any(when == base + k for when, _ in self.todo):
+                @pl.when(b == k)
+                def _():
+                    self.at(base + k)
+
+    def end(self):
+        for job in self.jobs:
+            job.end()
 
 
 class Links:
@@ -93,10 +549,13 @@
     links.make(base + 1, s, out.at[2 + s, 0], out.at[s, 0], links.peer).start()
 
 
-def gather_end(links, base, out):
+def gather_forward(links, base, out):
     for s in range(2):
         links.make(base + 1, s, out.at[2 + s, 0], out.at[s, 0], links.peer).wait_recv()
         links.make(base + 2, s, out.at[s, 0], out.at[s, 1], links.sib).start()
+
+
+def gather_wait(links, base, out):
     for s in range(2):
         for kind, src, dst, other in (
             (base, out.at[2 + s, 0], out.at[2 + s, 1], links.sib),
@@ -104,6 +563,11 @@
         ):
             links.make(kind, s, src, dst, other).wait()
         links.make(base + 1, s, out.at[2 + s, 0], out.at[s, 0], links.peer).wait_send()
+
+
+def gather_end(links, base, out):
+    gather_forward(links, base, out)
+    gather_wait(links, base, out)
 
 
 class Scatter:
@@ -155,19 +619,30 @@
     ]
 
 
-def enter_kernel(tok, cot, gain, shift, first, grad, send, recv):
+def enter_kernel(jobs, first, send, recv):
     t, sib, peer = partners()
-    entry_barrier(sib, peer)
+    tokens, params, weights = jobs
+    entry_barrier(jobs)
     links = Links(send, recv, sib, peer)
+    params.start()
+    tokens.start()
+    weights.start()
+    params.finish()
+    tokens.end()
     for s in range(2):
-        unit, _ = statistics(tok[s].astype(F32))
-        first[2 + s, 0] = (unit * gain[...] + shift[...]).astype(BF16)
+        unit, _ = statistics(tokens.out[s].astype(F32))
+        first[2 + s, 0] = (unit * params.out[0:1, :] + params.out[1:2, :]).astype(BF16)
         gather_start(links, 0, first, s)
-    for s in range(2):
-        grad[2 + s, 0] = cot[s]
-        gather_start(links, 3, grad, s)
-    gather_end(links, 0, first)
-    gather_end(links, 3, grad)
+    for hook, step in weights.steps():
+        if hook == 0:
+            step()
+    gather_forward(links, 0, first)
+    for hook, step in weights.steps():
+        if hook == 1:
+            step()
+    gather_wait(links, 0, first)
+    params.end()
+    weights.end()
 
 
 def pair_tile(pair, h):
@@ -176,16 +651,22 @@
 
 
 def attention_kernel(
-    heads,
-    first, weight, q_bias, v_bias, key_extra, resid, out_bias, gain, shift,
+    jobs, heads, base,
+    first, weight, params, key_extra, resid,
     second, middle, q_out, k_out, v_out, mixed_out,
     part, sent, got, own, send, recv,
 ):
     t, sib, peer = partners()
-    entry_barrier(sib, peer)
+    background = Background(jobs)
+    entry_barrier(jobs)
+    background.start()
     links = Links(send, recv, sib, peer)
     scatter = Scatter(links, part, sent, got, own)
     width = heads * HD
+    weight = whole(weight)
+    out_bias, gain, shift = (params[base + k : base + k + 1, :] for k in (2, 3, 4))
+    q_bias = params[base + 6 : base + 7, :width]
+    v_bias = params[base + 6 : base + 7, width : 2 * width]
     half = first.shape[2]
     rows = 2 * half
     lane = lax.broadcasted_iota(jnp.int32, (rows, LANES), 1)
@@ -196,9 +677,9 @@
     def project(b, carry):
         x = rows_of(first, b)
         y = mm(x, weight[:, : 3 * width])
-        q = ((y[:, :width] + q_bias[...]).astype(BF16) * SCALE).astype(BF16)
+        q = ((y[:, :width] + q_bias).astype(BF16) * SCALE).astype(BF16)
         k = y[:, width : 2 * width].astype(BF16)
-        v = (y[:, 2 * width :] + v_bias[...]).astype(BF16)
+        v = (y[:, 2 * width :] + v_bias).astype(BF16)
         g, s = b // 2, b % 2
         mine = jnp.where(g == 1, t, peer)
         other = mine + 1 - 2 * (mine % 2)
@@ -241,63 +722,80 @@
         mixed_out[at, :] = mixed
         part[...] = mm_nt(mixed, weight[:, 3 * width :])
         scatter.block(b)
+        background.loop(b)
         return carry
 
     lax.fori_loop(0, 4, attend, 0)
     for s in range(2):
-        mid = resid[s].astype(F32) + (scatter.total(s) + out_bias[...])
+        mid = resid[s].astype(F32) + (scatter.total(s) + out_bias)
         middle[s] = mid
         unit, _ = statistics(mid)
-        second[2 + s, 0] = (unit * gain[...] + shift[...]).astype(BF16)
+        second[2 + s, 0] = (unit * gain + shift).astype(BF16)
         gather_start(links, 3, second, s)
-    gather_end(links, 3, second)
+        background.at(4 + s)
+    gather_forward(links, 3, second)
+    background.at(6)
+    gather_wait(links, 3, second)
     scatter.end()
+    background.end()
 
 
 def mlp_kernel(
-    last,
-    second, weight, bias, middle, out_bias, gain, shift,
+    jobs, last, base,
+    second, weight, params, middle,
     active_out, slope_out, resid, nxt,
     part, sent, got, own, send, recv,
 ):
     t, sib, peer = partners()
-    entry_barrier(sib, peer)
+    background = Background(jobs)
+    entry_barrier(jobs)
+    background.start()
     links = Links(send, recv, sib, peer)
     scatter = Scatter(links, part, sent, got, own)
     half = second.shape[2]
     rows = 2 * half
-    hidden = bias.shape[1]
+    weight = whole(weight)
+    hidden = weight.shape[1] // 2
+    out_bias = params[base + 5 : base + 6, :]
+    following = 0 if last else base + 8
+    gain, shift = (params[following + k : following + k + 1, :] for k in (0, 1))
     step = 256
 
     def block(b, carry):
         at = pl.ds(pl.multiple_of(b * rows, rows), rows)
         x = rows_of(second, b)
         for n in range(0, hidden, step):
-            before = mm(x, weight[:, n : n + step]) + bias[:, n : n + step]
+            before = mm(x, weight[:, n : n + step]) + params[base + 7 : base + 8, n : n + step]
             cdf = 0.5 * (1.0 + lax.erf(before * INV_SQRT2))
             active_out[at, n : n + step] = (before * cdf).astype(BF16)
             slope = cdf + before * (jnp.exp(before * before * -0.5) * INV_SQRT_2PI)
             slope_out[at, n : n + step] = slope.astype(BF16)
         part[...] = mm_nt(active_out[at, :], weight[:, hidden:])
         scatter.block(b)
+        background.loop(b)
         return carry
 
     lax.fori_loop(0, 4, block, 0)
     for s in range(2):
-        res = middle[s] + (scatter.total(s) + out_bias[...])
+        res = middle[s] + (scatter.total(s) + out_bias)
         if last:
             nxt[s] = res.astype(BF16)
         else:
             resid[s] = res
             unit, _ = statistics(res)
-            nxt[2 + s, 0] = (unit * gain[...] + shift[...]).astype(BF16)
+            nxt[2 + s, 0] = (unit * gain + shift).astype(BF16)
             gather_start(links, 3, nxt, s)
+        background.at(4 + s)
     if not last:
-        gather_end(links, 3, nxt)
+        gather_forward(links, 3, nxt)
+    background.at(6)
+    if not last:
+        gather_wait(links, 3, nxt)
     scatter.end()
-
-
-def token_product(left, right, out, at, rows, offset):
+    background.end()
+
+
+def token_product(left, right, out, offset):
     depth = left.shape[-1]
     total = left.shape[0] * left.shape[1] * left.shape[2]
     step = 256
@@ -312,14 +810,19 @@
 
 
 def mlp_back_kernel(
-    grad, weight, active, slope, second, middle, carry_in, gain,
+    jobs, base,
+    grad, weight, active, slope, second, middle, carry_in, params,
     weight_grad, carry_out, rows_out, vectors,
     part, sent, got, own, send, recv, d_before,
 ):
     t, sib, peer = partners()
-    entry_barrier(sib, peer)
+    background = Background(jobs)
+    entry_barrier(jobs)
+    background.start()
     links = Links(send, recv, sib, peer)
     scatter = Scatter(links, part, sent, got, own)
+    weight = whole(weight)
+    gain = params[base + 3 : base + 4, :]
     half = grad.shape[2]
     rows = 2 * half
     hidden = active.shape[1]
@@ -336,13 +839,15 @@
             vectors[4:5, n : n + step] += jnp.sum(d_bef.astype(F32), axis=0, keepdims=True)
         part[...] = mm_nt(d_before[at, :], weight[:, :hidden])
         scatter.block(b)
+        background.loop(b)
         return carry
 
     lax.fori_loop(0, 4, block, 0)
-    token_product(grad, active, weight_grad, None, rows, hidden)
+    token_product(grad, active, weight_grad, hidden)
+    background.at(4)
 
     def finish(s):
-        back, d_gain, d_shift = norm_back(middle[s], scatter.total(s), gain[...])
+        back, d_gain, d_shift = norm_back(middle[s], scatter.total(s), gain)
         carry = carry_in[s].astype(F32)
         mid = carry + back
         carry_out[s] = mid
@@ -355,23 +860,31 @@
         vectors[3:4, :] += jnp.sum(carry.astype(BF16).astype(F32), axis=0, keepdims=True)
 
     finish(0)
-    token_product(second, d_before, weight_grad, None, rows, 0)
+    background.at(5)
+    token_product(second, d_before, weight_grad, 0)
     finish(1)
-    gather_end(links, 3, rows_out)
+    gather_forward(links, 3, rows_out)
+    background.at(6)
+    gather_wait(links, 3, rows_out)
     scatter.end()
+    background.end()
 
 
 def attention_back_kernel(
-    heads, last,
-    grad, weight, mixed, q_in, k_in, v_in, first, carry_in, resid, gain,
+    jobs, heads, last, base,
+    grad, weight, mixed, q_in, k_in, v_in, first, carry_in, resid, params,
     weight_grad, carry_out, rows_out, vectors,
     part, sent, got, own, send, recv, d_out, d_joint, d_key, d_value,
 ):
     t, sib, peer = partners()
-    entry_barrier(sib, peer)
+    background = Background(jobs)
+    entry_barrier(jobs)
+    background.start()
     links = Links(send, recv, sib, peer)
     scatter = Scatter(links, part, sent, got, own)
     width = heads * HD
+    weight = whole(weight)
+    gain = params[base : base + 1, :]
     half = grad.shape[2]
     rows = 2 * half
     lane = lax.broadcasted_iota(jnp.int32, (rows, LANES), 1)
@@ -415,6 +928,7 @@
             d_key[h] += mm(d_raw, q)
             d_queries.append(mm_tn(d_raw, k_in[h]) * SCALE)
         d_joint[at, :width] = pairs(d_queries).astype(BF16)
+        background.loop(b)
         return carry
 
     lax.fori_loop(0, 4, attend, 0)
@@ -429,13 +943,15 @@
         vectors[2:3, width : 2 * width] += sums[:, 2 * width :]
         part[...] = mm_nt(d_rows, weight[:, : 3 * width])
         scatter.block(b)
+        background.loop(b, 4, 4)
         return carry
 
     lax.fori_loop(0, 4, project, 0)
-    token_product(grad, mixed, weight_grad, None, rows, 3 * width)
+    token_product(grad, mixed, weight_grad, 3 * width)
+    background.at(8)
 
     def finish(s):
-        back, d_gain, d_shift = norm_back(resid[s].astype(F32), scatter.total(s), gain[...])
+        back, d_gain, d_shift = norm_back(resid[s].astype(F32), scatter.total(s), gain)
         carry = carry_in[s] + back
         if last:
             rows_out[s] = carry.astype(BF16)
@@ -447,29 +963,151 @@
         vectors[1:2, :] += d_shift
 
     finish(0)
-    token_product(first, d_joint, weight_grad, None, rows, 0)
+    background.at(9)
+    token_product(first, d_joint, weight_grad, 0)
     finish(1)
     if not last:
-        gather_end(links, 3, rows_out)
+        gather_forward(links, 3, rows_out)
+    background.at(10)
+    if not last:
+        gather_wait(links, 3, rows_out)
     scatter.end()
-
-
-def call(kernel, name, outs, scratch, collective_id, flops, args):
-    size = sum(a.size * a.dtype.itemsize for a in args) + sum(
-        math.prod(o.shape) * o.dtype.itemsize for o in outs
+    background.end()
+
+
+class VectorSum(Job):
+    uses_ctx = uses_fsdp = True
+
+    def __init__(self, vectors, n, hooks):
+        self.n, self.hooks = n, hooks
+        dim = vectors[0].shape[1]
+        self.ins = [(v, VMEM_SPEC) for v in vectors]
+        self.outs = [(jax.ShapeDtypeStruct((16, dim), F32), VMEM_SPEC)]
+        self.scratch = [
+            VMEM((4, 16, dim), F32), VMEM((3 + n, 16, dim), F32), DMA((3 + n,)), DMA((3 + n,))
+        ]
+
+    def refs(self, ins, outs, scratch):
+        self.vectors = ins
+        (self.out,) = outs
+        self.held, self.got, self.ssem, self.rsem = scratch
+        t, self.sib, self.peer = partners()
+
+    def copy(self, k):
+        if k < 2:
+            to = {"tp": self.sib if k == 0 else self.peer}
+        elif k == 2:
+            to = {"ctx": 1 - self.c}
+        else:
+            to = {"fsdp": (self.z + k - 2) % self.n}
+        return remote(
+            self.held.at[min(k, 3)], self.got.at[k], self.ssem.at[k], self.rsem.at[k], to
+        )
+
+    def start(self):
+        for l in range(LAYERS):
+            attn, mlp = self.vectors[2 * l], self.vectors[2 * l + 1]
+            for row, (ref, index) in enumerate(
+                ((attn, 0), (attn, 1), (mlp, 2), (mlp, 0), (mlp, 1), (mlp, 3), (attn, 2), (mlp, 4))
+            ):
+                self.held[0, 8 * l + row : 8 * l + row + 1, :] = ref[index : index + 1, :]
+        self.copy(0).start()
+
+    def fold(self, k):
+        self.copy(k).wait_recv()
+        came = self.got[k]
+        if k < 2:
+            row = lax.broadcasted_iota(jnp.int32, came.shape, 0)
+            came = jnp.where(row % 8 < 6, came, 0.0)
+        self.held[k + 1] = self.held[k] + came
+        if k < 2:
+            self.copy(k + 1).start()
+        else:
+            for j in range(1, self.n):
+                self.copy(2 + j).start()
+
+    def finish(self):
+        total = self.held[3]
+        for j in range(1, self.n):
+            self.copy(2 + j).wait_recv()
+            total += self.got[2 + j]
+        self.out[...] = total
+
+    def steps(self):
+        return [(self.hooks[k], functools.partial(self.fold, k)) for k in range(3)] + [
+            (self.hooks[3], self.finish)
+        ]
+
+    def end(self):
+        for k in range(2 + self.n):
+            self.copy(k).wait_send()
+
+
+def leave_kernel(jobs):
+    attn_ctx, attn_fsdp, mlp_fsdp, vectors, rows = jobs
+    entry_barrier(jobs)
+    mlp_fsdp.start()
+    vectors.start()
+    attn_ctx.start()
+    rows.start()
+    vectors.fold(0)
+    for i, k in enumerate(attn_ctx.order()):
+        attn_ctx.add(k)
+        attn_fsdp.send(k)
+        if i in (1, 2):
+            vectors.fold(i)
+        if i == 2 and mlp_fsdp.n == 4:
+            mlp_fsdp.relay()
+    if attn_fsdp.n == 4:
+        attn_fsdp.relay()
+    vectors.finish()
+    mlp_fsdp.total()
+    attn_fsdp.total()
+    for job in jobs:
+        job.end()
+
+
+def whole(ref):
+    return ref.reshape(ref.shape[0] * ref.shape[1] * ref.shape[2], ref.shape[3])
+
+
+def call(kernel, name, outs, scratch, collective_id, flops, args, jobs=()):
+    ins = [(a, VMEM_SPEC) for a in args] + [pair for job in jobs for pair in job.ins]
+    results = [(o, VMEM_SPEC) for o in outs] + [pair for job in jobs for pair in job.outs]
+    scratch = list(scratch)
+    n_scratch = len(scratch)
+    for job in jobs:
+        scratch += job.scratch
+
+    def body(*refs):
+        refs = list(refs)
+        in_refs = refs[: len(ins)]
+        out_refs = refs[len(ins) : len(ins) + len(results)]
+        scratch_refs = refs[len(ins) + len(results) :]
+        a, b, c = len(args), len(outs), n_scratch
+        for job in jobs:
+            ends = a + len(job.ins), b + len(job.outs), c + len(job.scratch)
+            job.bind(in_refs[a : ends[0]], out_refs[b : ends[1]], scratch_refs[c : ends[2]])
+            a, b, c = ends
+        kernel(
+            jobs, *in_refs[: len(args)], *out_refs[: len(outs)], *scratch_refs[:n_scratch]
+        )
+
+    size = sum(a.size * a.dtype.itemsize for a, _ in ins) + sum(
+        math.prod(o.shape) * o.dtype.itemsize for o, _ in results
     )
     return pl.pallas_call(
-        kernel,
+        body,
         name=name,
-        out_shape=tuple(outs),
-        in_specs=[pl.BlockSpec(memory_space=VMEM)] * len(args),
-        out_specs=tuple(pl.BlockSpec(memory_space=VMEM) for _ in outs),
+        out_shape=tuple(o for o, _ in results),
+        in_specs=[spec for _, spec in ins],
+        out_specs=tuple(spec for _, spec in results),
         scratch_shapes=scratch,
         compiler_params=pltpu.CompilerParams(
             collective_id=collective_id, has_side_effects=True, vmem_limit_bytes=VMEM_LIMIT
         ),
         cost_estimate=pl.CostEstimate(flops=flops, bytes_accessed=size, transcendentals=0),
-    )(*args)
+    )(*[a for a, _ in ins])
 
 
 def local(
@@ -483,54 +1121,43 @@
     clips, half, dim = tokens.shape
     assert clips == ctx_size == 2 and tp_size == 4 and joint_weight.shape[0] == LAYERS
     c = lax.axis_index("ctx")
-    t = lax.axis_index("tp")
     shard = joint_weight.shape[1]
     width = joint_weight.shape[3]
     heads = width // HD
     hidden = expand_weight.shape[2]
-    swap = [(0, 1), (1, 0)]
-
-    piece = shard // ctx_size
-
-    def gathered(parts):
-        packed = jnp.concatenate(parts, axis=1)
-        mine = lax.dynamic_slice_in_dim(packed, c * piece, piece, 0)
-        return lax.all_gather(mine, ("fsdp", "ctx"), axis=0, tiled=True)
-
-    attn_weights, mlp_weights = [], []
-    for l in range(LAYERS):
+    z = lax.axis_index("fsdp")
+
+    def packed(parts):
+        return jnp.concatenate(parts, axis=1).reshape(ctx_size, shard // ctx_size, -1)
+
+    def attn_parts(l):
         joint = joint_weight[l]
-        attn_weights.append(
-            gathered([joint[:, 0], joint[:, 1], joint[:, 2], out_weight[l].T])
-        )
-        mlp_weights.append(gathered([expand_weight[l], reduce_weight[l].T]))
-
-    wide = [first_gain, first_shift, out_bias, second_gain, second_shift, reduce_bias]
-    narrow = [query_bias, value_bias, expand_bias]
-    small = jnp.concatenate([a.reshape(-1) for a in wide + narrow])
-    small = lax.all_gather(small, "fsdp", axis=0).astype(F32)
-    params = []
-    at = 0
-    for a in wide:
-        n = a.size
-        got = small[:, at : at + n].reshape(fsdp_size, LAYERS, shard)
-        params.append(got.transpose(1, 0, 2).reshape(LAYERS, 1, dim))
-        at += n
-    for a in narrow:
-        n = a.size
-        got = small[:, at : at + n].reshape(fsdp_size, *a.shape)
-        params.append(got.transpose(1, 2, 0, 3).reshape(LAYERS, 1, a.shape[1] * HD))
-        at += n
-    g1, s1, ob, g2, s2, rb, qb, vb, eb = params
+        return packed([joint[:, 0], joint[:, 1], joint[:, 2], out_weight[l].T])
+
+    def mlp_parts(l):
+        return packed([expand_weight[l], reduce_weight[l].T])
+
+    slot = lax.broadcasted_iota(jnp.int32, (1, fsdp_size, 1), 1) == z
+
+    def placed(block):
+        spread = jnp.where(slot, block.reshape(-1, 1, block.shape[-1]), jnp.zeros((), BF16))
+        return spread.reshape(LAYERS, -1)
+
+    rows = [
+        placed(a)
+        for a in (first_gain, first_shift, out_bias, second_gain, second_shift, reduce_bias)
+    ]
+    both = jnp.concatenate([placed(query_bias), placed(value_bias)], axis=1)
+    rows.append(jnp.pad(both, ((0, 0), (0, dim - both.shape[1]))))
+    rows.append(placed(expand_bias))
+    params = jnp.stack(rows, axis=1).reshape(LAYERS * 8, dim)
 
     def regroup(both):
         mine = lax.dynamic_index_in_dim(both, c, 0, keepdims=False)
         theirs = lax.dynamic_index_in_dim(both, 1 - c, 0, keepdims=False)
-        got = lax.ppermute(theirs, "ctx", swap)
+        got = lax.ppermute(theirs, "ctx", [(0, 1), (1, 0)])
         return jnp.where(c == 0, jnp.stack([mine, got]), jnp.stack([got, mine]))
 
-    tok = regroup(tokens)
-    cot = regroup(cotangent)
     valid = lax.dynamic_index_in_dim(key_valid, c, 0, keepdims=False)
     bias = jnp.where(valid == 1, 0.0, MASKED).astype(F32)
     bias = bias.reshape(ctx_size, tp_size, half, 1).transpose(1, 0, 2, 3)
@@ -545,57 +1172,69 @@
     own_low = jax.ShapeDtypeStruct((2, half, dim), BF16)
     count = 8 * half
     scratch = scatter_scratch(half, dim)
-
-    first, grad = call(
-        enter_kernel, "enter", [every, every],
-        [pltpu.SemaphoreType.DMA((6, 2)), pltpu.SemaphoreType.DMA((6, 2))],
-        0, 10**7, [tok, cot, g1[0], s1[0]],
+    n = fsdp_size
+
+    jobs = [Exchange(tokens), ParamSum(params, n), WeightGather(attn_parts(0), n, (0, 1, 1))]
+    first, tok, params, attn_weight = call(
+        enter_kernel, "enter", [every], [DMA((3, 2)), DMA((3, 2))], 0, 10**7, [], jobs
     )
     resid = tok
     saved = []
     for l in range(LAYERS):
+        last = l == LAYERS - 1
         heads_shape = jax.ShapeDtypeStruct((heads, count, LANES), BF16)
-        second, middle, q, k, v, mixed = call(
-            functools.partial(attention_kernel, heads), "attention",
+        jobs = [WeightGather(mlp_parts(l), n, (1, 3, 6))]
+        if last:
+            jobs.append(RowGather(cot, 1))
+        second, middle, q, k, v, mixed, mlp_weight, *grad = call(
+            lambda jobs, *refs, base=8 * l: attention_kernel(jobs, heads, base, *refs),
+            f"attention_{l}",
             [every, own, heads_shape, heads_shape, heads_shape, jax.ShapeDtypeStruct((count, width), BF16)],
             scratch, 1 + 6 * l, 2 * count * dim * 4 * width + 16 * heads * count * count * HD,
-            [first, attn_weights[l], qb[l], vb[l], key_extra, resid, ob[l], g2[l], s2[l]],
-        )
-        last = l == LAYERS - 1
-        nxt_l = l if last else l + 1
+            [first, attn_weight, params, key_extra, resid], jobs,
+        )
         rows_hidden = jax.ShapeDtypeStruct((count, hidden), BF16)
-        active, slope, out, nxt = call(
-            functools.partial(mlp_kernel, last), "mlp_last" if last else "mlp",
+        jobs = [] if last else [WeightGather(attn_parts(l + 1), n, (2, 4, 5)), Exchange(cotangent)]
+        active, slope, out, nxt, *more = call(
+            lambda jobs, *refs, base=8 * l, last=last: mlp_kernel(jobs, last, base, *refs),
+            f"mlp_{l}",
             [rows_hidden, rows_hidden,
              jax.ShapeDtypeStruct((8, LANES), F32) if last else own, own_low if last else every],
             scratch, 2 + 6 * l, 4 * count * dim * hidden,
-            [second, mlp_weights[l], eb[l], middle, rb[l], g1[nxt_l], s1[nxt_l]],
-        )
-        saved.append((resid, first, q, k, v, mixed, middle, second, active, slope))
+            [second, mlp_weight, params, middle], jobs,
+        )
+        saved.append((resid, first, q, k, v, mixed, middle, second, active, slope, attn_weight, mlp_weight))
         resid, first = out, nxt
-    output = nxt
+        if not last:
+            attn_weight, cot = more
+    output = regroup(nxt)
 
     vec = jax.ShapeDtypeStruct((8, dim), F32)
     carry = cot
+    (grad,) = grad
     attn_grads, mlp_grads, attn_vec, mlp_vec = ([None] * LAYERS for _ in range(4))
-
-    def reduced(full):
-        part = lax.psum_scatter(full, ("fsdp", "ctx"), scatter_dimension=0, tiled=True)
-        return lax.all_gather(part, "ctx", axis=0, tiled=True).astype(F32)
-
+    attn_full = mlp_part = attn_part = None
     for l in reversed(range(LAYERS)):
-        resid, first, q, k, v, mixed, middle, second, active, slope = saved[l]
-        w_grad, carry, grad, mlp_vec[l] = call(
-            mlp_back_kernel, "mlp_back",
+        (resid, first, q, k, v, mixed, middle, second, active, slope, attn_weight, mlp_weight) = saved[l]
+        last = l == 0
+        jobs = []
+        if attn_full is not None:
+            jobs = [FsdpSum(mlp_part, n, (3, 6)), CtxSum(attn_full, n, (2, 4, 5, 6))]
+        mlp_full, carry, grad, mlp_vec[l], *more = call(
+            lambda jobs, *refs, base=8 * l: mlp_back_kernel(jobs, base, *refs),
+            f"mlp_back_{l}",
             [jax.ShapeDtypeStruct((dim, 2 * hidden), BF16), own, every, vec],
             scratch + [VMEM((count, hidden), BF16)], 3 + 6 * l, 8 * count * dim * hidden,
-            [grad, mlp_weights[l], active, slope, second, middle, carry, g2[l]],
-        )
-        mlp_grads[l] = reduced(w_grad)
-        last = l == 0
-        w_grad, carry, grad, attn_vec[l] = call(
-            functools.partial(attention_back_kernel, heads, last),
-            "attention_back_last" if last else "attention_back",
+            [grad, mlp_weight, active, slope, second, middle, carry, params], jobs,
+        )
+        if more:
+            mlp_grads[l + 1], attn_part = more
+        jobs = [CtxSum(mlp_full, n, (2, 5, 8, 10))]
+        if attn_part is not None:
+            jobs.append(FsdpSum(attn_part, n, (2, 5)))
+        attn_full, carry, grad, attn_vec[l], mlp_part, *more = call(
+            lambda jobs, *refs, base=8 * l, last=last: attention_back_kernel(jobs, heads, last, base, *refs),
+            f"attention_back_{l}",
             [jax.ShapeDtypeStruct((dim, 4 * width), BF16),
              jax.ShapeDtypeStruct((8, LANES), F32) if last else own, own_low if last else every, vec],
             scratch
@@ -606,56 +1245,49 @@
                 VMEM((heads, count, LANES), F32),
             ],
             4 + 6 * l, 4 * count * dim * 4 * width + 40 * heads * count * count * HD,
-            [grad, attn_weights[l], mixed, q, k, v, first, carry, resid, g1[l]],
-        )
-        attn_grads[l] = reduced(w_grad)
-    row_grad = grad
-
-    def ungroup(both):
-        mine = lax.dynamic_index_in_dim(both, c, 0, keepdims=False)
-        theirs = lax.dynamic_index_in_dim(both, 1 - c, 0, keepdims=False)
-        got = lax.ppermute(theirs, "ctx", swap)
-        return jnp.where(c == 0, jnp.stack([mine, got]), jnp.stack([got, mine]))
-
-    pieces = []
-    for l in range(LAYERS):
-        pieces += [attn_vec[l][0], attn_vec[l][1], mlp_vec[l][2], mlp_vec[l][0], mlp_vec[l][1], mlp_vec[l][3]]
-    flat = jnp.concatenate(pieces)
-    slots = jnp.concatenate(
-        [jnp.concatenate([attn_vec[l][2][: 2 * width], mlp_vec[l][4][:hidden]]) for l in range(LAYERS)]
+            [grad, attn_weight, mixed, q, k, v, first, carry, resid, params], jobs,
+        )
+        if more:
+            (attn_grads[l + 1],) = more
+
+    ctx_job = CtxSum(attn_full, n, (0, 1, 2, 3), keep=True)
+    attn_shape = jax.ShapeDtypeStruct((n, shard // 2, attn_full.shape[1]), BF16)
+    jobs = [
+        ctx_job,
+        FsdpSum(attn_shape, n, (0, 1), source=ctx_job),
+        FsdpSum(mlp_part, n, (0, 1)),
+        VectorSum([attn_vec[0], mlp_vec[0], attn_vec[1], mlp_vec[1]], n, (0, 1, 2, 3)),
+        Exchange(grad),
+    ]
+    attn_grads[0], mlp_grads[0], vectors, row_grad = call(
+        leave_kernel, "leave", [], [], 5, 10**7, [], jobs
     )
-    placed = jnp.where(
-        lax.broadcasted_iota(jnp.int32, (tp_size, 1), 0) == t, slots[None, :], 0.0
-    )
-    summed = lax.psum(jnp.concatenate([flat, placed.reshape(-1)]), ("fsdp", "ctx", "tp"))
-    f = lax.axis_index("fsdp")
-    rows = summed[: flat.size].reshape(LAYERS, 6, fsdp_size, shard)
-    rows = lax.dynamic_index_in_dim(rows, f, 2, keepdims=False)
-    mine = lax.dynamic_index_in_dim(summed[flat.size :].reshape(tp_size, -1), t, 0, keepdims=False)
-    mine = mine.reshape(LAYERS, 2 * width + hidden)
-    cut = HD // fsdp_size
-
-    def spread(block, n):
-        block = block.reshape(LAYERS, n // HD, fsdp_size, cut)
-        return lax.dynamic_index_in_dim(block, f, 2, keepdims=False)
-
-    joint = [g[:, : 3 * width].reshape(shard, 3, width) for g in attn_grads]
+    attn_grads = [g.reshape(shard, -1).astype(F32) for g in attn_grads]
+    mlp_grads = [g.reshape(shard, -1).astype(F32) for g in mlp_grads]
+
+    vectors = vectors.reshape(LAYERS, 8, dim)
+    wide = lax.dynamic_slice_in_dim(vectors[:, :6], z * shard, shard, 2)
+
+    def spread(block):
+        block = block.reshape(LAYERS, -1, fsdp_size, HD // fsdp_size)
+        return lax.dynamic_index_in_dim(block, z, 2, keepdims=False)
+
     return (
-        ungroup(output),
-        ungroup(row_grad),
-        rows[:, 0],
-        rows[:, 1],
-        jnp.stack(joint),
-        spread(mine[:, :width], width),
-        spread(mine[:, width : 2 * width], width),
+        output,
+        row_grad,
+        wide[:, 0],
+        wide[:, 1],
+        jnp.stack([g[:, : 3 * width].reshape(shard, 3, width) for g in attn_grads]),
+        spread(vectors[:, 6, :width]),
+        spread(vectors[:, 6, width : 2 * width]),
         jnp.stack([g[:, 3 * width :].T for g in attn_grads]),
-        rows[:, 2],
-        rows[:, 3],
-        rows[:, 4],
+        wide[:, 2],
+        wide[:, 3],
+        wide[:, 4],
         jnp.stack([g[:, :hidden] for g in mlp_grads]),
-        spread(mine[:, 2 * width :], hidden),
+        spread(vectors[:, 7, :hidden]),
         jnp.stack([g[:, hidden:].T for g in mlp_grads]),
-        rows[:, 5],
+        wide[:, 5],
     )
 
 

time: 966 us -> 620 us (0.64)
  waiting for transfers between devices: 529 us -> 0.01 us
  Pallas kernels: 330 us -> 564 us
  blocking collectives: 28.5 us -> 0 us
  between operations: 15.2 us -> 1.26 us
    reduce_scatter x4 -> x0, waiting for transfers between devices: 303 us -> none  [reduced(): lax.psum_scatter(full, ('fsdp', 'ctx'), scatter_dimension=0, tiled=True)]
    pallas_call x9 -> x10, Pallas kernels: 330 us -> 564 us  [call(): pl.pallas_call(body, name=name, out_shape=tuple((o for o, _ in results)),...]
    psum x1 -> x0, waiting for transfers between devices: 114 us -> none  [local(): lax.psum(jnp.concatenate([flat, placed.reshape(-1)]), ('fsdp', 'ctx', 'tp'))]
    all_gather x6 -> x0, waiting for transfers between devices: 110 us -> none  [the longest x4 71.8 us: gathered(): return lax.all_gather(mine, ('fsdp', 'ctx'), axis=0, tiled=True)]
    all_gather x3 -> x0, blocking collectives: 28.5 us -> none  [the longest x2 14.6 us: reduced(): return lax.all_gather(part, 'ctx', axis=0, tiled=True).astype(F32)]
  transfers between devices with their start and end apart: 15 -> 1, of which waited for: 10 -> 0; matrix products, arithmetic and copies ran while one was open for 4% -> 4% of each run, Pallas kernels for 15% -> 52%
where the time goes in v2:
time: 620 us; the launch traced here: 616 us
  Pallas kernels  564 us (91%)
  local copies, waits for them, and re-layouts  30.6 us (5%)
  other arithmetic  20.3 us (3%)
    pallas_call x10, Pallas kernels, call(): pl.pallas_call(body, name=name, out_shape=tuple((o for o, _ in results)),...  564 us
  transfers between devices with their start and end apart: 1, of which 0 were waited for; matrix products, arithmetic and copies ran while one was open for 4% of the time, Pallas kernels for 52%

profile of v2, /device:TPU:0, one launch (start us, length us, event | category | flops | bytes accessed | tf_op | source)
XLA Modules:
  0.0 616.4 jit_solution(2724315635650038715)
XLA Ops:
  8.9 1.0 slice_bitcast_fusion.6
  10.6 1.2 slice_bitcast_fusion.4
  12.1 1.3 fusion.9
  15.1 1.1 pad_maximum_fusion.3.refs_5_
  16.1 1.1 pad_maximum_fusion.4.refs_5_
  18.1 40.4 %enter.1 = (bf16[4,2,128,1024]{3,2,1,0:T(8,128)(2,1)}, bf16[2,128,1024]{2,1,0:T(8,128)(2,1)}, f32[16,1024]{1,0:T(8,128)}, bf16[4,2,128,1024]{3,2,1,0:T(8,128)(2,1)}) custom-call(bf16[2,128,1024]{2,1,0:T(8,128)(2,1)} %refs_0_.1, bf16[16,1024]{1,0:T(8,128)(2,1)} %bitcast.141, bf16[2,128,1024]{2,1,0:T(8,128)(2,1)} %pad_maximum_fusion.5.refs_2_), custom_call_target="tpu_custom_call" | custom-call | flops 10000000 | bytes 5865472 | tf_op jit(solution)/shard_map/enter/pallas_call | solution.py:1099
  58.5 0.9 pad_maximum_fusion.6.refs_4_
  59.3 1.0 select_convert_fusion.refs_3_
  60.4 63.2 %attention_0.1 = (bf16[4,2,128,1024]{3,2,1,0:T(8,128)(2,1)}, f32[2,128,1024]{2,1,0:T(8,128)}, bf16[4,1024,128]{2,1,0:T(8,128)(2,1)}, bf16[4,1024,128]{2,1,0:T(8,...) custom-call(bf16[4,2,128,1024]{3,2,1,0:T(8,128)(2,1)} %get-tuple-element.67.r, ...), custom_call_target="tpu_custom_call" | custom-call | flops 6442450944 | bytes 17104896 | tf_op jit(solution)/shard_map/attention_0/pallas_call | solution.py:1099
  123.6 43.6 %mlp_0.1 = (bf16[1024,1024]{1,0:T(8,128)(2,1)}, bf16[1024,1024]{1,0:T(8,128)(2,1)}, f32[2,128,1024]{2,1,0:T(8,128)}, bf16[4,2,128,1024]{3,2,1,0:T(8,128)(2,1)}, ...) custom-call(bf16[4,2,128,1024]{3,2,1,0:T(8,128)(2,1)} %get-tuple-element.71.refs_0_.refs_4_, ...), custom_call_target="tpu_custom_call" | custom-call | flops 4294967296 | bytes 18415616 | tf_op jit(solution)/shard_map/mlp_0/pallas_call | solution.py:1099
  167.3 72.0 %attention_1.1 = (bf16[4,2,128,1024]{3,2,1,0:T(8,128)(2,1)}, f32[2,128,1024]{2,1,0:T(8,128)}, bf16[4,1024,128]{2,1,0:T(8,128)(2,1)}, bf16[4,1024,128]{2,1,0:T(8,...) custom-call(bf16[4,2,128,1024]{3,2,1,0:T(8,128)(2,1)} %get-tuple-ele, ...), custom_call_target="tpu_custom_call" | custom-call | flops 6442450944 | bytes 20250624 | tf_op jit(solution)/shard_map/attention_1/pallas_call | solution.py:1099
  239.3 23.4 %mlp_1.1 = (bf16[1024,1024]{1,0:T(8,128)(2,1)}, bf16[1024,1024]{1,0:T(8,128)(2,1)}, f32[8,128]{1,0:T(8,128)}, bf16[2,128,1024]{2,1,0:T(8,128)(2,1)}) custom-call(bf16[4,2,128,1024]{3,2,1,0:T(8,128)(2,1)} %get-tuple-element.78.refs_0_.refs_4_, bf16[4,2,128,2048]{3,2,1,0:T(8,128)(2,1)} %get-tuple-element.79.refs_1_, ...), custom_call_target="tpu_custom_call" | custom-call | flops 4294967296 | bytes 12128256 | tf_op jit(solution)/shard_map/mlp_1/pallas_call | solution.py:1099
  262.7 1.9 constant_dynamic-slice_fusion.9
  264.5 37.6 %mlp_back_1.1 = (bf16[1024,2048]{1,0:T(8,128)(2,1)}, f32[2,128,1024]{2,1,0:T(8,128)}, bf16[4,2,128,1024]{3,2,1,0:T(8,128)(2,1)}, f32[8,1024]{1,0:T(8,128)}) custom-call(bf16[4,2,128,1024]{3,2,1,0:T(8,128)(2,1)} %get-tuple-element.82.refs_0_, bf16[4,2,128,2048]{3,2,1,0:T(8,128)(2,1)} %get-tuple-element.79.refs_1_, ...), custom_call_target="tpu_custom_call" | custom-call | flops 8589934592 | bytes 21594112 | tf_op jit(solution)/shard_map/mlp_back_1/pallas_call | solution.py:1099
  302.1 59.8 %attention_back_1.1 = (bf16[1024,1024]{1,0:T(8,128)(2,1)}, f32[2,128,1024]{2,1,0:T(8,128)}, bf16[4,2,128,1024]{3,2,1,0:T(8,128)(2,1)}, f32[8,1024]{1,0:T(8,128)}, bf16[4,128,2048]{2,1,0:T(8,128)(2,1)}) custom-call(bf16[4,2,128,1024]{3,2,1,0:T(8,128)(2,1)} %get-tuple-element.85.refs_0_, bf16[4,2,128,1024]{3,2,1,0:T(8,128)(2,1)} %get-tuple-element.75.refs_1_, ...), custom_call_target="tpu_custom_call" | custom-call | flops 15032385536 | bytes 23691264 | tf_op jit(solution)/shard_map/attention_back_1/pallas_call | solution.py:1099
  361.9 54.8 %mlp_back_0.1 = (bf16[1024,2048]{1,0:T(8,128)(2,1)}, f32[2,128,1024]{2,1,0:T(8,128)}, bf16[4,2,128,1024]{3,2,1,0:T(8,128)(2,1)}, f32[8,1024]{1,0:T(8,128)}, bf16...) custom-call(bf16[4,2,128,1024]{3,2,1,0:T(8,128)(2,1)} %get-tuple-element.92.refs_0_, ...), custom_call_target="tpu_custom_call" | custom-call | flops 8589934592 | bytes 28409856 | tf_op jit(solution)/shard_map/mlp_back_0/pallas_call | solution.py:1099
  416.7 71.2 %attention_back_0.1 = (bf16[1024,1024]{1,0:T(8,128)(2,1)}, f32[8,128]{1,0:T(8,128)}, bf16[2,128,1024]{2,1,0:T(8,128)(2,1)}, f32[8,1024]{1,0:T(8,128)}, bf16[4,12...) custom-call(bf16[4,2,128,1024]{3,2,1,0:T(8,128)(2,1)} %get-tuple-element.98.refs_0_, ...), custom_call_target="tpu_custom_call" | custom-call | flops 15032385536 | bytes 22122496 | tf_op jit(solution)/shard_map/attention_back_0/pallas_call | solution.py:1099
  487.9 1.1 bitcast_convert_fusion.2
  489.1 98.3 %leave.1 = (bf16[2,128,1024]{2,1,0:T(8,128)(2,1)}, bf16[2,128,2048]{2,1,0:T(8,128)(2,1)}, f32[16,1024]{1,0:T(8,128)}, bf16[2,128,1024]{2,1,0:T(8,128)(2,1)}) custom-call(bf16[4,2,128,1024]{3,2,1,0:T(8,128)(2,1)} %bitcast.126, bf16[4,128,2048]{2,1,0:T(8,128)(2,1)} %get-tuple-element.107.refs_1_, f32[8,1024]{1,0:T(8,128)} %get-tuple-element.108.refs_2_, ...), custom_call_target="tpu_custom_call" | custom-call | flops 10000000 | bytes 7012352 | tf_op jit(solution)/shard_map/leave/pallas_call | solution.py:1099
  587.4 1.2 bitcast_convert_fusion.3
  589.5 0.9 slice_reduce_fusion
  590.4 1.0 constant_dynamic-slice_fusion.8
  592.6 1.1 copy.64
  593.7 1.2 copy.63
  594.9 1.3 pad_maximum_fusion.2
  596.2 1.6 copy.58
  601.0 1.2 fusion.8
  602.8 1.2 fusion.7
  606.6 1.8 pad_maximum_fusion.7
  608.3 3.1 pad_maximum_fusion
  612.1 1.5 pad_maximum_fusion.1
  613.5 1.9 maximum_select_fusion
  (96 shorter events, 21.6 us)
Async XLA Ops:
  0.6 11.2 %copy-start.5 = (bf16[2,1024,256]{2,1,0:T(8,128)(2,1)S(1)}, bf16[2,1024,256]{2,1,0:T(8,128)(2,1)}, u32[]{:S(2)}) copy-start(bf16[2,1024,256]{2,1,0:T(8,128)(2,1)} %param.29) | copy-start | bytes 3145732
  15.1 2.1 copy-start.8
  15.1 2.1 copy-start.9
  16.1 42.3 %copy-start.10 = (bf16[256,256]{1,0:T(8,128)(2,1)S(1)}, bf16[256,256]{1,0:T(8,128)(2,1)}, u32[]{:S(2)}) copy-start(bf16[256,256]{1,0:T(8,128)(2,1)} %copy.46) | copy-start | bytes 393220
  17.2 42.1 %copy-start.11 = (pred[128]{0:T(512)(128)(4,1)S(1)}, pred[128]{0:T(512)(128)(4,1)}, u32[]{:S(2)}) copy-start(pred[128]{0:T(512)(128)(4,1)} %get-tuple-element.168) | copy-start | bytes 388
  264.5 349.0 %collective-permute-start = (bf16[128,1024]{1,0:T(8,128)(2,1)}, bf16[128,1024]{1,0:T(8,128)(2,1)}, u32[]{:S(2)}, u32[]{:S(2)}) collective-permute-start(bf16[128,1024]{1,0:T(8,128)(2,1)} %get-tuple-element.145), channel_id=1, source_target_pairs={{0,4},{4,0},{1,5},{5,1},{2,6},{6,2},{3,7},{7,3},{8,12},{12,8},{9,1... | collective-permute-start | bytes 786440 | tf_op jit(solution)/shard_map/ppermute | solution.py:1158
  489.1 98.3 %copy-start = (f32[256,1024]{1,0:T(8,128)}, f32[256,1024]{1,0:T(8,128)S(1)}, u32[]{:S(2)}) copy-start(f32[256,1024]{1,0:T(8,128)S(1)} %bitcast_convert_fusion.2) | copy-start | bytes 3145732
  587.3 5.2 slice-start
  588.6 6.3 %copy-start.1 = (f32[256,1024]{1,0:T(8,128)}, f32[256,1024]{1,0:T(8,128)S(1)}, u32[]{:S(2)}) copy-start(f32[256,1024]{1,0:T(8,128)S(1)} %bitcast_convert_fusion.3) | copy-start | bytes 3145732
  593.7 1.2 copy-start.2
  596.2 1.8 slice-start.1
  596.2 2.0 slice-start.2
  596.2 4.5 copy-start.3
  601.0 1.5 copy-start.4
  612.1 1.5 copy-start.6
  612.1 3.4 copy-start.7

commit v3 on v2

--- a/solution.py
+++ b/solution.py
@@ -96,60 +96,100 @@
     return 2 if rows % 128 == 0 else 1
 
 
-class WeightGather(Job):
-    uses_ctx = uses_fsdp = True
-
-    def __init__(self, packed, n, hooks):
-        self.n, self.hooks = n, hooks
-        self.ins = [(packed, HBM_SPEC)]
-        self.outs = [(jax.ShapeDtypeStruct((n, *packed.shape), BF16), HBM_SPEC)]
-        self.rows = packed.shape[1]
-        self.ch = chunks_of(self.rows)
-        self.scratch = [DMA((max(n, 5), self.ch))] + [DMA((n, self.ch))] * 3 + [DMA]
+def cut_rows(ref, start, size):
+    index = (slice(None),) * (len(ref.shape) - 2) + (pl.ds(start, size),)
+    return ref.at[index]
+
+
+class OverFsdp(Job):
+    uses_fsdp = True
+
+    def __init__(self, weight, layer, n, hook, chunks=1, ctx_hooks=None):
+        self.n, self.layer, self.hook, self.ctx_hooks = n, layer, hook, ctx_hooks
+        self.uses_ctx = ctx_hooks is not None
+        shape = weight.shape[1:]
+        self.rows = shape[-2] // 2
+        self.ch = chunks if self.rows % (chunks * 16) == 0 else 1
+        half = jax.ShapeDtypeStruct((n, *shape[:-2], self.rows, shape[-1]), BF16)
+        self.ins = [(weight, HBM_SPEC)]
+        self.outs = [(half, HBM_SPEC)] * (2 if self.uses_ctx else 1)
+        self.scratch = [DMA((n + 1, self.ch)), DMA((n, self.ch)), DMA]
+        if self.uses_ctx:
+            self.scratch += [DMA((n, self.ch)), DMA((n, self.ch)), DMA]
 
     def refs(self, ins, outs, scratch):
-        (self.src,), (self.out,) = ins, outs
-        self.z_send, self.z_recv, self.x_send, self.x_recv, self.near = scratch
-
-    def cut(self, ref, ch):
+        self.src = ins[0].at[self.layer]
+        self.near = outs[0]
+        self.send, self.recv, self.here = scratch[:3]
+        if self.uses_ctx:
+            self.far = outs[1]
+            self.x_send, self.x_recv, self.here_far = scratch[3:]
+
+    def mine(self, ch):
         size = self.rows // self.ch
-        return ref.at[pl.ds(ch * size, size)]
-
-    def over_z(self, k, ch, to):
+        start = pl.multiple_of(self.c * self.rows + ch * size, size)
+        return cut_rows(self.src, start, size)
+
+    def part(self, ref, frm, ch):
+        size = self.rows // self.ch
+        return cut_rows(ref.at[frm], ch * size, size)
+
+    def out_to(self, k, off, ch):
+        to = (self.z + off + self.n) % self.n
         return remote(
-            self.cut(self.src.at[self.c], ch), self.cut(self.out.at[self.z, self.c], ch),
-            self.z_send.at[k, ch], self.z_recv.at[self.z, ch], {"fsdp": to},
+            self.mine(ch), self.part(self.near, self.z, ch),
+            self.send.at[k, ch], self.recv.at[self.z, ch], {"fsdp": to},
         )
 
     def arrived(self, frm, ch):
-        block = self.cut(self.out.at[frm, self.c], ch)
-        return remote(block, block, self.z_send.at[4, ch], self.z_recv.at[frm, ch], {"fsdp": 3 - frm})
-
-    def over_x(self, frm, half, ch):
-        block = self.cut(self.out.at[frm, half], ch)
+        block = self.part(self.near, frm, ch)
         return remote(
-            block, block, self.x_send.at[frm, ch], self.x_recv.at[frm, ch], {"ctx": 1 - self.c}
-        )
-
-    def copy_near(self):
-        return pltpu.make_async_copy(self.src, self.out.at[self.z], self.near)
+            block, block, self.send.at[self.n, ch], self.recv.at[frm, ch], {"fsdp": self.n - 1 - frm}
+        )
+
+    def over_x(self, frm, ch):
+        return remote(
+            self.part(self.near, frm, ch), self.part(self.far, frm, ch),
+            self.x_send.at[frm, ch], self.x_recv.at[frm, ch], {"ctx": 1 - self.c},
+        )
+
+    def local(self, half, out, sem):
+        start = pl.multiple_of(half * self.rows, self.rows)
+        return pltpu.make_async_copy(
+            cut_rows(self.src, start, self.rows), out.at[self.z], sem
+        )
 
     def offsets(self):
-        if self.n == 4:
-            return [(k, off) for k, off in enumerate((1, -1, 2, -2))]
-        return [(k, k) for k in range(1, self.n)]
+        return (2, -2, 1, -1) if self.n == 4 else range(1, self.n)
+
+    def sources(self):
+        return (1, -1, 2, -2, 3, -3) if self.n == 4 else range(1, self.n)
 
     def inside(self, off):
         other = self.z + off
         return (other >= 0) & (other < self.n) if self.n == 4 else (other > -1)
 
+    def relays(self):
+        return (self.z == 1) | (self.z == 2)
+
     def start(self):
         for ch in range(self.ch):
-            for k, off in self.offsets():
+            for k, off in enumerate(self.offsets()):
                 @pl.when(self.inside(off))
                 def _():
-                    self.over_z(k, ch, (self.z + off + self.n) % self.n).start()
-        self.copy_near().start()
+                    self.out_to(k, off, ch).start()
+        self.local(self.c, self.near, self.here).start()
+        if self.uses_ctx:
+            self.local(1 - self.c, self.far, self.here_far).start()
+
+    def relay(self):
+        if self.n == 4:
+            @pl.when(self.relays())
+            def _():
+                for ch in range(self.ch):
+                    through = self.arrived(jnp.where(self.z == 2, 0, 3), ch)
+                    through.wait_recv()
+                    through.start()
 
     def take(self, off):
         frm = (self.z + off + self.n) % self.n
@@ -157,42 +197,167 @@
         @pl.when(self.inside(off))
         def _():
             for ch in range(self.ch):
-                self.arrived(frm, ch).wait_recv()
                 if self.n == 4 and abs(off) == 2:
-                    @pl.when((self.z == 2) & (frm == 0) | (self.z == 1) & (frm == 3))
+                    @pl.when(jnp.logical_not((self.z == 2) & (frm == 0) | (self.z == 1) & (frm == 3)))
                     def _():
-                        self.arrived(frm, ch).start()
-                self.over_x(frm, self.c, ch).start()
+                        self.arrived(frm, ch).wait_recv()
+                else:
+                    self.arrived(frm, ch).wait_recv()
+                if self.uses_ctx:
+                    self.over_x(frm, ch).start()
 
     def steps(self):
-        if self.n == 4:
-            groups = [(1, -1), (2, -2), (3, -3)]
-        else:
-            groups = [tuple(range(1, self.n))]
-        out = []
-        for hook, group in zip(self.hooks, groups):
-            for off in group:
-                out.append((hook, functools.partial(self.take, off)))
+        out = [(self.hook, self.relay)]
+        if self.uses_ctx:
+            for i, off in enumerate(self.sources()):
+                out.append((self.ctx_hooks[min(i // 2, 2)], functools.partial(self.take, off)))
         return out
 
     def end(self):
-        for ch in range(self.ch):
-            for off in (1, -1, 2, -2, 3, -3) if self.n == 4 else range(1, self.n):
-                frm = (self.z + off + self.n) % self.n
-
+        for off in self.sources():
+            frm = (self.z + off + self.n) % self.n
+            if not self.uses_ctx:
+                self.take(off)
+            else:
                 @pl.when(self.inside(off))
                 def _():
-                    self.over_x(frm, 1 - self.c, ch).wait_recv()
-                    self.over_x(frm, self.c, ch).wait_send()
-            for k, off in self.offsets():
+                    for ch in range(self.ch):
+                        self.over_x(frm, ch).wait()
+        for ch in range(self.ch):
+            for k, off in enumerate(self.offsets()):
                 @pl.when(self.inside(off))
                 def _():
-                    self.over_z(k, ch, (self.z + off + self.n) % self.n).wait_send()
+                    self.out_to(k, off, ch).wait_send()
             if self.n == 4:
-                @pl.when((self.z == 1) | (self.z == 2))
+                @pl.when(self.relays())
                 def _():
                     self.arrived(jnp.where(self.z == 2, 0, 3), ch).wait_send()
-        self.copy_near().wait()
+        self.local(self.c, self.near, self.here).wait()
+        if self.uses_ctx:
+            self.local(1 - self.c, self.far, self.here_far).wait()
+
+
+class OverCtx(Job):
+    uses_ctx = True
+
+    def __init__(self, weight, layer, near, n):
+        self.n, self.layer = n, layer
+        self.ins = [(weight, HBM_SPEC), (near, HBM_SPEC)]
+        self.outs = [(jax.ShapeDtypeStruct(near.shape, BF16), HBM_SPEC)]
+        self.scratch = [DMA((n,)), DMA((n,)), DMA]
+
+    def refs(self, ins, outs, scratch):
+        self.src, self.near = ins[0].at[self.layer], ins[1]
+        (self.far,) = outs
+        self.send, self.recv, self.here = scratch
+
+    def copy(self, k):
+        frm = (self.z + k) % self.n
+        return remote(
+            self.near.at[frm], self.far.at[frm], self.send.at[k], self.recv.at[k],
+            {"ctx": 1 - self.c},
+        )
+
+    def local(self):
+        rows = self.near.shape[-2]
+        start = pl.multiple_of((1 - self.c) * rows, rows)
+        return pltpu.make_async_copy(cut_rows(self.src, start, rows), self.far.at[self.z], self.here)
+
+    def start(self):
+        for k in range(1, self.n):
+            self.copy(k).start()
+        self.local().start()
+
+    def end(self):
+        for k in range(1, self.n):
+            self.copy(k).wait()
+        self.local().wait()
+
+
+class Loads:
+    def __init__(self, sems):
+        self.sems, self.copies = sems, []
+
+    def add(self, near, far, out):
+        c = lax.axis_index("ctx")
+        for half, ref in ((c, near), (1 - c, far)):
+            if len(ref.shape) == 3:
+                pairs = [(ref, out.at[:, half])]
+            else:
+                width = ref.shape[-1]
+                pairs = [
+                    (ref.at[:, j], out.at[:, half, :, j * width : (j + 1) * width])
+                    for j in range(ref.shape[1])
+                ]
+            for src, dst in pairs:
+                copy = pltpu.make_async_copy(src, dst, self.sems.at[len(self.copies)])
+                copy.start()
+                self.copies.append(copy)
+
+    def wait(self):
+        for copy in self.copies:
+            copy.wait()
+
+
+class ParamJob(Job):
+    uses_fsdp = True
+
+    def __init__(self, wide, narrow, n, dim):
+        self.n, self.n_wide = n, len(wide)
+        self.ins = [(a, VMEM_SPEC) for a in (*wide, *narrow)]
+        shape = (8 * LAYERS, dim)
+        self.outs = [(jax.ShapeDtypeStruct(shape, F32), VMEM_SPEC)]
+        self.scratch = [
+            VMEM(shape, F32), VMEM(shape, BF16), VMEM((n, *shape), BF16), DMA((n,)), DMA((n,))
+        ]
+
+    def refs(self, ins, outs, scratch):
+        self.wide, self.narrow = ins[: self.n_wide], ins[self.n_wide :]
+        (self.out,) = outs
+        self.work, self.src, self.got, self.ssem, self.rsem = scratch
+
+    def copy(self, k):
+        return remote(
+            self.src, self.got.at[k], self.ssem.at[k], self.rsem.at[k],
+            {"fsdp": (self.z + k) % self.n},
+        )
+
+    def start(self):
+        work = self.work
+        dim = work.shape[1]
+        work[...] = jnp.zeros_like(work)
+        shard = self.wide[0].shape[1]
+        query, value, expand = self.narrow
+        cut = query.shape[2]
+        heads = query.shape[1]
+        for l in range(LAYERS):
+            for k, ref in enumerate(self.wide):
+                work[8 * l + k : 8 * l + k + 1, :shard] = ref[l : l + 1, :].astype(F32)
+            for row, base, ref in ((6, 0, query), (6, heads * HD, value), (7, 0, expand)):
+                block = ref[l].astype(F32)
+                for h in range(ref.shape[1]):
+                    at = base + h * HD
+                    work[8 * l + row : 8 * l + row + 1, at : at + cut] = block[h : h + 1, :]
+        all_rows = work[...]
+        row = lax.broadcasted_iota(jnp.int32, all_rows.shape, 0) % 8
+        by_shard = pltpu.roll(all_rows, self.z * shard, 1)
+        by_cut = pltpu.roll(all_rows, self.z * cut, 1)
+        placed = jnp.where(row < 6, by_shard, by_cut)
+        work[...] = placed
+        self.src[...] = placed.astype(BF16)
+        for k in range(1, self.n):
+            self.copy(k).start()
+
+    def finish(self):
+        total = self.work[...]
+        for k in range(1, self.n):
+            self.copy(k).wait_recv()
+            total += self.got[k].astype(F32)
+        self.out[...] = total
+
+    def end(self):
+        for k in range(1, self.n):
+            self.copy(k).wait_send()
 
 
 class Exchange(Job):
@@ -240,40 +405,6 @@
 
     def end(self):
         gather_wait(self.links, 0, self.out)
-
-
-class ParamSum(Job):
-    uses_fsdp = True
-
-    def __init__(self, placed, n):
-        self.n = n
-        self.ins = [(placed, VMEM_SPEC)]
-        self.outs = [(jax.ShapeDtypeStruct(placed.shape, F32), VMEM_SPEC)]
-        self.scratch = [VMEM((n, *placed.shape), BF16), DMA((n,)), DMA((n,))]
-
-    def refs(self, ins, outs, scratch):
-        (self.src,), (self.out,), (self.got, self.ssem, self.rsem) = ins, outs, scratch
-
-    def copy(self, k):
-        return remote(
-            self.src, self.got.at[k], self.ssem.at[k], self.rsem.at[k],
-            {"fsdp": (self.z + k) % self.n},
-        )
-
-    def start(self):
-        for k in range(1, self.n):
-            self.copy(k).start()
-
-    def finish(self):
-        total = self.src[...].astype(F32)
-        for k in range(1, self.n):
-            self.copy(k).wait_recv()
-            total += self.got[k].astype(F32)
-        self.out[...] = total
-
-    def end(self):
-        for k in range(1, self.n):
-            self.copy(k).wait_send()
 
 
 class CtxSum(Job):
@@ -333,8 +464,8 @@
 class FsdpSum(Job):
     uses_ctx = uses_fsdp = True
 
-    def __init__(self, rows, n, hooks, source=None):
-        self.n, self.hooks, self.source = n, hooks, source
+    def __init__(self, rows, n, hooks, source=None, sends=()):
+        self.n, self.hooks, self.source, self.sends = n, hooks, source, sends
         shape = rows.shape
         self.ins = [] if source else [(rows, VMEM_SPEC)]
         self.outs = [(jax.ShapeDtypeStruct((2, *shape[1:]), BF16), VMEM_SPEC)]
@@ -404,7 +535,7 @@
                 self.send(d)
 
     def relay(self):
-        for d, me in ((0, 1), (3, 2)):
+        for d, me in ((0, 1), (3, 2)) if self.n == 4 else ():
             @pl.when(self.z == me)
             def _():
                 for ch in range(self.ch):
@@ -455,8 +586,12 @@
             self.over_x(ch).start()
 
     def steps(self):
-        out = [(self.hooks[0], self.relay)] if self.n == 4 else []
-        return out + [(self.hooks[1], self.total)]
+        out = [
+            (self.sends[i * len(self.sends) // self.n], functools.partial(self.send, d))
+            for i, d in enumerate(self.order())
+            if self.sends
+        ]
+        return out + [(self.hooks[0], self.relay), (self.hooks[1], self.total)]
 
     def end(self):
         for ch in range(self.ch):
@@ -621,28 +756,27 @@
 
 def enter_kernel(jobs, first, send, recv):
     t, sib, peer = partners()
-    tokens, params, weights = jobs
+    params, tokens, attn, expand = jobs
     entry_barrier(jobs)
     links = Links(send, recv, sib, peer)
+    tokens.start()
+    attn.start()
     params.start()
-    tokens.start()
-    weights.start()
+    expand.start()
     params.finish()
     tokens.end()
     for s in range(2):
         unit, _ = statistics(tokens.out[s].astype(F32))
         first[2 + s, 0] = (unit * params.out[0:1, :] + params.out[1:2, :]).astype(BF16)
         gather_start(links, 0, first, s)
-    for hook, step in weights.steps():
-        if hook == 0:
-            step()
+    attn.relay()
+    for off in attn.sources():
+        attn.take(off)
+    expand.relay()
     gather_forward(links, 0, first)
-    for hook, step in weights.steps():
-        if hook == 1:
-            step()
     gather_wait(links, 0, first)
-    params.end()
-    weights.end()
+    for job in (params, attn, expand):
+        job.end()
 
 
 def pair_tile(pair, h):
@@ -652,9 +786,9 @@
 
 def attention_kernel(
     jobs, heads, base,
-    first, weight, params, key_extra, resid,
+    first, params, key_extra, resid, near, far,
     second, middle, q_out, k_out, v_out, mixed_out,
-    part, sent, got, own, send, recv,
+    part, sent, got, own, send, recv, weight, load,
 ):
     t, sib, peer = partners()
     background = Background(jobs)
@@ -663,6 +797,9 @@
     links = Links(send, recv, sib, peer)
     scatter = Scatter(links, part, sent, got, own)
     width = heads * HD
+    loads = Loads(load)
+    loads.add(near, far, weight)
+    loads.wait()
     weight = whole(weight)
     out_bias, gain, shift = (params[base + k : base + k + 1, :] for k in (2, 3, 4))
     q_bias = params[base + 6 : base + 7, :width]
@@ -693,6 +830,7 @@
         return carry
 
     lax.fori_loop(0, 4, project, 0)
+    background.at(0)
 
     def attend(b, carry):
         at = pl.ds(pl.multiple_of(b * rows, rows), rows)
@@ -722,7 +860,7 @@
         mixed_out[at, :] = mixed
         part[...] = mm_nt(mixed, weight[:, 3 * width :])
         scatter.block(b)
-        background.loop(b)
+        background.loop(b, 4, 1)
         return carry
 
     lax.fori_loop(0, 4, attend, 0)
@@ -732,9 +870,9 @@
         unit, _ = statistics(mid)
         second[2 + s, 0] = (unit * gain + shift).astype(BF16)
         gather_start(links, 3, second, s)
-        background.at(4 + s)
+        background.at(5 + s)
     gather_forward(links, 3, second)
-    background.at(6)
+    background.at(7)
     gather_wait(links, 3, second)
     scatter.end()
     background.end()
@@ -742,9 +880,9 @@
 
 def mlp_kernel(
     jobs, last, base,
-    second, weight, params, middle,
+    second, params, middle, near_e, far_e, near_r, far_r,
     active_out, slope_out, resid, nxt,
-    part, sent, got, own, send, recv,
+    part, sent, got, own, send, recv, expand, reduce, load,
 ):
     t, sib, peer = partners()
     background = Background(jobs)
@@ -754,8 +892,12 @@
     scatter = Scatter(links, part, sent, got, own)
     half = second.shape[2]
     rows = 2 * half
-    weight = whole(weight)
-    hidden = weight.shape[1] // 2
+    loads = Loads(load)
+    loads.add(near_e, far_e, expand)
+    loads.add(near_r, far_r, reduce)
+    loads.wait()
+    expand, reduce = whole(expand), whole(reduce)
+    hidden = expand.shape[1]
     out_bias = params[base + 5 : base + 6, :]
     following = 0 if last else base + 8
     gain, shift = (params[following + k : following + k + 1, :] for k in (0, 1))
@@ -765,14 +907,14 @@
         at = pl.ds(pl.multiple_of(b * rows, rows), rows)
         x = rows_of(second, b)
         for n in range(0, hidden, step):
-            before = mm(x, weight[:, n : n + step]) + params[base + 7 : base + 8, n : n + step]
+            before = mm(x, expand[:, n : n + step]) + params[base + 7 : base + 8, n : n + step]
             cdf = 0.5 * (1.0 + lax.erf(before * INV_SQRT2))
             active_out[at, n : n + step] = (before * cdf).astype(BF16)
             slope = cdf + before * (jnp.exp(before * before * -0.5) * INV_SQRT_2PI)
             slope_out[at, n : n + step] = slope.astype(BF16)
-        part[...] = mm_nt(active_out[at, :], weight[:, hidden:])
+        part[...] = mm_nt(active_out[at, :], reduce[...])
         scatter.block(b)
-        background.loop(b)
+        background.loop(b, 4, 1)
         return carry
 
     lax.fori_loop(0, 4, block, 0)
@@ -785,17 +927,17 @@
             unit, _ = statistics(res)
             nxt[2 + s, 0] = (unit * gain + shift).astype(BF16)
             gather_start(links, 3, nxt, s)
-        background.at(4 + s)
+        background.at(5 + s)
     if not last:
         gather_forward(links, 3, nxt)
-    background.at(6)
+    background.at(7)
     if not last:
         gather_wait(links, 3, nxt)
     scatter.end()
     background.end()
 
 
-def token_product(left, right, out, offset):
+def token_product(left, right, out, offset=0):
     depth = left.shape[-1]
     total = left.shape[0] * left.shape[1] * left.shape[2]
     step = 256
@@ -811,9 +953,9 @@
 
 def mlp_back_kernel(
     jobs, base,
-    grad, weight, active, slope, second, middle, carry_in, params,
-    weight_grad, carry_out, rows_out, vectors,
-    part, sent, got, own, send, recv, d_before,
+    grad, active, slope, second, middle, carry_in, params, near_e, far_e, near_r, far_r,
+    expand_grad, reduce_grad, carry_out, rows_out, vectors,
+    part, sent, got, own, send, recv, d_before, expand, reduce, load,
 ):
     t, sib, peer = partners()
     background = Background(jobs)
@@ -821,7 +963,11 @@
     background.start()
     links = Links(send, recv, sib, peer)
     scatter = Scatter(links, part, sent, got, own)
-    weight = whole(weight)
+    loads = Loads(load)
+    loads.add(near_e, far_e, expand)
+    loads.add(near_r, far_r, reduce)
+    loads.wait()
+    expand, reduce = whole(expand), whole(reduce)
     gain = params[base + 3 : base + 4, :]
     half = grad.shape[2]
     rows = 2 * half
@@ -833,17 +979,17 @@
         at = pl.ds(pl.multiple_of(b * rows, rows), rows)
         x = rows_of(grad, b)
         for n in range(0, hidden, step):
-            d_act = mm(x, weight[:, hidden + n : hidden + n + step])
+            d_act = mm(x, reduce[:, n : n + step])
             d_bef = (d_act * slope[at, n : n + step].astype(F32)).astype(BF16)
             d_before[at, n : n + step] = d_bef
             vectors[4:5, n : n + step] += jnp.sum(d_bef.astype(F32), axis=0, keepdims=True)
-        part[...] = mm_nt(d_before[at, :], weight[:, :hidden])
+        part[...] = mm_nt(d_before[at, :], expand[...])
         scatter.block(b)
         background.loop(b)
         return carry
 
     lax.fori_loop(0, 4, block, 0)
-    token_product(grad, active, weight_grad, hidden)
+    token_product(grad, active, reduce_grad)
     background.at(4)
 
     def finish(s):
@@ -861,7 +1007,7 @@
 
     finish(0)
     background.at(5)
-    token_product(second, d_before, weight_grad, 0)
+    token_product(second, d_before, expand_grad)
     finish(1)
     gather_forward(links, 3, rows_out)
     background.at(6)
@@ -872,9 +1018,9 @@
 
 def attention_back_kernel(
     jobs, heads, last, base,
-    grad, weight, mixed, q_in, k_in, v_in, first, carry_in, resid, params,
+    grad, mixed, q_in, k_in, v_in, first, carry_in, resid, params, near, far,
     weight_grad, carry_out, rows_out, vectors,
-    part, sent, got, own, send, recv, d_out, d_joint, d_key, d_value,
+    part, sent, got, own, send, recv, d_joint, d_key, d_value, weight, load,
 ):
     t, sib, peer = partners()
     background = Background(jobs)
@@ -883,6 +1029,9 @@
     links = Links(send, recv, sib, peer)
     scatter = Scatter(links, part, sent, got, own)
     width = heads * HD
+    loads = Loads(load)
+    loads.add(near, far, weight)
+    loads.wait()
     weight = whole(weight)
     gain = params[base : base + 1, :]
     half = grad.shape[2]
@@ -1044,11 +1193,11 @@
 
 
 def leave_kernel(jobs):
-    attn_ctx, attn_fsdp, mlp_fsdp, vectors, rows = jobs
+    attn_ctx, attn_fsdp, reduce_fsdp, vectors, rows = jobs
     entry_barrier(jobs)
-    mlp_fsdp.start()
+    attn_ctx.start()
+    reduce_fsdp.start()
     vectors.start()
-    attn_ctx.start()
     rows.start()
     vectors.fold(0)
     for i, k in enumerate(attn_ctx.order()):
@@ -1056,23 +1205,56 @@
         attn_fsdp.send(k)
         if i in (1, 2):
             vectors.fold(i)
-        if i == 2 and mlp_fsdp.n == 4:
-            mlp_fsdp.relay()
-    if attn_fsdp.n == 4:
-        attn_fsdp.relay()
+        if i == 1:
+            reduce_fsdp.relay()
+    attn_fsdp.relay()
+    reduce_fsdp.total()
     vectors.finish()
-    mlp_fsdp.total()
     attn_fsdp.total()
     for job in jobs:
         job.end()
 
 
+def finish_kernel(
+    attn_0, attn_1, expand_0, expand_1, reduce_0, reduce_1, vectors,
+    joint, out, expand, reduce, wide, query, value, hidden,
+):
+    z = lax.axis_index("fsdp")
+    half = attn_0.shape[1]
+    width = joint.shape[3]
+    shard = 2 * half
+    for l, (a, e, r) in enumerate(((attn_0, expand_0, reduce_0), (attn_1, expand_1, reduce_1))):
+        rows = a[...].reshape(shard, a.shape[2]).astype(F32)
+        for k in range(3):
+            joint[l, k] = rows[:, k * width : (k + 1) * width]
+        out[l] = rows[:, 3 * width :].T
+        expand[l] = e[...].reshape(shard, e.shape[2]).astype(F32)
+        reduce[l] = r[...].reshape(shard, r.shape[2]).astype(F32).T
+    cut = query.shape[2]
+    heads = query.shape[1]
+    dim = vectors.shape[1]
+    own = pltpu.roll(vectors[...], lax.rem(dim - z * shard, dim), 1)
+    by_cut = pltpu.roll(vectors[...], lax.rem(dim - z * cut, dim), 1)
+    for l in range(LAYERS):
+        for k in range(6):
+            wide[k, l : l + 1, :] = own[8 * l + k : 8 * l + k + 1, :shard]
+        for row, base, ref in ((6, 0, query), (6, heads * HD, value), (7, 0, hidden)):
+            for h in range(ref.shape[1]):
+                at = base + h * HD
+                ref[l, h : h + 1, :] = by_cut[8 * l + row : 8 * l + row + 1, at : at + cut]
+
+
 def whole(ref):
     return ref.reshape(ref.shape[0] * ref.shape[1] * ref.shape[2], ref.shape[3])
 
 
 def call(kernel, name, outs, scratch, collective_id, flops, args, jobs=()):
-    ins = [(a, VMEM_SPEC) for a in args] + [pair for job in jobs for pair in job.ins]
+    args = [
+        (a, spec)
+        for arg in args
+        for a, spec in ([(arg, VMEM_SPEC)] if not isinstance(arg, tuple) else [(a, HBM_SPEC) for a in arg])
+    ]
+    ins = args + [pair for job in jobs for pair in job.ins]
     results = [(o, VMEM_SPEC) for o in outs] + [pair for job in jobs for pair in job.outs]
     scratch = list(scratch)
     n_scratch = len(scratch)
@@ -1125,38 +1307,10 @@
     width = joint_weight.shape[3]
     heads = width // HD
     hidden = expand_weight.shape[2]
-    z = lax.axis_index("fsdp")
-
-    def packed(parts):
-        return jnp.concatenate(parts, axis=1).reshape(ctx_size, shard // ctx_size, -1)
-
-    def attn_parts(l):
-        joint = joint_weight[l]
-        return packed([joint[:, 0], joint[:, 1], joint[:, 2], out_weight[l].T])
-
-    def mlp_parts(l):
-        return packed([expand_weight[l], reduce_weight[l].T])
-
-    slot = lax.broadcasted_iota(jnp.int32, (1, fsdp_size, 1), 1) == z
-
-    def placed(block):
-        spread = jnp.where(slot, block.reshape(-1, 1, block.shape[-1]), jnp.zeros((), BF16))
-        return spread.reshape(LAYERS, -1)
-
-    rows = [
-        placed(a)
-        for a in (first_gain, first_shift, out_bias, second_gain, second_shift, reduce_bias)
-    ]
-    both = jnp.concatenate([placed(query_bias), placed(value_bias)], axis=1)
-    rows.append(jnp.pad(both, ((0, 0), (0, dim - both.shape[1]))))
-    rows.append(placed(expand_bias))
-    params = jnp.stack(rows, axis=1).reshape(LAYERS * 8, dim)
-
-    def regroup(both):
-        mine = lax.dynamic_index_in_dim(both, c, 0, keepdims=False)
-        theirs = lax.dynamic_index_in_dim(both, 1 - c, 0, keepdims=False)
-        got = lax.ppermute(theirs, "ctx", [(0, 1), (1, 0)])
-        return jnp.where(c == 0, jnp.stack([mine, got]), jnp.stack([got, mine]))
+    attn_w = jnp.concatenate(
+        [joint_weight.transpose(0, 2, 1, 3), out_weight.transpose(0, 2, 1)[:, None]], axis=1
+    )
+    reduce_w = reduce_weight.transpose(0, 2, 1)
 
     valid = lax.dynamic_index_in_dim(key_valid, c, 0, keepdims=False)
     bias = jnp.where(valid == 1, 0.0, MASKED).astype(F32)
@@ -1170,12 +1324,29 @@
     every = jax.ShapeDtypeStruct((4, 2, half, dim), BF16)
     own = jax.ShapeDtypeStruct((2, half, dim), F32)
     own_low = jax.ShapeDtypeStruct((2, half, dim), BF16)
+    tiny = jax.ShapeDtypeStruct((8, LANES), F32)
+    vec = jax.ShapeDtypeStruct((8, dim), F32)
+    square = jax.ShapeDtypeStruct((dim, hidden), BF16)
     count = 8 * half
+    n = fsdp_size
     scratch = scatter_scratch(half, dim)
-    n = fsdp_size
-
-    jobs = [Exchange(tokens), ParamSum(params, n), WeightGather(attn_parts(0), n, (0, 1, 1))]
-    first, tok, params, attn_weight = call(
+
+    def held(columns):
+        return VMEM((n, 2, shard // 2, columns), BF16)
+
+    attn_scratch = [held(4 * width), DMA((8,))]
+    mlp_scratch = [held(hidden), held(hidden), DMA((4,))]
+
+    jobs = [
+        ParamJob(
+            [first_gain, first_shift, out_bias, second_gain, second_shift, reduce_bias],
+            [query_bias, value_bias, expand_bias], n, dim,
+        ),
+        Exchange(tokens),
+        OverFsdp(attn_w, 0, n, None, 2, (0, 0, 0)),
+        OverFsdp(expand_weight, 0, n, None),
+    ]
+    first, params, tok, near_a, far_a, near_e = call(
         enter_kernel, "enter", [every], [DMA((3, 2)), DMA((3, 2))], 0, 10**7, [], jobs
     )
     resid = tok
@@ -1183,111 +1354,128 @@
     for l in range(LAYERS):
         last = l == LAYERS - 1
         heads_shape = jax.ShapeDtypeStruct((heads, count, LANES), BF16)
-        jobs = [WeightGather(mlp_parts(l), n, (1, 3, 6))]
         if last:
-            jobs.append(RowGather(cot, 1))
-        second, middle, q, k, v, mixed, mlp_weight, *grad = call(
+            jobs = [
+                OverCtx(expand_weight, l, near_e, n), OverCtx(reduce_w, l, near_r, n), RowGather(cot, 1)
+            ]
+        else:
+            jobs = [
+                OverCtx(expand_weight, l, near_e, n),
+                OverFsdp(reduce_w, l, n, 1, 1, (2, 3, 3)),
+                OverFsdp(attn_w, l + 1, n, 4),
+            ]
+        second, middle, q, k, v, mixed, far_e, *more = call(
             lambda jobs, *refs, base=8 * l: attention_kernel(jobs, heads, base, *refs),
             f"attention_{l}",
             [every, own, heads_shape, heads_shape, heads_shape, jax.ShapeDtypeStruct((count, width), BF16)],
-            scratch, 1 + 6 * l, 2 * count * dim * 4 * width + 16 * heads * count * count * HD,
-            [first, attn_weight, params, key_extra, resid], jobs,
-        )
+            scratch + attn_scratch, 1 + 6 * l,
+            2 * count * dim * 4 * width + 16 * heads * count * count * HD,
+            [first, params, key_extra, resid, (near_a, far_a)], jobs,
+        )
+        attn_pair = (near_a, far_a)
+        if last:
+            far_r, grad = more
+        else:
+            near_r, far_r, near_a = more
+        mlp_pairs = ((near_e, far_e), (near_r, far_r))
         rows_hidden = jax.ShapeDtypeStruct((count, hidden), BF16)
-        jobs = [] if last else [WeightGather(attn_parts(l + 1), n, (2, 4, 5)), Exchange(cotangent)]
+        jobs = [] if last else [
+            OverCtx(attn_w, l + 1, near_a, n),
+            OverFsdp(expand_weight, l + 1, n, 3),
+            OverFsdp(reduce_w, l + 1, n, 6),
+            Exchange(cotangent),
+        ]
         active, slope, out, nxt, *more = call(
             lambda jobs, *refs, base=8 * l, last=last: mlp_kernel(jobs, last, base, *refs),
             f"mlp_{l}",
-            [rows_hidden, rows_hidden,
-             jax.ShapeDtypeStruct((8, LANES), F32) if last else own, own_low if last else every],
-            scratch, 2 + 6 * l, 4 * count * dim * hidden,
-            [second, mlp_weight, params, middle], jobs,
-        )
-        saved.append((resid, first, q, k, v, mixed, middle, second, active, slope, attn_weight, mlp_weight))
+            [rows_hidden, rows_hidden, tiny if last else own, own_low if last else every],
+            scratch + mlp_scratch, 2 + 6 * l, 4 * count * dim * hidden,
+            [second, params, middle, *mlp_pairs], jobs,
+        )
+        saved.append((resid, first, q, k, v, mixed, middle, second, active, slope, attn_pair, mlp_pairs))
         resid, first = out, nxt
         if not last:
-            attn_weight, cot = more
-    output = regroup(nxt)
-
-    vec = jax.ShapeDtypeStruct((8, dim), F32)
+            far_a, near_e, near_r, cot = more
+
     carry = cot
-    (grad,) = grad
-    attn_grads, mlp_grads, attn_vec, mlp_vec = ([None] * LAYERS for _ in range(4))
-    attn_full = mlp_part = attn_part = None
+    attn_grads, expand_grads, reduce_grads, attn_vec, mlp_vec = ([None] * LAYERS for _ in range(5))
     for l in reversed(range(LAYERS)):
-        (resid, first, q, k, v, mixed, middle, second, active, slope, attn_weight, mlp_weight) = saved[l]
+        (resid, first, q, k, v, mixed, middle, second, active, slope, attn_pair, mlp_pairs) = saved[l]
         last = l == 0
-        jobs = []
-        if attn_full is not None:
-            jobs = [FsdpSum(mlp_part, n, (3, 6)), CtxSum(attn_full, n, (2, 4, 5, 6))]
-        mlp_full, carry, grad, mlp_vec[l], *more = call(
+        if last:
+            jobs = [
+                FsdpSum(expand_part, n, (3, 5)), FsdpSum(reduce_part, n, (5, 6)),
+                CtxSum(attn_full, n, (1, 3, 4, 5)),
+            ]
+        else:
+            jobs = [Exchange(nxt)]
+        expand_full, reduce_full, carry, grad, mlp_vec[l], *more = call(
             lambda jobs, *refs, base=8 * l: mlp_back_kernel(jobs, base, *refs),
             f"mlp_back_{l}",
-            [jax.ShapeDtypeStruct((dim, 2 * hidden), BF16), own, every, vec],
-            scratch + [VMEM((count, hidden), BF16)], 3 + 6 * l, 8 * count * dim * hidden,
-            [grad, mlp_weight, active, slope, second, middle, carry, params], jobs,
-        )
-        if more:
-            mlp_grads[l + 1], attn_part = more
-        jobs = [CtxSum(mlp_full, n, (2, 5, 8, 10))]
-        if attn_part is not None:
-            jobs.append(FsdpSum(attn_part, n, (2, 5)))
-        attn_full, carry, grad, attn_vec[l], mlp_part, *more = call(
+            [square, square, own, every, vec],
+            scratch + [VMEM((count, hidden), BF16)] + mlp_scratch, 3 + 6 * l, 8 * count * dim * hidden,
+            [grad, active, slope, second, middle, carry, params, *mlp_pairs], jobs,
+        )
+        if last:
+            expand_grads[l + 1], reduce_grads[l + 1], attn_part = more
+            ctx_job = CtxSum(expand_full, n, (0, 1, 2, 3), keep=True)
+            jobs = [
+                ctx_job, FsdpSum(expand_shape, n, (7, 9), source=ctx_job, sends=(0, 1, 2, 3)),
+                CtxSum(reduce_full, n, (5, 7, 9, 10)), FsdpSum(attn_part, n, (2, 3)),
+            ]
+        else:
+            (output,) = more
+            jobs = [CtxSum(expand_full, n, (0, 1, 2, 3)), CtxSum(reduce_full, n, (4, 7, 8, 10))]
+        attn_full, carry, grad, attn_vec[l], *more = call(
             lambda jobs, *refs, base=8 * l, last=last: attention_back_kernel(jobs, heads, last, base, *refs),
             f"attention_back_{l}",
-            [jax.ShapeDtypeStruct((dim, 4 * width), BF16),
-             jax.ShapeDtypeStruct((8, LANES), F32) if last else own, own_low if last else every, vec],
+            [jax.ShapeDtypeStruct((dim, 4 * width), BF16), tiny if last else own, own_low if last else every, vec],
             scratch
             + [
-                VMEM((heads, 8, LANES), BF16),
                 VMEM((count, 3 * width), BF16),
                 VMEM((heads, count, LANES), F32),
                 VMEM((heads, count, LANES), F32),
-            ],
+            ]
+            + attn_scratch,
             4 + 6 * l, 4 * count * dim * 4 * width + 40 * heads * count * count * HD,
-            [grad, attn_weight, mixed, q, k, v, first, carry, resid, params], jobs,
-        )
-        if more:
-            (attn_grads[l + 1],) = more
+            [grad, mixed, q, k, v, first, carry, resid, params, attn_pair], jobs,
+        )
+        if last:
+            expand_grads[l], reduce_part, attn_grads[l + 1] = more
+        else:
+            expand_part, reduce_part = more
+            expand_shape = jax.ShapeDtypeStruct(expand_part.shape, BF16)
 
     ctx_job = CtxSum(attn_full, n, (0, 1, 2, 3), keep=True)
-    attn_shape = jax.ShapeDtypeStruct((n, shard // 2, attn_full.shape[1]), BF16)
     jobs = [
         ctx_job,
-        FsdpSum(attn_shape, n, (0, 1), source=ctx_job),
-        FsdpSum(mlp_part, n, (0, 1)),
+        FsdpSum(jax.ShapeDtypeStruct((n, shard // 2, 4 * width), BF16), n, (0, 1), source=ctx_job),
+        FsdpSum(reduce_part, n, (0, 1)),
         VectorSum([attn_vec[0], mlp_vec[0], attn_vec[1], mlp_vec[1]], n, (0, 1, 2, 3)),
         Exchange(grad),
     ]
-    attn_grads[0], mlp_grads[0], vectors, row_grad = call(
+    attn_grads[0], reduce_grads[0], vectors, row_grad = call(
         leave_kernel, "leave", [], [], 5, 10**7, [], jobs
     )
-    attn_grads = [g.reshape(shard, -1).astype(F32) for g in attn_grads]
-    mlp_grads = [g.reshape(shard, -1).astype(F32) for g in mlp_grads]
-
-    vectors = vectors.reshape(LAYERS, 8, dim)
-    wide = lax.dynamic_slice_in_dim(vectors[:, :6], z * shard, shard, 2)
-
-    def spread(block):
-        block = block.reshape(LAYERS, -1, fsdp_size, HD // fsdp_size)
-        return lax.dynamic_index_in_dim(block, z, 2, keepdims=False)
-
+    results = [
+        jax.ShapeDtypeStruct(shape, F32)
+        for shape in (
+            (LAYERS, 3, shard, width), (LAYERS, width, shard), (LAYERS, shard, hidden),
+            (LAYERS, hidden, shard), (6, LAYERS, shard), query_bias.shape, value_bias.shape,
+            expand_bias.shape,
+        )
+    ]
+    joint, out, expand, reduce, wide, query, value, hidden_bias = pl.pallas_call(
+        finish_kernel,
+        name="finish",
+        out_shape=tuple(results),
+        in_specs=[VMEM_SPEC] * 7,
+        out_specs=tuple([VMEM_SPEC] * 8),
+        compiler_params=pltpu.CompilerParams(vmem_limit_bytes=VMEM_LIMIT),
+    )(*attn_grads, *expand_grads, *reduce_grads, vectors)
     return (
-        output,
-        row_grad,
-        wide[:, 0],
-        wide[:, 1],
-        jnp.stack([g[:, : 3 * width].reshape(shard, 3, width) for g in attn_grads]),
-        spread(vectors[:, 6, :width]),
-        spread(vectors[:, 6, width : 2 * width]),
-        jnp.stack([g[:, 3 * width :].T for g in attn_grads]),
-        wide[:, 2],
-        wide[:, 3],
-        wide[:, 4],
-        jnp.stack([g[:, :hidden] for g in mlp_grads]),
-        spread(vectors[:, 7, :hidden]),
-        jnp.stack([g[:, hidden:].T for g in mlp_grads]),
-        wide[:, 5],
+        output, row_grad, wide[0], wide[1], joint.transpose(0, 2, 1, 3), query, value, out,
+        wide[2], wide[3], wide[4], expand, hidden_bias, reduce, wide[5],
     )
 
 

time: 620 us -> 534 us (0.86)
  Pallas kernels: 564 us -> 515 us
  local copies, waits for them, and re-layouts: 30.6 us -> 5.36 us
  other arithmetic: 20.3 us -> 4.05 us
    pallas_call x10, Pallas kernels: 564 us -> 510 us  [call(): pl.pallas_call(body, name=name, out_shape=tuple((o for o, _ in results)),...]
    another operation x4 -> x0, other arithmetic: 7.61 us -> none  [the longest x1 3.11 us: local(): jnp.stack([g[:, :hidden] for g in mlp_grads])]
    slice x14 -> x0, local copies, waits for them, and re-layouts: 7.12 us -> none  [the longest x2 2.33 us: local(): g[:, hidden:]]
  transfers between devices with their start and end apart: 1 -> 0, of which waited for: 0 -> 0; matrix products, arithmetic and copies ran while one was open for 4% -> 0% of each run, Pallas kernels for 52% -> 0%
where the time goes in v3:
time: 534 us; the launch traced here: 525 us
  Pallas kernels  515 us (96%)
  local copies, waits for them, and re-layouts  5.36 us (1%)
    pallas_call x10, Pallas kernels, call(): pl.pallas_call(body, name=name, out_shape=tuple((o for o, _ in results)),...  510 us

profile of v3, /device:TPU:0, one launch (start us, length us, event | category | flops | bytes accessed | tf_op | source)
XLA Modules:
  0.0 525.5 jit_solution(1474262335984312120)
XLA Ops:
  0.6 0.0 copy-start
  0.7 0.8 compare_select_fusion
  1.5 1.0 select_convert_fusion.refs_2_
  2.5 1.1 copy.31
  3.6 2.2 pad_maximum_fusion.refs_10_.refs_9_.refs_7_
  5.8 0.0 copy-done
  5.8 1.3 copy.33
  7.1 53.0 %enter.1 = (bf16[4,2,128,1024]{3,2,1,0:T(8,128)(2,1)}, f32[16,1024]{1,0:T(8,128)}, bf16[2,128,1024]{2,1,0:T(8,128)(2,1)}, bf16[4,4,128,256]{3,2,1,0:T(8,128)(2,1...) custom-call(bf16[2,256]{1,0:T(2,128)(2,1)} %refs_0_.1, bf16[2,256]{1,0:T(2,128)(2,1)} %refs_1_.1, ...), custom_call_target="tpu_custom_call" | custom-call | flops 10000000 | bytes 8461824 | tf_op jit(solution)/shard_map/enter/pallas_call | solution.py:1281
  60.2 49.0 %attention_0.1 = (bf16[4,2,128,1024]{3,2,1,0:T(8,128)(2,1)}, f32[2,128,1024]{2,1,0:T(8,128)}, bf16[4,1024,128]{2,1,0:T(8,128)(2,1)}, bf16[4,1024,128]{2,1,0:T(8,...) custom-call(bf16[4,2,128,1024]{3,2,1,0:T(8,128)(2,1)} %get-tuple-ele, ...), custom_call_target="tpu_custom_call" | custom-call | flops 6442450944 | bytes 20250624 | tf_op jit(solution)/shard_map/attention_0/pallas_call | solution.py:1281
  109.2 45.8 %mlp_0.1 = (bf16[1024,1024]{1,0:T(8,128)(2,1)}, bf16[1024,1024]{1,0:T(8,128)(2,1)}, f32[2,128,1024]{2,1,0:T(8,128)}, bf16[4,2,128,1024]{3,2,1,0:T(8,128)(2,1)}, ...) custom-call(bf16[4,2,128,1024]{3,2,1,0:T(8,128)(2,1)} %get-tuple-ele, ...), custom_call_target="tpu_custom_call" | custom-call | flops 4294967296 | bytes 23134208 | tf_op jit(solution)/shard_map/mlp_0/pallas_call | solution.py:1281
  155.0 43.9 %attention_1.1 = (bf16[4,2,128,1024]{3,2,1,0:T(8,128)(2,1)}, f32[2,128,1024]{2,1,0:T(8,128)}, bf16[4,1024,128]{2,1,0:T(8,128)(2,1)}, bf16[4,1024,128]{2,1,0:T(8,...) custom-call(bf16[4,2,128,1024]{3,2,1,0:T(8,128)(2,1)} %get-tuple-ele, ...), custom_call_target="tpu_custom_call" | custom-call | flops 6442450944 | bytes 21299200 | tf_op jit(solution)/shard_map/attention_1/pallas_call | solution.py:1281
  198.9 24.1 %mlp_1.1 = (bf16[1024,1024]{1,0:T(8,128)(2,1)}, bf16[1024,1024]{1,0:T(8,128)(2,1)}, f32[8,128]{1,0:T(8,128)}, bf16[2,128,1024]{2,1,0:T(8,128)(2,1)}) custom-call(bf16[4,2,128,1024]{3,2,1,0:T(8,128)(2,1)} %get-tuple-element.108.refs_0_.refs_3_, f32[16,1024]{1,0:T(8,128)} %get-tuple-element.90.refs_1_.refs_6_.refs_8_, ...), custom_call_target="tpu_custom_call" | custom-call | flops 4294967296 | bytes 12128256 | tf_op jit(solution)/shard_map/mlp_1/pallas_call | solution.py:1281
  223.0 39.0 %mlp_back_1.1 = (bf16[1024,1024]{1,0:T(8,128)(2,1)}, bf16[1024,1024]{1,0:T(8,128)(2,1)}, f32[2,128,1024]{2,1,0:T(8,128)}, bf16[4,2,128,1024]{3,2,1,0:T(8,128)(2,...) custom-call(bf16[4,2,128,1024]{3,2,1,0:T(8,128)(2,1)} %get-tuple-element.107.refs_0_, ...), custom_call_target="tpu_custom_call" | custom-call | flops 8589934592 | bytes 22642688 | tf_op jit(solution)/shard_map/mlp_back_1/pallas_call | solution.py:1281
  262.0 64.2 %attention_back_1.1 = (bf16[1024,1024]{1,0:T(8,128)(2,1)}, f32[2,128,1024]{2,1,0:T(8,128)}, bf16[4,2,128,1024]{3,2,1,0:T(8,128)(2,1)}, f32[8,1024]{1,0:T(8,128)}...) custom-call(bf16[4,2,128,1024]{3,2,1,0:T(8,128)(2,1)} %get-tuple-element.116.refs_0_, ...), custom_call_target="tpu_custom_call" | custom-call | flops 15032385536 | bytes 23691264 | tf_op jit(solution)/shard_map/attention_back_1/pallas_call | solution.py:1281
  326.2 62.9 %mlp_back_0.1 = (bf16[1024,1024]{1,0:T(8,128)(2,1)}, bf16[1024,1024]{1,0:T(8,128)(2,1)}, f32[2,128,1024]{2,1,0:T(8,128)}, bf16[4,2,128,1024]{3,2,1,0:T(8,128)(2,...) custom-call(bf16[4,2,128,1024]{3,2,1,0:T(8,128)(2,1)} %get-tuple-ele, ...), custom_call_target="tpu_custom_call" | custom-call | flops 8589934592 | bytes 28409856 | tf_op jit(solution)/shard_map/mlp_back_0/pallas_call | solution.py:1281
  389.1 66.0 %attention_back_0.1 = (bf16[1024,1024]{1,0:T(8,128)(2,1)}, f32[8,128]{1,0:T(8,128)}, bf16[2,128,1024]{2,1,0:T(8,128)(2,1)}, f32[8,1024]{1,0:T(8,128)}, bf16[2,12...) custom-call(bf16[4,2,128,1024]{3,2,1,0:T(8,128)(2,1)} %get-tuple-element.131.refs_0_, ...), custom_call_target="tpu_custom_call" | custom-call | flops 15032385536 | bytes 21598208 | tf_op jit(solution)/shard_map/attention_back_0/pallas_call | solution.py:1281
  455.1 62.1 %leave.1 = (bf16[2,128,1024]{2,1,0:T(8,128)(2,1)}, bf16[2,128,1024]{2,1,0:T(8,128)(2,1)}, f32[16,1024]{1,0:T(8,128)}, bf16[2,128,1024]{2,1,0:T(8,128)(2,1)}) custom-call(bf16[4,2,128,1024]{3,2,1,0:T(8,128)(2,1)} %bitcast.38, bf16[4,128,1024]{2,1,0:T(8,128)(2,1)} %get-tuple-element.141.refs_1_, f32[8,1024]{1,0:T(8,128)} %get-tuple-element.142.refs_2_, ...), custom_call_target="tpu_custom_call" | custom-call | flops 10000000 | bytes 5439488 | tf_op jit(solution)/shard_map/leave/pallas_call | solution.py:1281
  517.2 0.0 copy-start.1
  517.2 0.0 copy-start.2
  517.2 4.9 finish.1
  522.1 1.4 slice_bitcast_fusion
  523.5 0.0 copy-done.1
  523.5 0.8 copy.43
  524.3 0.0 copy-done.2
  524.3 0.8 copy.44
  (4 shorter events, 0.0 us)
Async XLA Ops:
  0.6 5.2 copy-start
  517.2 6.3 %copy-start.1 = (bf16[2,128,1024]{2,1,0:T(8,128)(2,1)S(1)}, bf16[2,128,1024]{2,1,0:T(8,128)(2,1)}, u32[]{:S(2)}) copy-start(bf16[2,128,1024]{2,1,0:T(8,128)(2,1)} %get-tuple-element.186) | copy-start | bytes 1572868
  517.2 7.1 %copy-start.2 = (bf16[2,128,1024]{2,1,0:T(8,128)(2,1)S(1)}, bf16[2,128,1024]{2,1,0:T(8,128)(2,1)}, u32[]{:S(2)}) copy-start(bf16[2,128,1024]{2,1,0:T(8,128)(2,1)} %get-tuple-element.187) | copy-start | bytes 1572868

commit v4 on v3

--- a/solution.py
+++ b/solution.py
@@ -39,9 +39,9 @@
     return t, t + 1 - 2 * (t % 2), (t + 2) % 4
 
 
-def entry_barrier(jobs=()):
+def entry_barrier(jobs=(), tp=True):
     t, sib, peer = partners()
-    others = [{"tp": sib}, {"tp": peer}]
+    others = [{"tp": sib}, {"tp": peer}] if tp or any(job.uses_tp for job in jobs) else []
     if any(job.uses_ctx for job in jobs):
         others.append({"ctx": 1 - lax.axis_index("ctx")})
     if any(job.uses_fsdp for job in jobs):
@@ -71,11 +71,17 @@
 
 
 class Job:
+    uses_tp = False
     uses_ctx = False
     uses_fsdp = False
     ins = ()
     outs = ()
     scratch = ()
+    start_hook = None
+
+    def after(self, hook):
+        self.start_hook = hook
+        return self
 
     def bind(self, ins, outs, scratch):
         self.c = lax.axis_index("ctx")
@@ -383,30 +389,6 @@
         self.copy().wait()
 
 
-class RowGather(Job):
-    def __init__(self, own, hook):
-        self.hook = hook
-        self.ins = [(own, VMEM_SPEC)]
-        self.outs = [(jax.ShapeDtypeStruct((4, 2, *own.shape[1:]), own.dtype), VMEM_SPEC)]
-        self.scratch = [DMA((3, 2)), DMA((3, 2))]
-
-    def refs(self, ins, outs, scratch):
-        (self.src,), (self.out,) = ins, outs
-        t, sib, peer = partners()
-        self.links = Links(*scratch, sib, peer)
-
-    def start(self):
-        for s in range(2):
-            self.out[2 + s, 0] = self.src[s]
-            gather_start(self.links, 0, self.out, s)
-
-    def steps(self):
-        return [(self.hook, lambda: gather_forward(self.links, 0, self.out))]
-
-    def end(self):
-        gather_wait(self.links, 0, self.out)
-
-
 class CtxSum(Job):
     uses_ctx = True
 
@@ -462,13 +444,16 @@
 
 
 class FsdpSum(Job):
-    uses_ctx = uses_fsdp = True
-
-    def __init__(self, rows, n, hooks, source=None, sends=()):
+    uses_fsdp = True
+
+    def __init__(self, rows, n, hooks, source=None, sends=(), spread=True, direct=False):
         self.n, self.hooks, self.source, self.sends = n, hooks, source, sends
+        self.relays = n == 4 and not direct
+        self.spread = self.uses_ctx = spread
         shape = rows.shape
         self.ins = [] if source else [(rows, VMEM_SPEC)]
-        self.outs = [(jax.ShapeDtypeStruct((2, *shape[1:]), BF16), VMEM_SPEC)]
+        result = (2, *shape[1:]) if spread else shape[1:]
+        self.outs = [(jax.ShapeDtypeStruct(result, BF16), VMEM_SPEC)]
         self.rows = shape[1]
         self.ch = chunks_of(self.rows)
         self.scratch = [
@@ -500,7 +485,7 @@
     def to_relay(self, d, ch):
         return remote(
             self.cut(self.src.at[d], ch), self.cut(self.via.at[0], ch),
-            self.via_send.at[0, ch], self.via_recv.at[0, ch], {"fsdp": 1 if d == 0 else 2},
+            self.via_send.at[0, ch], self.via_recv.at[0, ch], {"fsdp": 2 if d == 0 else 1},
         )
 
     def relayed(self, d, ch):
@@ -510,12 +495,12 @@
         )
 
     def directly(self, d):
-        if self.n == 4 and d in (0, 3):
-            return (self.z == 2) if d == 0 else (self.z == 1)
+        if self.relays and d in (0, 3):
+            return (self.z == 1) if d == 0 else (self.z == 2)
         return self.z != d
 
     def send(self, d):
-        if self.n == 4 and d in (0, 3):
+        if self.relays and d in (0, 3):
             @pl.when(self.z == 3 - d)
             def _():
                 for ch in range(self.ch):
@@ -535,7 +520,7 @@
                 self.send(d)
 
     def relay(self):
-        for d, me in ((0, 1), (3, 2)) if self.n == 4 else ():
+        for d, me in ((0, 2), (3, 1)) if self.relays else ():
             @pl.when(self.z == me)
             def _():
                 for ch in range(self.ch):
@@ -545,15 +530,20 @@
                     self.cut(self.via.at[1], ch)[...] = (mine + theirs).astype(BF16)
                     self.relayed(d, ch).start()
 
+    then = None
+
+    def result(self, ch):
+        return self.cut(self.out.at[self.c] if self.spread else self.out, ch)
+
     def over_x(self, ch):
-        block = self.cut(self.out.at[self.c], ch)
+        block = self.result(ch)
         return remote(block, block, self.x_send.at[ch], self.x_recv.at[ch], {"ctx": 1 - self.c})
 
     def total(self):
         n = self.n
         for ch in range(self.ch):
             mine = self.cut(self.src.at[self.z], ch)
-            if n == 4:
+            if self.relays:
                 near = (self.z + 1) % 4
                 last = jnp.where(self.z == 0, 2, jnp.where(self.z == 3, 1, (self.z + 3) % 4))
                 first = jnp.where(self.z == 3, 2, near)
@@ -565,7 +555,7 @@
                     + self.cut(self.got.at[first], ch)[...].astype(F32)
                     + self.cut(self.got.at[last], ch)[...].astype(F32)
                 )
-                block = self.cut(self.out.at[self.c], ch)
+                block = self.result(ch)
 
                 @pl.when(inner)
                 def _():
@@ -582,8 +572,11 @@
                     frm = (self.z + k) % n
                     self.landed(frm, ch).wait_recv()
                     part += self.cut(self.got.at[frm], ch)[...].astype(F32)
-                self.cut(self.out.at[self.c], ch)[...] = part.astype(BF16)
-            self.over_x(ch).start()
+                self.result(ch)[...] = part.astype(BF16)
+            if self.spread:
+                self.over_x(ch).start()
+            elif self.then is not None:
+                self.then(ch)
 
     def steps(self):
         out = [
@@ -595,16 +588,19 @@
 
     def end(self):
         for ch in range(self.ch):
-            other = self.cut(self.out.at[1 - self.c], ch)
-            remote(other, other, self.x_send.at[ch], self.x_recv.at[ch], {"ctx": 1 - self.c}).wait_recv()
-            self.over_x(ch).wait_send()
+            if self.spread:
+                other = self.cut(self.out.at[1 - self.c], ch)
+                remote(
+                    other, other, self.x_send.at[ch], self.x_recv.at[ch], {"ctx": 1 - self.c}
+                ).wait_recv()
+                self.over_x(ch).wait_send()
             for d in range(self.n):
-                if self.n == 4 and d in (0, 3):
+                if self.relays and d in (0, 3):
                     @pl.when(self.z == 3 - d)
                     def _():
                         self.to_relay(d, ch).wait_send()
 
-                    @pl.when(self.z == (1 if d == 0 else 2))
+                    @pl.when(self.z == (2 if d == 0 else 1))
                     def _():
                         self.relayed(d, ch).wait_send()
 
@@ -613,14 +609,69 @@
                     self.direct(d, ch).wait_send()
 
 
+class CtxAdd(Job):
+    uses_ctx = True
+
+    def __init__(self, rows, hook, source=None):
+        self.hook, self.source = hook, source
+        self.ins = [] if source else [(rows, VMEM_SPEC)]
+        self.outs = [(jax.ShapeDtypeStruct(rows.shape, BF16), VMEM_SPEC)]
+        self.rows = rows.shape[0]
+        self.ch = chunks_of(self.rows)
+        self.scratch = [VMEM(rows.shape, BF16), DMA((self.ch,)), DMA((self.ch,))]
+
+    def refs(self, ins, outs, scratch):
+        self.src = self.source.out if self.source else ins[0]
+        (self.out,) = outs
+        self.got, self.ssem, self.rsem = scratch
+        if self.source:
+            self.source.then = self.send
+
+    def cut(self, ref, ch):
+        size = self.rows // self.ch
+        return ref.at[pl.ds(ch * size, size)]
+
+    def copy(self, ch):
+        return remote(
+            self.cut(self.src, ch), self.cut(self.got, ch), self.ssem.at[ch], self.rsem.at[ch],
+            {"ctx": 1 - self.c},
+        )
+
+    def send(self, ch):
+        self.copy(ch).start()
+
+    def start(self):
+        if not self.source:
+            for ch in range(self.ch):
+                self.send(ch)
+
+    def add(self):
+        for ch in range(self.ch):
+            self.copy(ch).wait_recv()
+            mine, theirs = self.cut(self.src, ch)[...], self.cut(self.got, ch)[...]
+            self.cut(self.out, ch)[...] = (mine.astype(F32) + theirs.astype(F32)).astype(BF16)
+
+    def steps(self):
+        return [(self.hook, self.add)]
+
+    def end(self):
+        for ch in range(self.ch):
+            self.copy(ch).wait_send()
+
+
 class Background:
     def __init__(self, jobs):
         self.jobs = jobs
-        self.todo = [step for job in jobs for step in job.steps()]
+        self.todo = []
+        for job in jobs:
+            if job.start_hook is not None:
+                self.todo.append((job.start_hook, job.start))
+            self.todo += job.steps()
 
     def start(self):
         for job in self.jobs:
-            job.start()
+            if job.start_hook is None:
+                job.start()
 
     def at(self, hook):
         for when, function in self.todo:
@@ -679,30 +730,42 @@
     return block.reshape(block.shape[0] * block.shape[1], block.shape[2])
 
 
-def gather_start(links, base, out, s):
-    links.make(base, s, out.at[2 + s, 0], out.at[2 + s, 1], links.sib).start()
-    links.make(base + 1, s, out.at[2 + s, 0], out.at[s, 0], links.peer).start()
-
-
-def gather_forward(links, base, out):
-    for s in range(2):
-        links.make(base + 1, s, out.at[2 + s, 0], out.at[s, 0], links.peer).wait_recv()
-        links.make(base + 2, s, out.at[s, 0], out.at[s, 1], links.sib).start()
-
-
-def gather_wait(links, base, out):
-    for s in range(2):
-        for kind, src, dst, other in (
-            (base, out.at[2 + s, 0], out.at[2 + s, 1], links.sib),
-            (base + 2, out.at[s, 0], out.at[s, 1], links.sib),
-        ):
-            links.make(kind, s, src, dst, other).wait()
-        links.make(base + 1, s, out.at[2 + s, 0], out.at[s, 0], links.peer).wait_send()
-
-
-def gather_end(links, base, out):
-    gather_forward(links, base, out)
-    gather_wait(links, base, out)
+class Gather:
+    def __init__(self, links, out):
+        self.links, self.out = links, out
+
+    def near(self, s):
+        return self.links.make(3, s, self.out.at[2 + s, 0], self.out.at[2 + s, 1], self.links.sib)
+
+    def across(self, s):
+        return self.links.make(4, s, self.out.at[2 + s, 0], self.out.at[s, 0], self.links.peer)
+
+    def onward(self, s):
+        return self.links.make(5, s, self.out.at[s, 0], self.out.at[s, 1], self.links.sib)
+
+    def start(self, rows):
+        for s in range(2):
+            self.out[2 + s, 0] = rows(s)
+            self.near(s).start()
+            self.across(s).start()
+
+    def need(self, b):
+        s = b % 2
+
+        @pl.when(b >= 2)
+        def _():
+            self.near(s).wait_recv()
+
+        @pl.when(b < 2)
+        def _():
+            self.across(s).wait_recv()
+            self.onward(s).start()
+            self.onward(s).wait_recv()
+
+    def end(self):
+        for s in range(2):
+            for copy in (self.near(s), self.across(s), self.onward(s)):
+                copy.wait_send()
 
 
 class Scatter:
@@ -754,27 +817,24 @@
     ]
 
 
-def enter_kernel(jobs, first, send, recv):
-    t, sib, peer = partners()
+def enter_kernel(jobs, first):
     params, tokens, attn, expand = jobs
-    entry_barrier(jobs)
-    links = Links(send, recv, sib, peer)
+    entry_barrier(jobs, False)
     tokens.start()
+    params.start()
     attn.start()
-    params.start()
+    params.finish()
+    attn.relay()
     expand.start()
-    params.finish()
     tokens.end()
     for s in range(2):
         unit, _ = statistics(tokens.out[s].astype(F32))
-        first[2 + s, 0] = (unit * params.out[0:1, :] + params.out[1:2, :]).astype(BF16)
-        gather_start(links, 0, first, s)
-    attn.relay()
-    for off in attn.sources():
+        first[s] = (unit * params.out[0:1, :] + params.out[1:2, :]).astype(BF16)
+    for off in attn.sources()[:4]:
         attn.take(off)
     expand.relay()
-    gather_forward(links, 0, first)
-    gather_wait(links, 0, first)
+    for off in attn.sources()[4:]:
+        attn.take(off)
     for job in (params, attn, expand):
         job.end()
 
@@ -786,8 +846,8 @@
 
 def attention_kernel(
     jobs, heads, base,
-    first, params, key_extra, resid, near, far,
-    second, middle, q_out, k_out, v_out, mixed_out,
+    own_first, params, key_extra, resid, near, far,
+    first, second, middle, q_out, k_out, v_out, mixed_out,
     part, sent, got, own, send, recv, weight, load,
 ):
     t, sib, peer = partners()
@@ -797,6 +857,8 @@
     links = Links(send, recv, sib, peer)
     scatter = Scatter(links, part, sent, got, own)
     width = heads * HD
+    gather = Gather(links, first)
+    gather.start(lambda s: own_first[s])
     loads = Loads(load)
     loads.add(near, far, weight)
     loads.wait()
@@ -811,7 +873,9 @@
     q_extra = jnp.where(lane < HD + 2, 1.0, 0.0).astype(BF16)
     v_extra = jnp.where(lane < HD + 3, 1.0, 0.0).astype(BF16)
 
-    def project(b, carry):
+    def project(j, carry):
+        b = (j + 2) % 4
+        gather.need(b)
         x = rows_of(first, b)
         y = mm(x, weight[:, : 3 * width])
         q = ((y[:, :width] + q_bias).astype(BF16) * SCALE).astype(BF16)
@@ -827,6 +891,7 @@
             q_out[h, at, :] = jnp.where(head_lane, pair_tile(q[:, cut], h), q_extra)
             k_out[h, at, :] = jnp.where(head_lane, pair_tile(k[:, cut], h), extra)
             v_out[h, at, :] = jnp.where(head_lane, pair_tile(v[:, cut], h), v_extra)
+        background.loop(j, 4, 20)
         return carry
 
     lax.fori_loop(0, 4, project, 0)
@@ -868,20 +933,17 @@
         mid = resid[s].astype(F32) + (scatter.total(s) + out_bias)
         middle[s] = mid
         unit, _ = statistics(mid)
-        second[2 + s, 0] = (unit * gain + shift).astype(BF16)
-        gather_start(links, 3, second, s)
+        second[s] = (unit * gain + shift).astype(BF16)
         background.at(5 + s)
-    gather_forward(links, 3, second)
-    background.at(7)
-    gather_wait(links, 3, second)
+    gather.end()
     scatter.end()
     background.end()
 
 
 def mlp_kernel(
     jobs, last, base,
-    second, params, middle, near_e, far_e, near_r, far_r,
-    active_out, slope_out, resid, nxt,
+    own_second, params, middle, near_e, far_e, near_r, far_r,
+    second, active_out, slope_out, resid, nxt,
     part, sent, got, own, send, recv, expand, reduce, load,
 ):
     t, sib, peer = partners()
@@ -892,6 +954,8 @@
     scatter = Scatter(links, part, sent, got, own)
     half = second.shape[2]
     rows = 2 * half
+    gather = Gather(links, second)
+    gather.start(lambda s: own_second[s])
     loads = Loads(load)
     loads.add(near_e, far_e, expand)
     loads.add(near_r, far_r, reduce)
@@ -903,7 +967,9 @@
     gain, shift = (params[following + k : following + k + 1, :] for k in (0, 1))
     step = 256
 
-    def block(b, carry):
+    def block(j, carry):
+        b = (j + 2) % 4
+        gather.need(b)
         at = pl.ds(pl.multiple_of(b * rows, rows), rows)
         x = rows_of(second, b)
         for n in range(0, hidden, step):
@@ -914,7 +980,7 @@
             slope_out[at, n : n + step] = slope.astype(BF16)
         part[...] = mm_nt(active_out[at, :], reduce[...])
         scatter.block(b)
-        background.loop(b, 4, 1)
+        background.loop(j, 4, 1)
         return carry
 
     lax.fori_loop(0, 4, block, 0)
@@ -925,19 +991,14 @@
         else:
             resid[s] = res
             unit, _ = statistics(res)
-            nxt[2 + s, 0] = (unit * gain + shift).astype(BF16)
-            gather_start(links, 3, nxt, s)
+            nxt[s] = (unit * gain + shift).astype(BF16)
         background.at(5 + s)
-    if not last:
-        gather_forward(links, 3, nxt)
-    background.at(7)
-    if not last:
-        gather_wait(links, 3, nxt)
+    gather.end()
     scatter.end()
     background.end()
 
 
-def token_product(left, right, out, offset=0):
+def token_product(left, right, outs, offset=0):
     depth = left.shape[-1]
     total = left.shape[0] * left.shape[1] * left.shape[2]
     step = 256
@@ -945,7 +1006,10 @@
     def body(j, carry):
         cut = pl.ds(pl.multiple_of(j * step, step), step)
         x = left[:, :, :, cut].reshape(total, step)
-        out[cut, offset : offset + right.shape[-1]] = mm_tn(x, right[...]).astype(BF16)
+        product = mm_tn(x, right[...]).astype(BF16)
+        width = right.shape[-1] // len(outs)
+        for k, out in enumerate(outs):
+            out[cut, offset : offset + width] = product[:, k * width : (k + 1) * width]
         return carry
 
     lax.fori_loop(0, depth // step, body, 0)
@@ -953,9 +1017,9 @@
 
 def mlp_back_kernel(
     jobs, base,
-    grad, active, slope, second, middle, carry_in, params, near_e, far_e, near_r, far_r,
-    expand_grad, reduce_grad, carry_out, rows_out, vectors,
-    part, sent, got, own, send, recv, d_before, expand, reduce, load,
+    active, slope, second, middle, carry_in, params, near_e, far_e, near_r, far_r,
+    expand_grad, reduce_left, reduce_right, carry_out, vectors,
+    part, sent, got, own, send, recv, grad, d_before, expand, reduce, load,
 ):
     t, sib, peer = partners()
     background = Background(jobs)
@@ -963,6 +1027,8 @@
     background.start()
     links = Links(send, recv, sib, peer)
     scatter = Scatter(links, part, sent, got, own)
+    gather = Gather(links, grad)
+    gather.start(lambda s: carry_in[s].astype(BF16))
     loads = Loads(load)
     loads.add(near_e, far_e, expand)
     loads.add(near_r, far_r, reduce)
@@ -975,7 +1041,9 @@
     step = 256
     vectors[...] = jnp.zeros_like(vectors)
 
-    def block(b, carry):
+    def block(j, carry):
+        b = (j + 2) % 4
+        gather.need(b)
         at = pl.ds(pl.multiple_of(b * rows, rows), rows)
         x = rows_of(grad, b)
         for n in range(0, hidden, step):
@@ -985,11 +1053,11 @@
             vectors[4:5, n : n + step] += jnp.sum(d_bef.astype(F32), axis=0, keepdims=True)
         part[...] = mm_nt(d_before[at, :], expand[...])
         scatter.block(b)
-        background.loop(b)
+        background.loop(j)
         return carry
 
     lax.fori_loop(0, 4, block, 0)
-    token_product(grad, active, reduce_grad)
+    token_product(grad, active, (reduce_left, reduce_right))
     background.at(4)
 
     def finish(s):
@@ -998,8 +1066,6 @@
         mid = carry + back
         carry_out[s] = mid
         low = mid.astype(BF16)
-        rows_out[2 + s, 0] = low
-        gather_start(links, 3, rows_out, s)
         vectors[0:1, :] += d_gain
         vectors[1:2, :] += d_shift
         vectors[2:3, :] += jnp.sum(low.astype(F32), axis=0, keepdims=True)
@@ -1007,20 +1073,19 @@
 
     finish(0)
     background.at(5)
-    token_product(second, d_before, expand_grad)
+    token_product(second, d_before, (expand_grad,))
     finish(1)
-    gather_forward(links, 3, rows_out)
     background.at(6)
-    gather_wait(links, 3, rows_out)
+    gather.end()
     scatter.end()
     background.end()
 
 
 def attention_back_kernel(
-    jobs, heads, last, base,
-    grad, mixed, q_in, k_in, v_in, first, carry_in, resid, params, near, far,
-    weight_grad, carry_out, rows_out, vectors,
-    part, sent, got, own, send, recv, d_joint, d_key, d_value, weight, load,
+    jobs, heads, base,
+    mixed, q_in, k_in, v_in, first, carry_in, resid, params, near, far,
+    weight_grad, carry_out, vectors,
+    part, sent, got, own, send, recv, grad, d_joint, d_key, d_value, weight, load,
 ):
     t, sib, peer = partners()
     background = Background(jobs)
@@ -1029,6 +1094,8 @@
     links = Links(send, recv, sib, peer)
     scatter = Scatter(links, part, sent, got, own)
     width = heads * HD
+    gather = Gather(links, grad)
+    gather.start(lambda s: carry_in[s].astype(BF16))
     loads = Loads(load)
     loads.add(near, far, weight)
     loads.wait()
@@ -1051,7 +1118,9 @@
             axis=1,
         )
 
-    def attend(b, carry):
+    def attend(j, carry):
+        b = (j + 2) % 4
+        gather.need(b)
         at = pl.ds(pl.multiple_of(b * rows, rows), rows)
         d_mixed = mm(rows_of(grad, b), weight[:, 3 * width :]).astype(BF16)
         product = d_mixed.astype(F32) * mixed[at, :].astype(F32)
@@ -1077,7 +1146,7 @@
             d_key[h] += mm(d_raw, q)
             d_queries.append(mm_tn(d_raw, k_in[h]) * SCALE)
         d_joint[at, :width] = pairs(d_queries).astype(BF16)
-        background.loop(b)
+        background.loop(j)
         return carry
 
     lax.fori_loop(0, 4, attend, 0)
@@ -1096,36 +1165,28 @@
         return carry
 
     lax.fori_loop(0, 4, project, 0)
-    token_product(grad, mixed, weight_grad, 3 * width)
+    token_product(grad, mixed, (weight_grad,), 3 * width)
     background.at(8)
 
     def finish(s):
         back, d_gain, d_shift = norm_back(resid[s].astype(F32), scatter.total(s), gain)
         carry = carry_in[s] + back
-        if last:
-            rows_out[s] = carry.astype(BF16)
-        else:
-            carry_out[s] = carry
-            rows_out[2 + s, 0] = carry.astype(BF16)
-            gather_start(links, 3, rows_out, s)
+        carry_out[s] = carry.astype(carry_out.dtype)
         vectors[0:1, :] += d_gain
         vectors[1:2, :] += d_shift
 
     finish(0)
     background.at(9)
-    token_product(first, d_joint, weight_grad, 0)
+    token_product(first, d_joint, (weight_grad,))
     finish(1)
-    if not last:
-        gather_forward(links, 3, rows_out)
     background.at(10)
-    if not last:
-        gather_wait(links, 3, rows_out)
+    gather.end()
     scatter.end()
     background.end()
 
 
 class VectorSum(Job):
-    uses_ctx = uses_fsdp = True
+    uses_tp = uses_ctx = uses_fsdp = True
 
     def __init__(self, vectors, n, hooks):
         self.n, self.hooks = n, hooks
@@ -1193,43 +1254,56 @@
 
 
 def leave_kernel(jobs):
-    attn_ctx, attn_fsdp, reduce_fsdp, vectors, rows = jobs
-    entry_barrier(jobs)
+    attn_ctx, attn_fsdp, left, right, right_ctx, vectors, rows, former = jobs
+    entry_barrier(jobs, False)
     attn_ctx.start()
-    reduce_fsdp.start()
+    left.start()
+    right.start()
     vectors.start()
     rows.start()
+    former.start()
     vectors.fold(0)
-    for i, k in enumerate(attn_ctx.order()):
+    left.relay()
+    order = list(attn_ctx.order())
+    for i, k in enumerate(order):
         attn_ctx.add(k)
-        attn_fsdp.send(k)
+        if i == 1:
+            right.relay()
+            for j in order[:2]:
+                attn_fsdp.send(j)
+        elif i > 1:
+            attn_fsdp.send(k)
         if i in (1, 2):
             vectors.fold(i)
-        if i == 1:
-            reduce_fsdp.relay()
+    left.total()
     attn_fsdp.relay()
-    reduce_fsdp.total()
+    right.total()
     vectors.finish()
+    former.add()
     attn_fsdp.total()
+    right_ctx.add()
     for job in jobs:
         job.end()
 
 
 def finish_kernel(
-    attn_0, attn_1, expand_0, expand_1, reduce_0, reduce_1, vectors,
+    attn_0, attn_1, expand_0, expand_1, left_0, left_1, right_0, right_1, vectors,
     joint, out, expand, reduce, wide, query, value, hidden,
 ):
     z = lax.axis_index("fsdp")
     half = attn_0.shape[1]
     width = joint.shape[3]
     shard = 2 * half
-    for l, (a, e, r) in enumerate(((attn_0, expand_0, reduce_0), (attn_1, expand_1, reduce_1))):
+    layers = ((attn_0, expand_0, left_0, right_0), (attn_1, expand_1, left_1, right_1))
+    for l, (a, e, left, right) in enumerate(layers):
         rows = a[...].reshape(shard, a.shape[2]).astype(F32)
         for k in range(3):
             joint[l, k] = rows[:, k * width : (k + 1) * width]
         out[l] = rows[:, 3 * width :].T
         expand[l] = e[...].reshape(shard, e.shape[2]).astype(F32)
-        reduce[l] = r[...].reshape(shard, r.shape[2]).astype(F32).T
+        part = left.shape[-1]
+        for k, r in enumerate((left, right)):
+            reduce[l, k * part : (k + 1) * part, :] = r[...].reshape(shard, part).astype(F32).T
     cut = query.shape[2]
     heads = query.shape[1]
     dim = vectors.shape[1]
@@ -1327,6 +1401,7 @@
     tiny = jax.ShapeDtypeStruct((8, LANES), F32)
     vec = jax.ShapeDtypeStruct((8, dim), F32)
     square = jax.ShapeDtypeStruct((dim, hidden), BF16)
+    narrow = jax.ShapeDtypeStruct((dim, hidden // 2), BF16)
     count = 8 * half
     n = fsdp_size
     scratch = scatter_scratch(half, dim)
@@ -1346,115 +1421,122 @@
         OverFsdp(attn_w, 0, n, None, 2, (0, 0, 0)),
         OverFsdp(expand_weight, 0, n, None),
     ]
-    first, params, tok, near_a, far_a, near_e = call(
-        enter_kernel, "enter", [every], [DMA((3, 2)), DMA((3, 2))], 0, 10**7, [], jobs
+    rows, params, tok, near_a, far_a, near_e = call(
+        enter_kernel, "enter", [own_low], [], 0, 10**7, [], jobs
     )
     resid = tok
     saved = []
     for l in range(LAYERS):
         last = l == LAYERS - 1
         heads_shape = jax.ShapeDtypeStruct((heads, count, LANES), BF16)
-        if last:
-            jobs = [
-                OverCtx(expand_weight, l, near_e, n), OverCtx(reduce_w, l, near_r, n), RowGather(cot, 1)
-            ]
-        else:
-            jobs = [
-                OverCtx(expand_weight, l, near_e, n),
-                OverFsdp(reduce_w, l, n, 1, 1, (2, 3, 3)),
-                OverFsdp(attn_w, l + 1, n, 4),
-            ]
-        second, middle, q, k, v, mixed, far_e, *more = call(
+        jobs = [
+            OverCtx(expand_weight, l, near_e, n),
+            OverFsdp(reduce_w, l, n, 22, 1, (23, 0, 1)),
+        ]
+        if not last:
+            jobs.append(OverFsdp(attn_w, l + 1, n, 3).after(22))
+        first, rows, middle, q, k, v, mixed, *more = call(
             lambda jobs, *refs, base=8 * l: attention_kernel(jobs, heads, base, *refs),
             f"attention_{l}",
-            [every, own, heads_shape, heads_shape, heads_shape, jax.ShapeDtypeStruct((count, width), BF16)],
+            [every, own_low, own, heads_shape, heads_shape, heads_shape,
+             jax.ShapeDtypeStruct((count, width), BF16)],
             scratch + attn_scratch, 1 + 6 * l,
             2 * count * dim * 4 * width + 16 * heads * count * count * HD,
-            [first, params, key_extra, resid, (near_a, far_a)], jobs,
+            [rows, params, key_extra, resid, (near_a, far_a)], jobs,
         )
         attn_pair = (near_a, far_a)
-        if last:
-            far_r, grad = more
-        else:
-            near_r, far_r, near_a = more
+        far_e, near_r, far_r, *more = more
+        if not last:
+            (near_a,) = more
         mlp_pairs = ((near_e, far_e), (near_r, far_r))
         rows_hidden = jax.ShapeDtypeStruct((count, hidden), BF16)
-        jobs = [] if last else [
-            OverCtx(attn_w, l + 1, near_a, n),
-            OverFsdp(expand_weight, l + 1, n, 3),
-            OverFsdp(reduce_w, l + 1, n, 6),
-            Exchange(cotangent),
+        jobs = [Exchange(cotangent)] if last else [
+            OverCtx(attn_w, l + 1, near_a, n), OverFsdp(expand_weight, l + 1, n, 3),
         ]
-        active, slope, out, nxt, *more = call(
+        second, active, slope, out, rows, *more = call(
             lambda jobs, *refs, base=8 * l, last=last: mlp_kernel(jobs, last, base, *refs),
             f"mlp_{l}",
-            [rows_hidden, rows_hidden, tiny if last else own, own_low if last else every],
+            [every, rows_hidden, rows_hidden, tiny if last else own, own_low],
             scratch + mlp_scratch, 2 + 6 * l, 4 * count * dim * hidden,
-            [second, params, middle, *mlp_pairs], jobs,
+            [rows, params, middle, *mlp_pairs], jobs,
         )
         saved.append((resid, first, q, k, v, mixed, middle, second, active, slope, attn_pair, mlp_pairs))
-        resid, first = out, nxt
-        if not last:
-            far_a, near_e, near_r, cot = more
+        resid = out
+        if last:
+            (cot,) = more
+        else:
+            far_a, near_e = more
 
     carry = cot
-    attn_grads, expand_grads, reduce_grads, attn_vec, mlp_vec = ([None] * LAYERS for _ in range(5))
+    attn_grads, expand_grads, left_grads, right_grads, attn_vec, mlp_vec = (
+        [None] * LAYERS for _ in range(6)
+    )
     for l in reversed(range(LAYERS)):
         (resid, first, q, k, v, mixed, middle, second, active, slope, attn_pair, mlp_pairs) = saved[l]
         last = l == 0
         if last:
             jobs = [
-                FsdpSum(expand_part, n, (3, 5)), FsdpSum(reduce_part, n, (5, 6)),
-                CtxSum(attn_full, n, (1, 3, 4, 5)),
+                CtxSum(attn_full, n, (6, 6, 6, 6)), FsdpSum(expand_part, n, (2, 4)),
+                FsdpSum(left_part, n, (4, 5)).after(2),
             ]
         else:
-            jobs = [Exchange(nxt)]
-        expand_full, reduce_full, carry, grad, mlp_vec[l], *more = call(
+            jobs = [Exchange(rows)]
+        expand_full, left_full, right_full, carry, mlp_vec[l], *more = call(
             lambda jobs, *refs, base=8 * l: mlp_back_kernel(jobs, base, *refs),
             f"mlp_back_{l}",
-            [square, square, own, every, vec],
-            scratch + [VMEM((count, hidden), BF16)] + mlp_scratch, 3 + 6 * l, 8 * count * dim * hidden,
-            [grad, active, slope, second, middle, carry, params, *mlp_pairs], jobs,
+            [square, narrow, narrow, own, vec],
+            scratch + [VMEM(every.shape, BF16), VMEM((count, hidden), BF16)] + mlp_scratch, 3 + 6 * l, 8 * count * dim * hidden,
+            [active, slope, second, middle, carry, params, *mlp_pairs], jobs,
         )
         if last:
-            expand_grads[l + 1], reduce_grads[l + 1], attn_part = more
-            ctx_job = CtxSum(expand_full, n, (0, 1, 2, 3), keep=True)
+            attn_part, expand_grads[l + 1], left_grads[l + 1] = more
+            ctx_job = CtxSum(expand_full, n, (1, 2, 3, 4), keep=True)
             jobs = [
-                ctx_job, FsdpSum(expand_shape, n, (7, 9), source=ctx_job, sends=(0, 1, 2, 3)),
-                CtxSum(reduce_full, n, (5, 7, 9, 10)), FsdpSum(attn_part, n, (2, 3)),
+                FsdpSum(attn_part, n, (1, 4)), ctx_job,
+                FsdpSum(expand_shape, n, (5, 9), source=ctx_job, sends=(1, 2, 3, 4)),
+                CtxSum(left_full, n, (10, 10, 10, 10)),
             ]
         else:
             (output,) = more
-            jobs = [CtxSum(expand_full, n, (0, 1, 2, 3)), CtxSum(reduce_full, n, (4, 7, 8, 10))]
-        attn_full, carry, grad, attn_vec[l], *more = call(
-            lambda jobs, *refs, base=8 * l, last=last: attention_back_kernel(jobs, heads, last, base, *refs),
+            jobs = [
+                CtxSum(expand_full, n, (5, 6, 7, 8)), CtxSum(left_full, n, (10, 10, 10, 10)),
+                FsdpSum(right_full.reshape(n, shard, -1), n, (1, 10), spread=False),
+            ]
+        attn_full, carry, attn_vec[l], *more = call(
+            lambda jobs, *refs, base=8 * l: attention_back_kernel(jobs, heads, base, *refs),
             f"attention_back_{l}",
-            [jax.ShapeDtypeStruct((dim, 4 * width), BF16), tiny if last else own, own_low if last else every, vec],
+            [jax.ShapeDtypeStruct((dim, 4 * width), BF16), own_low if last else own, vec],
             scratch
             + [
+                VMEM(every.shape, BF16),
                 VMEM((count, 3 * width), BF16),
                 VMEM((heads, count, LANES), F32),
                 VMEM((heads, count, LANES), F32),
             ]
             + attn_scratch,
             4 + 6 * l, 4 * count * dim * 4 * width + 40 * heads * count * count * HD,
-            [grad, mixed, q, k, v, first, carry, resid, params, attn_pair], jobs,
+            [mixed, q, k, v, first, carry, resid, params, attn_pair], jobs,
         )
         if last:
-            expand_grads[l], reduce_part, attn_grads[l + 1] = more
+            attn_grads[l + 1], expand_grads[l], left_part = more
         else:
-            expand_part, reduce_part = more
+            expand_part, left_part, right_part = more
             expand_shape = jax.ShapeDtypeStruct(expand_part.shape, BF16)
 
     ctx_job = CtxSum(attn_full, n, (0, 1, 2, 3), keep=True)
+    attn_shape = jax.ShapeDtypeStruct((n, shard // 2, 4 * width), BF16)
+    right_job = FsdpSum(right_full.reshape(n, shard, -1), n, (0, 1), spread=False)
     jobs = [
         ctx_job,
-        FsdpSum(jax.ShapeDtypeStruct((n, shard // 2, 4 * width), BF16), n, (0, 1), source=ctx_job),
-        FsdpSum(reduce_part, n, (0, 1)),
+        FsdpSum(attn_shape, n, (0, 1), source=ctx_job),
+        FsdpSum(left_part, n, (0, 1)),
+        right_job,
+        CtxAdd(right_part, 0, source=right_job),
         VectorSum([attn_vec[0], mlp_vec[0], attn_vec[1], mlp_vec[1]], n, (0, 1, 2, 3)),
-        Exchange(grad),
+        Exchange(carry),
+        CtxAdd(right_part, 0),
     ]
-    attn_grads[0], reduce_grads[0], vectors, row_grad = call(
+    attn_grads[0], left_grads[0], _, right_grads[0], vectors, row_grad, right_grads[1] = call(
         leave_kernel, "leave", [], [], 5, 10**7, [], jobs
     )
     results = [
@@ -1469,10 +1551,10 @@
         finish_kernel,
         name="finish",
         out_shape=tuple(results),
-        in_specs=[VMEM_SPEC] * 7,
+        in_specs=[VMEM_SPEC] * 9,
         out_specs=tuple([VMEM_SPEC] * 8),
         compiler_params=pltpu.CompilerParams(vmem_limit_bytes=VMEM_LIMIT),
-    )(*attn_grads, *expand_grads, *reduce_grads, vectors)
+    )(*attn_grads, *expand_grads, *left_grads, *right_grads, vectors)
     return (
         output, row_grad, wide[0], wide[1], joint.transpose(0, 2, 1, 3), query, value, out,
         wide[2], wide[3], wide[4], expand, hidden_bias, reduce, wide[5],

time: 534 us -> 476 us (0.89)
  the two profiles are of different devices: /device:TPU:0 before, /device:TPU:24 now
where the time goes in v4:
time: 476 us; the launch traced here: 468 us
  Pallas kernels  457 us (96%)
  local copies, waits for them, and re-layouts  5.36 us (1%)
    pallas_call x10, Pallas kernels, call(): pl.pallas_call(body, name=name, out_shape=tuple((o for o, _ in results)),...  452 us

profile of v4, /device:TPU:24, one launch (start us, length us, event | category | flops | bytes accessed | tf_op | source)
XLA Modules:
  0.0 467.8 jit_solution(6424537137909437751)
XLA Ops:
  0.6 0.0 copy-start
  0.7 0.8 compare_select_fusion
  1.5 1.0 select_convert_fusion.refs_2_
  2.5 1.1 copy.31
  3.6 2.2 pad_maximum_fusion.refs_10_.refs_9_.refs_7_
  5.8 0.0 copy-done
  5.8 1.3 copy.33
  7.1 42.6 %enter.1 = (bf16[2,128,1024]{2,1,0:T(8,128)(2,1)}, f32[16,1024]{1,0:T(8,128)}, bf16[2,128,1024]{2,1,0:T(8,128)(2,1)}, bf16[4,4,128,256]{3,2,1,0:T(8,128)(2,1)}, ...) custom-call(bf16[2,256]{1,0:T(2,128)(2,1)} %refs_0_.1, bf16[2,256]{1,0:T(2,128)(2,1)} %refs_1_.1, ...), custom_call_target="tpu_custom_call" | custom-call | flops 10000000 | bytes 6888960 | tf_op jit(solution)/shard_map/enter/pallas_call | solution.py:1355
  49.7 52.2 %attention_0.1 = (bf16[4,2,128,1024]{3,2,1,0:T(8,128)(2,1)}, bf16[2,128,1024]{2,1,0:T(8,128)(2,1)}, f32[2,128,1024]{2,1,0:T(8,128)}, bf16[4,1024,128]{2,1,0:T(8,...) custom-call(bf16[2,128,1024]{2,1,0:T(8,128)(2,1)} %get-tuple-element, ...), custom_call_target="tpu_custom_call" | custom-call | flops 6442450944 | bytes 19202048 | tf_op jit(solution)/shard_map/attention_0/pallas_call | solution.py:1355
  102.0 31.4 %mlp_0.1 = (bf16[4,2,128,1024]{3,2,1,0:T(8,128)(2,1)}, bf16[1024,1024]{1,0:T(8,128)(2,1)}, bf16[1024,1024]{1,0:T(8,128)(2,1)}, f32[2,128,1024]{2,1,0:T(8,128)}, ...) custom-call(bf16[2,128,1024]{2,1,0:T(8,128)(2,1)} %get-tuple-element.100.refs_0_, ...), custom_call_target="tpu_custom_call" | custom-call | flops 4294967296 | bytes 18939904 | tf_op jit(solution)/shard_map/mlp_0/pallas_call | solution.py:1355
  133.4 40.9 %attention_1.1 = (bf16[4,2,128,1024]{3,2,1,0:T(8,128)(2,1)}, bf16[2,128,1024]{2,1,0:T(8,128)(2,1)}, f32[2,128,1024]{2,1,0:T(8,128)}, bf16[4,1024,128]{2,1,0:T(8,...) custom-call(bf16[2,128,1024]{2,1,0:T(8,128)(2,1)} %get-tuple-element, ...), custom_call_target="tpu_custom_call" | custom-call | flops 6442450944 | bytes 17629184 | tf_op jit(solution)/shard_map/attention_1/pallas_call | solution.py:1355
  174.3 31.8 %mlp_1.1 = (bf16[4,2,128,1024]{3,2,1,0:T(8,128)(2,1)}, bf16[1024,1024]{1,0:T(8,128)(2,1)}, bf16[1024,1024]{1,0:T(8,128)(2,1)}, f32[8,128]{1,0:T(8,128)}, bf16[2,...) custom-call(bf16[2,128,1024]{2,1,0:T(8,128)(2,1)} %get-tuple-element.110.refs_0_, ...), custom_call_target="tpu_custom_call" | custom-call | flops 4294967296 | bytes 13701120 | tf_op jit(solution)/shard_map/mlp_1/pallas_call | solution.py:1355
  206.2 32.6 %mlp_back_1.1 = (bf16[1024,1024]{1,0:T(8,128)(2,1)}, bf16[1024,512]{1,0:T(8,128)(2,1)}, bf16[1024,512]{1,0:T(8,128)(2,1)}, f32[2,128,1024]{2,1,0:T(8,128)}, f32[...) custom-call(bf16[1024,1024]{1,0:T(8,128)(2,1)} %get-tuple-element.115.refs_0_, ...), custom_call_target="tpu_custom_call" | custom-call | flops 8589934592 | bytes 18448384 | tf_op jit(solution)/shard_map/mlp_back_1/pallas_call | solution.py:1355
  238.8 42.9 %attention_back_1.1 = (bf16[1024,1024]{1,0:T(8,128)(2,1)}, f32[2,128,1024]{2,1,0:T(8,128)}, f32[8,1024]{1,0:T(8,128)}, bf16[4,128,1024]{2,1,0:T(8,128)(2,1)}, bf...) custom-call(bf16[1024,256]{1,0:T(8,128)(2,1)} %get-tuple-element.129.refs_0_, ...), custom_call_target="tpu_custom_call" | custom-call | flops 15032385536 | bytes 19234816 | tf_op jit(solution)/shard_map/attention_back_1/pallas_call | solution.py:1355
  281.7 55.6 %mlp_back_0.1 = (bf16[1024,1024]{1,0:T(8,128)(2,1)}, bf16[1024,512]{1,0:T(8,128)(2,1)}, bf16[1024,512]{1,0:T(8,128)(2,1)}, f32[2,128,1024]{2,1,0:T(8,128)}, f32[...) custom-call(bf16[1024,1024]{1,0:T(8,128)(2,1)} %get-tuple-element.12, ...), custom_call_target="tpu_custom_call" | custom-call | flops 8589934592 | bytes 23429120 | tf_op jit(solution)/shard_map/mlp_back_0/pallas_call | solution.py:1355
  337.3 55.2 %attention_back_0.1 = (bf16[1024,1024]{1,0:T(8,128)(2,1)}, bf16[2,128,1024]{2,1,0:T(8,128)(2,1)}, f32[8,1024]{1,0:T(8,128)}, bf16[2,128,1024]{2,1,0:T(8,128)(2,1...) custom-call(bf16[1024,256]{1,0:T(8,128)(2,1)} %get-tuple-element.121.refs_0_, ...), custom_call_target="tpu_custom_call" | custom-call | flops 15032385536 | bytes 17924096 | tf_op jit(solution)/shard_map/attention_back_0/pallas_call | solution.py:1355
  392.5 67.1 %leave.1 = (bf16[2,128,1024]{2,1,0:T(8,128)(2,1)}, bf16[2,128,512]{2,1,0:T(8,128)(2,1)}, bf16[256,512]{1,0:T(8,128)(2,1)}, bf16[256,512]{1,0:T(8,128)(2,1)}, f32...) custom-call(bf16[4,2,128,1024]{3,2,1,0:T(8,128)(2,1)} %bitcast.40, ...), custom_call_target="tpu_custom_call" | custom-call | flops 10000000 | bytes 6750208 | tf_op jit(solution)/shard_map/leave/pallas_call | solution.py:1355
  459.7 0.0 copy-start.1
  459.7 0.0 copy-start.2
  459.7 4.9 %finish.1 = (f32[2,3,256,256]{3,2,1,0:T(8,128)}, f32[2,256,256]{2,1,0:T(8,128)}, f32[2,256,1024]{2,1,0:T(8,128)}, f32[2,1024,256]{2,1,0:T(8,128)}, f32[6,2,256]{...) custom-call(bf16[2,128,1024]{2,1,0:T(8,128)(2,1)} %get-tuple-element.156.attn_0, ...), custom_call_target="tpu_custom_call" | custom-call | tf_op jit(solution)/shard_map/finish/pallas_call | solution.py:1550
  464.6 1.4 slice_bitcast_fusion
  466.0 0.0 copy-done.1
  466.0 0.8 copy.43
  466.8 0.0 copy-done.2
  466.8 0.8 copy.44
  (4 shorter events, 0.0 us)
Async XLA Ops:
  0.6 5.2 %copy-start = (bf16[2,1024,256]{2,1,0:T(8,128)(2,1)S(1)}, bf16[2,1024,256]{2,1,0:T(8,128)(2,1)}, u32[]{:S(2)}) copy-start(bf16[2,1024,256]{2,1,0:T(8,128)(2,1)} %param.29) | copy-start | bytes 3145732
  459.7 6.3 %copy-start.1 = (bf16[2,128,1024]{2,1,0:T(8,128)(2,1)S(1)}, bf16[2,128,1024]{2,1,0:T(8,128)(2,1)}, u32[]{:S(2)}) copy-start(bf16[2,128,1024]{2,1,0:T(8,128)(2,1)} %get-tuple-element.196) | copy-start | bytes 1572868
  459.7 7.1 %copy-start.2 = (bf16[2,128,1024]{2,1,0:T(8,128)(2,1)S(1)}, bf16[2,128,1024]{2,1,0:T(8,128)(2,1)}, u32[]{:S(2)}) copy-start(bf16[2,128,1024]{2,1,0:T(8,128)(2,1)} %get-tuple-element.197) | copy-start | bytes 1572868

commit v5 on v4

--- a/solution.py
+++ b/solution.py
@@ -14,7 +14,7 @@
 EPS = 1e-06
 MASKED = -10000.0
 SCALE = HD ** (-0.5)
-VMEM_LIMIT = 60 * 1024 * 1024
+VMEM_LIMIT = 62 * 1024 * 1024
 F32 = jnp.float32
 BF16 = jnp.bfloat16
 VMEM = pltpu.VMEM
@@ -78,6 +78,7 @@
     outs = ()
     scratch = ()
     start_hook = None
+    name = None
 
     def after(self, hook):
         self.start_hook = hook
@@ -392,11 +393,10 @@
 class CtxSum(Job):
     uses_ctx = True
 
-    def __init__(self, full, n, hooks, keep=False):
-        self.n, self.hooks = n, hooks
-        full = full.reshape(n, 2, full.shape[0] // (2 * n), full.shape[1])
-        shape = (n, *full.shape[2:])
-        self.ins = [(full, HBM_SPEC)]
+    def __init__(self, full, n, hooks, keep=False, name=None):
+        self.n, self.hooks, self.name = n, hooks, name
+        shape = (n, full.shape[0] // (2 * n), full.shape[1])
+        self.ins = [] if name else [(full.reshape(n, 2, *shape[1:]), HBM_SPEC)]
         self.keep = keep
         self.outs = [] if keep else [(jax.ShapeDtypeStruct(shape, BF16), VMEM_SPEC)]
         self.scratch = [VMEM(shape, BF16), DMA((n,)), DMA((n,)), DMA((n,))]
@@ -404,9 +404,13 @@
             self.scratch.append(VMEM(shape, BF16))
 
     def refs(self, ins, outs, scratch):
-        (self.full,) = ins
+        if not self.name:
+            (self.full,) = ins
         self.got, self.ssem, self.rsem, self.near = scratch[:4]
         self.out = scratch[4] if self.keep else outs[0]
+
+    def attach(self, ref):
+        self.full = ref.reshape(self.n, 2, ref.shape[0] // (2 * self.n), ref.shape[1])
 
     def order(self):
         return (0, 3, 1, 2) if self.n == 4 else range(self.n)
@@ -424,12 +428,15 @@
         for k in self.order():
             self.copy(k).start()
         for k in self.order():
-            self.load(k).start()
+            if not self.name:
+                self.load(k).start()
 
     def add(self, k):
-        self.load(k).wait()
+        if not self.name:
+            self.load(k).wait()
         self.copy(k).wait_recv()
-        self.out[k] = (self.out[k].astype(F32) + self.got[k].astype(F32)).astype(BF16)
+        mine = self.full[k, self.c] if self.name else self.out[k]
+        self.out[k] = (mine.astype(F32) + self.got[k].astype(F32)).astype(BF16)
 
     def steps(self):
         per = -(-self.n // len(self.hooks))
@@ -446,12 +453,13 @@
 class FsdpSum(Job):
     uses_fsdp = True
 
-    def __init__(self, rows, n, hooks, source=None, sends=(), spread=True, direct=False):
+    def __init__(self, rows, n, hooks, source=None, sends=(), spread=True, direct=False, name=None):
+        self.name = name
         self.n, self.hooks, self.source, self.sends = n, hooks, source, sends
         self.relays = n == 4 and not direct
         self.spread = self.uses_ctx = spread
         shape = rows.shape
-        self.ins = [] if source else [(rows, VMEM_SPEC)]
+        self.ins = [] if source or name else [(rows, VMEM_SPEC)]
         result = (2, *shape[1:]) if spread else shape[1:]
         self.outs = [(jax.ShapeDtypeStruct(result, BF16), VMEM_SPEC)]
         self.rows = shape[1]
@@ -463,10 +471,14 @@
         ]
 
     def refs(self, ins, outs, scratch):
-        self.src = self.source.out if self.source else ins[0]
+        if not self.name:
+            self.src = self.source.out if self.source else ins[0]
         (self.out,) = outs
         (self.got, self.via, self.ssem, self.rsem, self.via_send, self.via_recv, self.x_send,
          self.x_recv) = scratch
+
+    def attach(self, ref):
+        self.src = ref.reshape(self.n, self.rows, ref.shape[1])
 
     def cut(self, ref, ch):
         size = self.rows // self.ch
@@ -667,6 +679,7 @@
             if job.start_hook is not None:
                 self.todo.append((job.start_hook, job.start))
             self.todo += job.steps()
+        self.ended = []
 
     def start(self):
         for job in self.jobs:
@@ -678,16 +691,29 @@
             if when == hook:
                 function()
 
+    def phase(self, tag):
+        return Phase(self, tag)
+
+    def end(self, jobs=None):
+        for job in self.jobs if jobs is None else jobs:
+            if job not in self.ended:
+                self.ended.append(job)
+                job.end()
+
+
+class Phase:
+    def __init__(self, whole, tag):
+        self.whole, self.tag = whole, tag
+
+    def at(self, hook):
+        self.whole.at((self.tag, hook))
+
     def loop(self, b, count=4, base=0):
         for k in range(count):
-            if any(when == base + k for when, _ in self.todo):
+            if any(when == (self.tag, base + k) for when, _ in self.whole.todo):
                 @pl.when(b == k)
                 def _():
                     self.at(base + k)
-
-    def end(self):
-        for job in self.jobs:
-            job.end()
 
 
 class Links:
@@ -807,17 +833,21 @@
 
 
 def scatter_scratch(half, width):
-    return [
-        VMEM((2 * half, width), F32),
-        VMEM((3, 2, half, width), BF16),
-        VMEM((3, 2, half, width), BF16),
-        VMEM((2, half, width), F32),
-        pltpu.SemaphoreType.DMA((6, 2)),
-        pltpu.SemaphoreType.DMA((6, 2)),
+    local = [VMEM((2 * half, width), F32), VMEM((2, half, width), F32)]
+    linked = [
+        VMEM((3, 2, half, width), BF16), VMEM((3, 2, half, width), BF16), DMA((6, 2)), DMA((6, 2))
     ]
-
-
-def enter_kernel(jobs, first):
+    return local + linked + linked
+
+
+def scatter_refs(scratch, phase):
+    part, own = scratch[:2]
+    sent, got, send, recv = scratch[2 + 4 * phase : 6 + 4 * phase]
+    return part, sent, got, own, send, recv
+
+
+def enter_kernel(jobs, refs):
+    first = refs[1][0]
     params, tokens, attn, expand = jobs
     entry_barrier(jobs, False)
     tokens.start()
@@ -844,16 +874,13 @@
     return tile
 
 
-def attention_kernel(
-    jobs, heads, base,
+def attention_phase(
+    background, heads, base,
     own_first, params, key_extra, resid, near, far,
     first, second, middle, q_out, k_out, v_out, mixed_out,
     part, sent, got, own, send, recv, weight, load,
 ):
     t, sib, peer = partners()
-    background = Background(jobs)
-    entry_barrier(jobs)
-    background.start()
     links = Links(send, recv, sib, peer)
     scatter = Scatter(links, part, sent, got, own)
     width = heads * HD
@@ -937,19 +964,15 @@
         background.at(5 + s)
     gather.end()
     scatter.end()
-    background.end()
-
-
-def mlp_kernel(
-    jobs, last, base,
+
+
+def mlp_phase(
+    background, last, base,
     own_second, params, middle, near_e, far_e, near_r, far_r,
     second, active_out, slope_out, resid, nxt,
     part, sent, got, own, send, recv, expand, reduce, load,
 ):
     t, sib, peer = partners()
-    background = Background(jobs)
-    entry_barrier(jobs)
-    background.start()
     links = Links(send, recv, sib, peer)
     scatter = Scatter(links, part, sent, got, own)
     half = second.shape[2]
@@ -995,7 +1018,6 @@
         background.at(5 + s)
     gather.end()
     scatter.end()
-    background.end()
 
 
 def token_product(left, right, outs, offset=0):
@@ -1015,16 +1037,13 @@
     lax.fori_loop(0, depth // step, body, 0)
 
 
-def mlp_back_kernel(
-    jobs, base,
+def mlp_back_phase(
+    background, base,
     active, slope, second, middle, carry_in, params, near_e, far_e, near_r, far_r,
     expand_grad, reduce_left, reduce_right, carry_out, vectors,
     part, sent, got, own, send, recv, grad, d_before, expand, reduce, load,
 ):
     t, sib, peer = partners()
-    background = Background(jobs)
-    entry_barrier(jobs)
-    background.start()
     links = Links(send, recv, sib, peer)
     scatter = Scatter(links, part, sent, got, own)
     gather = Gather(links, grad)
@@ -1078,19 +1097,15 @@
     background.at(6)
     gather.end()
     scatter.end()
-    background.end()
-
-
-def attention_back_kernel(
-    jobs, heads, base,
+
+
+def attention_back_phase(
+    background, heads, base,
     mixed, q_in, k_in, v_in, first, carry_in, resid, params, near, far,
-    weight_grad, carry_out, vectors,
+    carry_out, vectors,
     part, sent, got, own, send, recv, grad, d_joint, d_key, d_value, weight, load,
 ):
     t, sib, peer = partners()
-    background = Background(jobs)
-    entry_barrier(jobs)
-    background.start()
     links = Links(send, recv, sib, peer)
     scatter = Scatter(links, part, sent, got, own)
     width = heads * HD
@@ -1165,7 +1180,7 @@
         return carry
 
     lax.fori_loop(0, 4, project, 0)
-    token_product(grad, mixed, (weight_grad,), 3 * width)
+    token_product(grad, mixed, (weight,), 3 * width)
     background.at(8)
 
     def finish(s):
@@ -1177,12 +1192,68 @@
 
     finish(0)
     background.at(9)
-    token_product(first, d_joint, (weight_grad,))
+    token_product(first, d_joint, (weight,))
     finish(1)
     background.at(10)
     gather.end()
     scatter.end()
+
+
+def forward_kernel(jobs, urgent, heads, last, base, refs):
+    ins, outs, scratch = refs
+    own_first, params, key_extra, resid, near_a, far_a, *near = ins
+    first, own_rows, middle, q, k, v, mixed, second, active, slope, out, rows = outs
+    attn_w, attn_load, expand, reduce, mlp_load = scratch[10:]
+    background = Background(jobs)
+    entry_barrier(jobs)
+    background.start()
+    attention_phase(
+        background.phase("A"), heads, base,
+        own_first, params, key_extra, resid, near_a, far_a,
+        first, own_rows, middle, q, k, v, mixed, *scatter_refs(scratch, 0), attn_w, attn_load,
+    )
+    background.end(urgent)
+    near_e = near[0]
+    near_r = near[1] if len(near) > 1 else urgent[1].near
+    mlp_phase(
+        background.phase("M"), last, base,
+        own_rows, params, middle, near_e, urgent[0].far, near_r, urgent[1].far,
+        second, active, slope, out, rows, *scatter_refs(scratch, 1), expand, reduce, mlp_load,
+    )
     background.end()
+
+
+def backward_kernel(jobs, heads, base, refs):
+    ins, outs, scratch = refs
+    (active, slope, second, middle, carry_in, params, mixed, q, k, v, first, resid,
+     near_e, far_e, near_r, far_r, near_a, far_a) = ins
+    attn_grad, carry_out, mlp_vec, attn_vec = outs
+    (left_grad, right_grad, carry_mid, grad_rows, attn_rows, d_before, expand, reduce,
+     mlp_load, d_joint, d_key, d_value, attn_w, attn_load) = scratch[10:]
+    expand_grad = whole(expand)
+    named = dict(expand=expand_grad, left=left_grad, right=right_grad)
+    for job in jobs:
+        if job.name:
+            job.attach(named[job.name])
+    background = Background(jobs)
+    entry_barrier(jobs)
+    background.start()
+    mlp_back_phase(
+        background.phase("M"), base,
+        active, slope, second, middle, carry_in, params, near_e, far_e, near_r, far_r,
+        expand_grad, left_grad, right_grad, carry_mid, mlp_vec,
+        *scatter_refs(scratch, 0), grad_rows, d_before, expand, reduce, mlp_load,
+    )
+    attention_back_phase(
+        background.phase("A"), heads, base,
+        mixed, q, k, v, first, carry_mid, resid, params, near_a, far_a,
+        carry_out, attn_vec,
+        *scatter_refs(scratch, 1), attn_rows, d_joint, d_key, d_value, attn_w, attn_load,
+    )
+    copy = pltpu.make_async_copy(whole(attn_w), attn_grad, attn_load.at[0])
+    copy.start()
+    background.end()
+    copy.wait()
 
 
 class VectorSum(Job):
@@ -1253,35 +1324,35 @@
             self.copy(k).wait_send()
 
 
-def leave_kernel(jobs):
-    attn_ctx, attn_fsdp, left, right, right_ctx, vectors, rows, former = jobs
+def leave_kernel(jobs, refs):
+    attn_ctx, attn, expand, left, vectors, rows, right = jobs
     entry_barrier(jobs, False)
     attn_ctx.start()
+    expand.start()
+    vectors.start()
+    for job in (rows, right):
+        job.start()
+    order = list(attn_ctx.order())
+    vectors.fold(0)
+    expand.relay()
     left.start()
-    right.start()
-    vectors.start()
-    rows.start()
-    former.start()
-    vectors.fold(0)
+    attn_ctx.add(order[0])
+    attn.send(order[0])
+    vectors.fold(1)
+    attn_ctx.add(order[1])
+    attn.send(order[1])
+    vectors.fold(2)
+    attn_ctx.add(order[2])
+    attn.send(order[2])
     left.relay()
-    order = list(attn_ctx.order())
-    for i, k in enumerate(order):
-        attn_ctx.add(k)
-        if i == 1:
-            right.relay()
-            for j in order[:2]:
-                attn_fsdp.send(j)
-        elif i > 1:
-            attn_fsdp.send(k)
-        if i in (1, 2):
-            vectors.fold(i)
+    expand.total()
+    attn_ctx.add(order[3])
+    attn.send(order[3])
+    attn.relay()
     left.total()
-    attn_fsdp.relay()
-    right.total()
     vectors.finish()
-    former.add()
-    attn_fsdp.total()
-    right_ctx.add()
+    right.add()
+    attn.total()
     for job in jobs:
         job.end()
 
@@ -1329,7 +1400,7 @@
         for a, spec in ([(arg, VMEM_SPEC)] if not isinstance(arg, tuple) else [(a, HBM_SPEC) for a in arg])
     ]
     ins = args + [pair for job in jobs for pair in job.ins]
-    results = [(o, VMEM_SPEC) for o in outs] + [pair for job in jobs for pair in job.outs]
+    results = [o if isinstance(o, tuple) else (o, VMEM_SPEC) for o in outs] + [pair for job in jobs for pair in job.outs]
     scratch = list(scratch)
     n_scratch = len(scratch)
     for job in jobs:
@@ -1345,9 +1416,7 @@
             ends = a + len(job.ins), b + len(job.outs), c + len(job.scratch)
             job.bind(in_refs[a : ends[0]], out_refs[b : ends[1]], scratch_refs[c : ends[2]])
             a, b, c = ends
-        kernel(
-            jobs, *in_refs[: len(args)], *out_refs[: len(outs)], *scratch_refs[:n_scratch]
-        )
+        kernel(jobs, (in_refs[: len(args)], out_refs[: len(outs)], scratch_refs[:n_scratch]))
 
     size = sum(a.size * a.dtype.itemsize for a, _ in ins) + sum(
         math.prod(o.shape) * o.dtype.itemsize for o, _ in results
@@ -1426,119 +1495,113 @@
     )
     resid = tok
     saved = []
+    heads_shape = jax.ShapeDtypeStruct((heads, count, LANES), BF16)
+    rows_width = jax.ShapeDtypeStruct((count, width), BF16)
+    rows_hidden = jax.ShapeDtypeStruct((count, hidden), BF16)
     for l in range(LAYERS):
         last = l == LAYERS - 1
-        heads_shape = jax.ShapeDtypeStruct((heads, count, LANES), BF16)
-        jobs = [
+        urgent = [
             OverCtx(expand_weight, l, near_e, n),
-            OverFsdp(reduce_w, l, n, 22, 1, (23, 0, 1)),
+            OverFsdp(reduce_w, l, n, ("A", 22), 1, (("A", 23), ("A", 0), ("A", 1))),
         ]
-        if not last:
-            jobs.append(OverFsdp(attn_w, l + 1, n, 3).after(22))
-        first, rows, middle, q, k, v, mixed, *more = call(
-            lambda jobs, *refs, base=8 * l: attention_kernel(jobs, heads, base, *refs),
-            f"attention_{l}",
-            [every, own_low, own, heads_shape, heads_shape, heads_shape,
-             jax.ShapeDtypeStruct((count, width), BF16)],
-            scratch + attn_scratch, 1 + 6 * l,
-            2 * count * dim * 4 * width + 16 * heads * count * count * HD,
-            [rows, params, key_extra, resid, (near_a, far_a)], jobs,
+        jobs = list(urgent)
+        if last:
+            jobs.append(Exchange(cotangent).after(("M", 1)))
+        else:
+            jobs += [
+                OverFsdp(attn_w, l + 1, n, ("A", 3), 1, (("A", 4), ("A", 5), ("M", 1))).after(("A", 22)),
+                OverFsdp(expand_weight, l + 1, n, ("M", 2)).after(("A", 5)),
+            ]
+        (first, _, middle, q, k, v, mixed, second, active, slope, out, rows,
+         far_e, near_r, far_r, *more) = call(
+            lambda jobs, refs, base=8 * l, last=last, urgent=urgent: forward_kernel(
+                jobs, urgent, heads, last, base, refs
+            ),
+            f"forward_{l}",
+            [every, own_low, own, heads_shape, heads_shape, heads_shape, rows_width, every,
+             rows_hidden, rows_hidden, tiny if last else own, own_low],
+            scratch + attn_scratch + mlp_scratch, 1 + 2 * l,
+            2 * count * dim * 4 * width + 16 * heads * count * count * HD + 4 * count * dim * hidden,
+            [rows, params, key_extra, resid, (near_a, far_a, near_e)], jobs,
         )
-        attn_pair = (near_a, far_a)
-        far_e, near_r, far_r, *more = more
-        if not last:
-            (near_a,) = more
-        mlp_pairs = ((near_e, far_e), (near_r, far_r))
-        rows_hidden = jax.ShapeDtypeStruct((count, hidden), BF16)
-        jobs = [Exchange(cotangent)] if last else [
-            OverCtx(attn_w, l + 1, near_a, n), OverFsdp(expand_weight, l + 1, n, 3),
-        ]
-        second, active, slope, out, rows, *more = call(
-            lambda jobs, *refs, base=8 * l, last=last: mlp_kernel(jobs, last, base, *refs),
-            f"mlp_{l}",
-            [every, rows_hidden, rows_hidden, tiny if last else own, own_low],
-            scratch + mlp_scratch, 2 + 6 * l, 4 * count * dim * hidden,
-            [rows, params, middle, *mlp_pairs], jobs,
-        )
-        saved.append((resid, first, q, k, v, mixed, middle, second, active, slope, attn_pair, mlp_pairs))
+        weights = (near_e, far_e, near_r, far_r, near_a, far_a)
+        saved.append((resid, first, q, k, v, mixed, middle, second, active, slope, weights))
         resid = out
         if last:
             (cot,) = more
         else:
-            far_a, near_e = more
+            near_a, far_a, near_e = more
 
     carry = cot
     attn_grads, expand_grads, left_grads, right_grads, attn_vec, mlp_vec = (
         [None] * LAYERS for _ in range(6)
     )
     for l in reversed(range(LAYERS)):
-        (resid, first, q, k, v, mixed, middle, second, active, slope, attn_pair, mlp_pairs) = saved[l]
+        resid, first, q, k, v, mixed, middle, second, active, slope, weights = saved[l]
         last = l == 0
+        halves = jax.ShapeDtypeStruct((n, shard, hidden // 2), BF16)
+        made = [
+            CtxSum(narrow, n, (("A", 2),) * 4, name="left").after(("M", 4)),
+            FsdpSum(halves, n, (("A", 1), ("A", 6)), spread=False, name="right").after(("M", 4)),
+            CtxSum(square, n, (("A", 6), ("A", 7), ("A", 8), ("A", 10)), name="expand").after(("M", 6)),
+        ]
         if last:
+            ctx_job = CtxSum(attn_full, n, (("M", 4), ("M", 4), ("M", 5), ("M", 6)), keep=True)
+            attn_shape = jax.ShapeDtypeStruct((n, shard // 2, 4 * width), BF16)
             jobs = [
-                CtxSum(attn_full, n, (6, 6, 6, 6)), FsdpSum(expand_part, n, (2, 4)),
-                FsdpSum(left_part, n, (4, 5)).after(2),
+                FsdpSum(expand_part, n, (("M", 2), ("M", 6))),
+                FsdpSum(left_part, n, (("M", 4), ("A", 0))).after(("M", 2)),
+                ctx_job,
+                FsdpSum(
+                    attn_shape, n, (("A", 0), ("A", 3)), source=ctx_job,
+                    sends=(("M", 4), ("M", 4), ("M", 5), ("M", 6)),
+                ),
+                CtxAdd(right_part, ("M", 6)),
             ]
         else:
             jobs = [Exchange(rows)]
-        expand_full, left_full, right_full, carry, mlp_vec[l], *more = call(
-            lambda jobs, *refs, base=8 * l: mlp_back_kernel(jobs, base, *refs),
-            f"mlp_back_{l}",
-            [square, narrow, narrow, own, vec],
-            scratch + [VMEM(every.shape, BF16), VMEM((count, hidden), BF16)] + mlp_scratch, 3 + 6 * l, 8 * count * dim * hidden,
-            [active, slope, second, middle, carry, params, *mlp_pairs], jobs,
-        )
-        if last:
-            attn_part, expand_grads[l + 1], left_grads[l + 1] = more
-            ctx_job = CtxSum(expand_full, n, (1, 2, 3, 4), keep=True)
-            jobs = [
-                FsdpSum(attn_part, n, (1, 4)), ctx_job,
-                FsdpSum(expand_shape, n, (5, 9), source=ctx_job, sends=(1, 2, 3, 4)),
-                CtxSum(left_full, n, (10, 10, 10, 10)),
-            ]
-        else:
-            (output,) = more
-            jobs = [
-                CtxSum(expand_full, n, (5, 6, 7, 8)), CtxSum(left_full, n, (10, 10, 10, 10)),
-                FsdpSum(right_full.reshape(n, shard, -1), n, (1, 10), spread=False),
-            ]
-        attn_full, carry, attn_vec[l], *more = call(
-            lambda jobs, *refs, base=8 * l: attention_back_kernel(jobs, heads, base, *refs),
-            f"attention_back_{l}",
-            [jax.ShapeDtypeStruct((dim, 4 * width), BF16), own_low if last else own, vec],
+        attn_full, carry, mlp_vec[l], attn_vec[l], *more = call(
+            lambda jobs, refs, base=8 * l: backward_kernel(jobs, heads, base, refs),
+            f"backward_{l}",
+            [(jax.ShapeDtypeStruct((dim, 4 * width), BF16), HBM_SPEC), own_low if last else own, vec, vec],
             scratch
             + [
-                VMEM(every.shape, BF16),
+                VMEM((dim, hidden // 2), BF16), VMEM((dim, hidden // 2), BF16),
+                VMEM(own.shape, F32), VMEM(every.shape, BF16), VMEM(every.shape, BF16),
+                VMEM((count, hidden), BF16),
+            ]
+            + mlp_scratch
+            + [
                 VMEM((count, 3 * width), BF16),
                 VMEM((heads, count, LANES), F32),
                 VMEM((heads, count, LANES), F32),
             ]
             + attn_scratch,
-            4 + 6 * l, 4 * count * dim * 4 * width + 40 * heads * count * count * HD,
-            [mixed, q, k, v, first, carry, resid, params, attn_pair], jobs,
+            2 + 2 * l,
+            4 * count * dim * 4 * width + 40 * heads * count * count * HD + 8 * count * dim * hidden,
+            [active, slope, second, middle, carry, params, mixed, q, k, v, first, resid, weights],
+            jobs + made,
         )
         if last:
-            attn_grads[l + 1], expand_grads[l], left_part = more
+            expand_grads[1], left_grads[1], attn_grads[1], right_grads[1], *more = more
         else:
-            expand_part, left_part, right_part = more
-            expand_shape = jax.ShapeDtypeStruct(expand_part.shape, BF16)
+            output, *more = more
+        left_part, right_part, expand_part = more
 
     ctx_job = CtxSum(attn_full, n, (0, 1, 2, 3), keep=True)
     attn_shape = jax.ShapeDtypeStruct((n, shard // 2, 4 * width), BF16)
-    right_job = FsdpSum(right_full.reshape(n, shard, -1), n, (0, 1), spread=False)
     jobs = [
         ctx_job,
         FsdpSum(attn_shape, n, (0, 1), source=ctx_job),
+        FsdpSum(expand_part, n, (0, 1)),
         FsdpSum(left_part, n, (0, 1)),
-        right_job,
-        CtxAdd(right_part, 0, source=right_job),
         VectorSum([attn_vec[0], mlp_vec[0], attn_vec[1], mlp_vec[1]], n, (0, 1, 2, 3)),
         Exchange(carry),
         CtxAdd(right_part, 0),
     ]
-    attn_grads[0], left_grads[0], _, right_grads[0], vectors, row_grad, right_grads[1] = call(
-        leave_kernel, "leave", [], [], 5, 10**7, [], jobs
-    )
+    (
+        attn_grads[0], expand_grads[0], left_grads[0], vectors, row_grad, right_grads[0],
+    ) = call(leave_kernel, "leave", [], [], 5, 10**7, [], jobs)
     results = [
         jax.ShapeDtypeStruct(shape, F32)
         for shape in (

time: 476 us -> 453 us (0.952)
  the two profiles are of different devices: /device:TPU:24 before, /device:TPU:0 now
where the time goes in v5:
time: 453 us; the launch traced here: 445 us
  Pallas kernels  434 us (96%)
  local copies, waits for them, and re-layouts  5.36 us (1%)
    pallas_call x6, Pallas kernels, call(): pl.pallas_call(body, name=name, out_shape=tuple((o for o, _ in results)),...  429 us

profile of v5, /device:TPU:0, one launch (start us, length us, event | category | flops | bytes accessed | tf_op | source)
XLA Modules:
  0.0 444.5 jit_solution(6027467111824917169)
XLA Ops:
  0.6 0.0 copy-start
  0.7 0.8 compare_select_fusion
  1.5 1.0 select_convert_fusion.refs_2_
  2.5 1.1 copy.31
  3.6 2.2 pad_maximum_fusion.refs_10_
  5.8 0.0 copy-done
  5.8 1.3 copy.33
  7.1 45.4 %enter.1 = (bf16[2,128,1024]{2,1,0:T(8,128)(2,1)}, f32[16,1024]{1,0:T(8,128)}, bf16[2,128,1024]{2,1,0:T(8,128)(2,1)}, bf16[4,4,128,256]{3,2,1,0:T(8,128)(2,1)}, ...) custom-call(bf16[2,256]{1,0:T(2,128)(2,1)} %refs_0_.1, bf16[2,256]{1,0:T(2,128)(2,1)} %refs_1_.1, ...), custom_call_target="tpu_custom_call" | custom-call | flops 10000000 | bytes 6888960 | tf_op jit(solution)/shard_map/enter/pallas_call | solution.py:1424
  52.6 75.2 %forward_0.1 = (bf16[4,2,128,1024]{3,2,1,0:T(8,128)(2,1)}, bf16[2,128,1024]{2,1,0:T(8,128)(2,1)}, f32[2,128,1024]{2,1,0:T(8,128)}, bf16[4,1024,128]{2,1,0:T(8,12...) custom-call(bf16[2,128,1024]{2,1,0:T(8,128)(2,1)} %get-tuple-element, ...), custom_call_target="tpu_custom_call" | custom-call | flops 10737418240 | bytes 31260672 | tf_op jit(solution)/shard_map/forward_0/pallas_call | solution.py:1424
  127.8 72.8 %forward_1.1 = (bf16[4,2,128,1024]{3,2,1,0:T(8,128)(2,1)}, bf16[2,128,1024]{2,1,0:T(8,128)(2,1)}, f32[2,128,1024]{2,1,0:T(8,128)}, bf16[4,1024,128]{2,1,0:T(8,12...) custom-call(bf16[2,128,1024]{2,1,0:T(8,128)(2,1)} %get-tuple-element, ...), custom_call_target="tpu_custom_call" | custom-call | flops 10737418240 | bytes 26546176 | tf_op jit(solution)/shard_map/forward_1/pallas_call | solution.py:1424
  200.6 72.4 %backward_1.1 = (bf16[1024,1024]{1,0:T(8,128)(2,1)}, f32[2,128,1024]{2,1,0:T(8,128)}, f32[8,1024]{1,0:T(8,128)}, f32[8,1024]{1,0:T(8,128)}, bf16[2,128,1024]{2,1...) custom-call(bf16[1024,1024]{1,0:T(8,128)(2,1)} %get-tuple-element.96.refs_0_, ...), custom_call_target="tpu_custom_call" | custom-call | flops 23622320128 | bytes 27131904 | tf_op jit(solution)/shard_map/backward_1/pallas_call | solution.py:1424
  273.0 89.9 %backward_0.1 = (bf16[1024,1024]{1,0:T(8,128)(2,1)}, bf16[2,128,1024]{2,1,0:T(8,128)(2,1)}, f32[8,1024]{1,0:T(8,128)}, f32[8,1024]{1,0:T(8,128)}, bf16[2,128,102...) custom-call(bf16[1024,1024]{1,0:T(8,128)(2,1)} %get-tuple-element.11, ...), custom_call_target="tpu_custom_call" | custom-call | flops 23622320128 | bytes 31064064 | tf_op jit(solution)/shard_map/backward_0/pallas_call | solution.py:1424
  363.0 73.2 %leave.1 = (bf16[2,128,1024]{2,1,0:T(8,128)(2,1)}, bf16[2,128,1024]{2,1,0:T(8,128)(2,1)}, bf16[2,128,512]{2,1,0:T(8,128)(2,1)}, f32[16,1024]{1,0:T(8,128)}, bf16...) custom-call(bf16[4,2,128,1024]{3,2,1,0:T(8,128)(2,1)} %bitcast.34, bf16[4,128,1024]{2,1,0:T(8,128)(2,1)} %get-tuple-element.129.refs_1_, ...), custom_call_target="tpu_custom_call" | custom-call | flops 10000000 | bytes 6750208 | tf_op jit(solution)/shard_map/leave/pallas_call | solution.py:1424
  436.2 0.0 copy-start.1
  436.2 0.0 copy-start.2
  436.2 4.9 %finish.1 = (f32[2,3,256,256]{3,2,1,0:T(8,128)}, f32[2,256,256]{2,1,0:T(8,128)}, f32[2,256,1024]{2,1,0:T(8,128)}, f32[2,1024,256]{2,1,0:T(8,128)}, f32[6,2,256]{...) custom-call(bf16[2,128,1024]{2,1,0:T(8,128)(2,1)} %get-tuple-element.138.attn_0, ...), custom_call_target="tpu_custom_call" | custom-call | tf_op jit(solution)/shard_map/finish/pallas_call | solution.py:1613
  441.1 1.4 slice_bitcast_fusion
  442.5 0.0 copy-done.1
  442.5 0.8 copy.43
  443.3 0.0 copy-done.2
  443.3 0.8 copy.44
  (4 shorter events, 0.0 us)
Async XLA Ops:
  0.6 5.2 %copy-start = (bf16[2,1024,256]{2,1,0:T(8,128)(2,1)S(1)}, bf16[2,1024,256]{2,1,0:T(8,128)(2,1)}, u32[]{:S(2)}) copy-start(bf16[2,1024,256]{2,1,0:T(8,128)(2,1)} %param.29) | copy-start | bytes 3145732
  436.2 6.3 %copy-start.1 = (bf16[2,128,1024]{2,1,0:T(8,128)(2,1)S(1)}, bf16[2,128,1024]{2,1,0:T(8,128)(2,1)}, u32[]{:S(2)}) copy-start(bf16[2,128,1024]{2,1,0:T(8,128)(2,1)} %get-tuple-element.178) | copy-start | bytes 1572868
  436.2 7.1 %copy-start.2 = (bf16[2,128,1024]{2,1,0:T(8,128)(2,1)S(1)}, bf16[2,128,1024]{2,1,0:T(8,128)(2,1)}, u32[]{:S(2)}) copy-start(bf16[2,128,1024]{2,1,0:T(8,128)(2,1)} %get-tuple-element.179) | copy-start | bytes 1572868
